TPU v7x, 512 devices: a whole 4x4x16 slice. The times are simulated.
512 devices in a mesh: gx: 16 (over x, z_hi, core), gy: 4 (over y), gz: 8 (over z_lo).
Axes of the slice: x: 4, y: 4, z: 16 (z_hi: 2, z_lo: 8; z = z_hi * 8 + z_lo), core: 2. Of those that a mesh axis runs over, the one named last changes fastest.
Arguments:
- positions: float32 [3, 32768], P(None, ('gx', 'gy', 'gz')), may hold values from 0 to 6
- species: int32 [32768], P(('gx', 'gy', 'gz')), may hold values from 0 to 6
- counts: int32 [512], P(('gx', 'gy', 'gz')), may hold values from 16 to 64, as said below
- neighbours: int32 [32, 32768], P(None, ('gx', 'gy', 'gz')), may hold values from 0 to 495, as said below
- exports: int32 [8192], P(('gx', 'gy', 'gz')), may hold values from 0 to 63, as said below
- embedding: bfloat16 [7, 128], replicated, may hold values from -5 to 5
- radial_in: bfloat16 [2, 8, 64], replicated, may hold values from -2 to 2
- radial_out_one: bfloat16 [64, 256], replicated, may hold values from -0.75 to 0.75
- radial_out_two: bfloat16 [64, 512], replicated, may hold values from -0.75 to 0.75
- mix_one: bfloat16 [6, 128, 128], replicated, may hold values from -0.5 to 0.5
- mix_two: bfloat16 [5, 128, 128], replicated, may hold values from -0.5 to 0.5
- readout: float32 [2, 128], replicated, may hold values from -0.5 to 0.5
Outputs:
- forces: float32 [3, 32768], P(None, ('gx', 'gy', 'gz'))
- site_energies: float32 [32768], P(('gx', 'gy', 'gz'))
Inputs may be any that keep to these rules, and one draw needn't show every extreme that they name: `counts`: one domain in each draw holds exactly 64 live atoms; the others are spread with many near 64 // 4. `neighbours`: column i of domain d lists table indices: live local slots other than i, or 64 + b * 16 + e with b never 13. Entries equal to i are padding; columns of slots at or past the domain's count hold only i. Slot 0 of every domain has 32 entries other than itself. `exports`: the 16 entries of a domain are distinct slots below its count.
All inputs are finite; a program needn't handle non-finite values.
Results may differ from a plain program's by a relative error of at most 0.025.
Values may be sent and summed in bfloat16 or wider, within the bound.
No kernel may reach another device: no remote copies, remote signals or barrier semaphores. Data moves between devices by JAX's collectives and lax.ppermute only.
A program may use at most 64 MiB of HBM per device.

v0:
```python
import math

import jax
import jax.numpy as jnp
from jax import lax
from jax.sharding import PartitionSpec as P

C = 128
NB = 8
NSPEC = 7
SLOTS = 64
BLOCK = 32
EXPORT = 16


DOMAIN_LENGTH = 6.0
CUTOFF = 6.0
SOFTEN = 0.25


def padded(block, sides, width):
    for axis, dim in sides:
        count = lax.axis_size(axis)
        forward = [(i, i + 1) for i in range(count - 1)]
        forward.append((count - 1, 0))
        backward = [(target, source) for source, target in forward]
        low = lax.ppermute(
            lax.slice_in_dim(block, block.shape[dim] - width, None, axis=dim), axis, forward
        )
        high = lax.ppermute(lax.slice_in_dim(block, 0, width, axis=dim), axis, backward)
        block = jnp.concatenate([low, block, high], axis=dim)
    return block


def mixed(values, matrix):
    return jnp.dot(values, matrix.astype(jnp.float32), precision=lax.Precision.HIGHEST)


def pair_terms(positions_all, neighbour_rows, first_row, live_count, radial_first, radial_second):
    list_depth, block_rows = neighbour_rows.shape
    receivers = first_row + jnp.arange(block_rows, dtype=jnp.int32)
    centre = lax.dynamic_slice_in_dim(positions_all, first_row, block_rows, 1)
    others = jnp.take(positions_all, neighbour_rows, axis=1)
    offset_vec = others - centre[:, None, :]
    distance = jnp.sqrt(jnp.sum(offset_vec * offset_vec, axis=0) + SOFTEN)
    live_rows = (receivers < live_count).astype(jnp.float32)
    paired = (neighbour_rows != receivers[None, :]).astype(jnp.float32) * live_rows[None, :]
    direction = jnp.moveaxis(offset_vec / distance[None], 0, -1)[..., None]
    orders = jnp.arange(1, NB + 1).astype(jnp.float32)[:, None, None]
    scaled = jnp.minimum(distance / CUTOFF, 1.0)
    envelope = 1.0 - 28.0 * scaled**6 + 48.0 * scaled**7 - 21.0 * scaled**8
    basis_rows = (
        jnp.sin(orders * (math.pi / CUTOFF) * distance[None])
        / distance[None]
        * (envelope * paired)[None]
    )
    flattened = basis_rows.reshape(NB, list_depth * block_rows).T.astype(jnp.bfloat16)
    hidden = jax.nn.silu(
        jnp.dot(flattened, radial_first, preferred_element_type=jnp.float32)
    ).astype(jnp.bfloat16)
    radial = jnp.dot(hidden, radial_second, preferred_element_type=jnp.float32)
    radial = radial.reshape(list_depth, block_rows, radial_second.shape[1] // C, C)
    return (radial, direction, 1.0 / math.sqrt(list_depth), live_rows)


def layer_one(
    positions_all,
    projected,
    own_scalar,
    neighbour_rows,
    first_row,
    live_count,
    radial_first,
    radial_second,
    mixing,
    readout_row,
):
    radial, direction, norm_factor, live_rows = pair_terms(
        positions_all, neighbour_rows, first_row, live_count, radial_first, radial_second
    )
    source = jnp.take(projected, neighbour_rows, axis=0)
    first_sum = jnp.sum(radial[:, :, 0] * source, axis=0) * norm_factor
    second_sum = (
        jnp.sum(radial[:, :, 1, None] * source[:, :, None] * direction, axis=0) * norm_factor
    )
    quadratic = jnp.sum(second_sum * second_sum, axis=1)
    scalar_out = (
        own_scalar
        + mixed(first_sum, mixing[1])
        + mixed(first_sum * first_sum, mixing[2])
        + mixed(quadratic, mixing[3])
    )
    vector_out = mixed(second_sum, mixing[4]) + mixed(first_sum[:, None] * second_sum, mixing[5])
    energy = jnp.dot(scalar_out, readout_row, precision=lax.Precision.HIGHEST) * live_rows
    return (jnp.concatenate([scalar_out[:, None], vector_out], axis=1), energy)


def layer_two(
    positions_all,
    projected,
    own_scalar,
    neighbour_rows,
    first_row,
    live_count,
    radial_first,
    radial_second,
    mixing,
    readout_row,
):
    radial, direction, norm_factor, live_rows = pair_terms(
        positions_all, neighbour_rows, first_row, live_count, radial_first, radial_second
    )
    source = jnp.take(projected, neighbour_rows, axis=0)
    scalar_src = source[:, :, 0]
    vector_src = source[:, :, 1:]
    along_unit = jnp.sum(vector_src * direction, axis=2)
    first_sum = (
        jnp.sum(radial[:, :, 0] * scalar_src + radial[:, :, 3] * along_unit, axis=0) * norm_factor
    )
    second_sum = (
        jnp.sum(
            radial[:, :, 1, None] * scalar_src[:, :, None] * direction
            + radial[:, :, 2, None] * vector_src,
            axis=0,
        )
        * norm_factor
    )
    quadratic = jnp.sum(second_sum * second_sum, axis=1)
    scalar_out = (
        own_scalar
        + mixed(first_sum, mixing[2])
        + mixed(first_sum * first_sum, mixing[3])
        + mixed(quadratic, mixing[4])
    )
    return jnp.dot(scalar_out, readout_row, precision=lax.Precision.HIGHEST) * live_rows


def project_two(features, mixing):
    return jnp.concatenate(
        [mixed(features[:, :1], mixing[0]), mixed(features[:, 1:], mixing[1])], axis=1
    )


def owners_sum(buffer):
    extended = padded(buffer.astype(jnp.bfloat16), (("gx", 0), ("gy", 1), ("gz", 2)), 1).astype(
        buffer.dtype
    )
    return jnp.sum(extended[0::2, 0::2, 0::2], axis=(0, 1, 2))


def body(
    positions,
    species,
    counts,
    neighbours,
    exports,
    embedding,
    radial_in,
    radial_out_one,
    radial_out_two,
    mix_one,
    mix_two,
    readout,
):
    live_count = counts[0]
    ghost_rows = 27 * EXPORT
    live = (jnp.arange(SLOTS, dtype=jnp.int32) < live_count).astype(jnp.float32)
    packed = jnp.concatenate(
        [
            jnp.take(positions, exports, axis=1),
            jnp.take(species, exports).astype(jnp.float32)[None],
        ],
        axis=0,
    )
    arrived = padded(packed[None, None, None], (("gx", 0), ("gy", 1), ("gz", 2)), 1)
    step_size = (jnp.arange(3) - 1).astype(jnp.float32) * DOMAIN_LENGTH
    shifts = jnp.stack(
        [
            jnp.broadcast_to(step_size[:, None, None], (3, 3, 3)),
            jnp.broadcast_to(step_size[None, :, None], (3, 3, 3)),
            jnp.broadcast_to(step_size[None, None, :], (3, 3, 3)),
        ]
    )
    ghost_at = (jnp.moveaxis(arrived[:, :, :, 0:3, :], 3, 0) + shifts[..., None]).reshape(
        3, ghost_rows
    )
    ghost_kind = arrived[:, :, :, 3, :].reshape(ghost_rows)
    table_at = jnp.concatenate([positions, ghost_at], axis=1)
    kind_all = jnp.concatenate([species.astype(jnp.float32), ghost_kind])
    one_hot = (kind_all[:, None] == jnp.arange(NSPEC).astype(jnp.float32)[None, :]).astype(
        jnp.bfloat16
    )
    scalar0 = jnp.dot(one_hot, embedding, preferred_element_type=jnp.float32)
    projected0 = mixed(scalar0, mix_one[0])
    block_count = SLOTS // BLOCK

    def first_block(first_row, atoms_at):
        return layer_one(
            atoms_at,
            projected0,
            lax.dynamic_slice_in_dim(scalar0, first_row, BLOCK, 0),
            lax.dynamic_slice_in_dim(neighbours, first_row, BLOCK, 1),
            first_row,
            live_count,
            radial_in[0],
            radial_out_one,
            mix_one,
            readout[0],
        )

    def forward_block(block_index, running):
        features1, energy1 = running
        first_row = block_index * BLOCK
        rows_out, energy_rows = first_block(first_row, table_at)
        return (
            lax.dynamic_update_slice_in_dim(features1, rows_out, first_row, 0),
            lax.dynamic_update_slice_in_dim(energy1, energy_rows, first_row, 0),
        )

    features1, energy1 = lax.fori_loop(
        0,
        block_count,
        forward_block,
        (jnp.zeros((SLOTS, 4, C), jnp.float32), jnp.zeros((SLOTS,), jnp.float32)),
    )
    rounded = lax.optimization_barrier(features1.astype(jnp.bfloat16))
    outgoing = jnp.take(rounded, exports, axis=0).reshape(EXPORT, 4 * C)
    ghost_feat = padded(outgoing[None, None, None], (("gx", 0), ("gy", 1), ("gz", 2)), 1)
    table_feat = jnp.concatenate([rounded, ghost_feat.reshape(ghost_rows, 4, C)], axis=0).astype(
        jnp.float32
    )

    def project_table(table_rows):
        return project_two(table_rows, mix_two)

    projected1, project_pull = jax.vjp(project_table, table_feat)

    def second_block(block_index, running):
        energy2, grad_at, grad_proj, grad_own = running
        first_row = block_index * BLOCK
        neighbour_rows = lax.dynamic_slice_in_dim(neighbours, first_row, BLOCK, 1)
        own_rows = lax.dynamic_slice_in_dim(table_feat[:, 0], first_row, BLOCK, 0)

        def energy_of(atoms_at, projected, own_scalar):
            return layer_two(
                atoms_at,
                projected,
                own_scalar,
                neighbour_rows,
                first_row,
                live_count,
                radial_in[1],
                radial_out_two,
                mix_two,
                readout[1],
            )

        energy_rows, pullback = jax.vjp(energy_of, table_at, projected1, own_rows)
        part_at, part_proj, part_own = pullback(lax.dynamic_slice_in_dim(live, first_row, BLOCK, 0))
        return (
            lax.dynamic_update_slice_in_dim(energy2, energy_rows, first_row, 0),
            grad_at + part_at,
            grad_proj + part_proj,
            lax.dynamic_update_slice_in_dim(grad_own, part_own, first_row, 0),
        )

    start_state = (
        jnp.zeros((SLOTS,), jnp.float32),
        jnp.zeros(table_at.shape, jnp.float32),
        jnp.zeros(projected1.shape, jnp.float32),
        jnp.zeros((SLOTS, C), jnp.float32),
    )
    energy2, grad_at, grad_proj, grad_own = lax.fori_loop(0, block_count, second_block, start_state)
    (grad_table,) = project_pull(grad_proj)
    grad_table = grad_table.at[:SLOTS, 0].add(grad_own)
    returned = owners_sum(grad_table[SLOTS:].reshape(3, 3, 3, EXPORT, 4 * C)).reshape(EXPORT, 4, C)
    grad_local = grad_table[:SLOTS].at[exports].add(returned)

    def backward_block(block_index, grad_total):
        first_row = block_index * BLOCK

        def features_of(atoms_at):
            return first_block(first_row, atoms_at)

        unused, pullback = jax.vjp(features_of, table_at)
        cotangent = (
            lax.dynamic_slice_in_dim(grad_local, first_row, BLOCK, 0),
            lax.dynamic_slice_in_dim(live, first_row, BLOCK, 0),
        )
        (part_at,) = pullback(cotangent)
        return grad_total + part_at

    grad_at = lax.fori_loop(0, block_count, backward_block, grad_at)
    ghost_grad = jnp.moveaxis(grad_at[:, SLOTS:].reshape(3, 3, 3, 3, EXPORT), 0, 3)
    returned_at = owners_sum(ghost_grad)
    local_at = grad_at[:, :SLOTS].at[:, exports].add(returned_at)
    return (-local_at, live * (energy1 + energy2))


def solution(mesh):
    in_specs = (
        P(None, ("gx", "gy", "gz")),
        P(("gx", "gy", "gz")),
        P(("gx", "gy", "gz")),
        P(None, ("gx", "gy", "gz")),
        P(("gx", "gy", "gz")),
        P(),
        P(),
        P(),
        P(),
        P(),
        P(),
        P(),
    )
    out_specs = (P(None, ("gx", "gy", "gz")), P(("gx", "gy", "gz")))
    return jax.shard_map(body, mesh=mesh, in_specs=in_specs, out_specs=out_specs, check_vma=False)
```

profile of v0, /device:TPU:8, one launch (start us, length us, event | category | flops | bytes accessed | tf_op | source)
XLA Modules:
  0.0 680.5 jit_solution(8387171752119926470)
XLA Ops:
  4.9 17.4 %collective-permute-start.1 = (f32[1,1,1,4,16]{4,3,2,1,0:T(4,128)S(1)}, f32[1,1,1,4,16]{4,3,2,1,0:T(4,128)S(1)}, u32[]{:S(2)}, u32[]{:S(2)}) collective-permute-start(f32[1,1,1,4,16]{4,3,2,1,0:T(4,128)S(1)} %maximum_bitcast_fusion), channel_id=1, source_target_pairs={{32,0},{64,32},{96,64},{128,96},{160,128},{192,160},{224,192},{256... | collective-permute-start | bytes 776 | tf_op jit(solution)/shard_map/ppermute | solution.py:30
  24.2 13.8 %collective-permute-done = f32[1,1,1,4,16]{4,3,2,1,0:T(4,128)S(1)} collective-permute-done((f32[1,1,1,4,16]{4,3,2,1,0:T(4,128)S(1)}, f32[1,1,1,4,16]{4,3,2,1,0:T(4,128)S(1)}, u32[]{:S(2)}, u32[]{:S(2)}) %collective-permute-start) | collective-permute-done | bytes 288 | tf_op jit(solution)/shard_map/ppermute | solution.py:27
  40.3 3.5 collective-permute-start.2
  46.8 5.7 collective-permute-start.5
  55.1 9.7 %collective-permute-done.4 = f32[3,3,1,4,16]{4,3,2,1,0:T(4,128)S(1)} collective-permute-done((f32[3,3,1,4,16]{4,3,2,1,0:T(4,128)S(1)}, f32[3,3,1,4,16]{4,3,2,1,0:T(4,128)S(1)}, u32[]{:S(2)}, u32[]{:S(2)}) %collective-permute-start.4) | collective-permute-done | bytes 2336 | tf_op jit(solution)/shard_map/ppermute | solution.py:27
  67.5 29.7 %while.51 = (s32[]{:T(128)}, bf16[64,4,128]{2,0,1:T(8,128)(2,1)S(1)}, f32[64]{0:T(128)S(1)}, f32[496,128]{1,0:T(8,128)}, s32[32,64]{1,0:T(8,128)S(1)}, /*index=5...) while((s32[]{:T(128)}, ...), condition=%wide.region_5.7_spmd, body=%wide.region_0.6_spmd.sunk | while | flops 93152512 | bytes 9939416 | solution.py:220
  74.8 2.8 gather_fusion.1
  102.3 13.5 %collective-permute-done.6 = bf16[1,1,1,16,512]{4,3,2,1,0:T(8,128)(2,1)S(1)} collective-permute-done((bf16[1,1,1,16,512]{4,3,2,1,0:T(8,128)(2,1)S(1)}, bf16[1,1,1,16,512]{4,3,2,1,0:T(8,128)(2,1)S(1)}, u32[]{:S(2)}, u32[]{:S(2)}) %collective-permute-start.6) | collective-permute-done | bytes 16416 | tf_op jit(solution)/shard_map/ppermute | solution.py:27
  115.7 5.1 collective-permute-start.9
  122.8 4.0 collective-permute-done.8
  128.8 3.9 collective-permute-start.10
  133.9 8.5 %collective-permute-done.10 = bf16[3,3,1,16,512]{4,3,2,1,0:T(8,128)(2,1)S(1)} collective-permute-done((bf16[3,3,1,16,512]{4,3,2,1,0:T(8,128)(2,1)S(1)}, bf16[3,3,1,16,512]{4,3,2,1,0:T(8,128)(2,1)S(1)}, u32[]{:S(2)}, u32[]{:S(2)}) %collective-permute-start.10) | collective-permute-done | bytes 147488 | tf_op jit(solution)/shard_map/ppermute | solution.py:27
  149.5 369.3 %while.53 = (s32[]{:T(128)}, f32[64]{0:T(128)}, f32[3,496]{0,1:T(8,128)S(1)}, f32[496,4,128]{2,1,0:T(4,128)}, f32[64,128]{1,0:T(8,128)}, /*index=5*/s32[]{:T(128...) while((s32[]{:T(128)}, f32[64]{0:T(128)}, ...), condition=%wide.region_23.26_spmd.clone, body=%wide.region_6.25_spmd.clone.sunk | while | flops 187080032 | bytes 74716368 | solution.py:273
  162.4 9.2 %gather_fusion.4 = f32[1024,4,128]{2,1,0:T(4,128)} fusion(f32[496,4,128]{2,1,0:T(4,128)} %get-tuple-element.1743, s32[1024]{0:T(1024)S(1)} %broadcast_clamp_fusion.8), kind=kCustom, calls=%fused_computation.3.clone.clone.1 | custom fusion | bytes 4198400 | tf_op jit(solution)/shard_map/while/body/eval_jaxpr/jvp(jit(_take))/gather | solution.py:113
  171.6 3.2 broadcast_select_fusion.5
  175.4 2.8 gather_fusion.5
  184.3 2.9 reshape.777
  187.2 7.0 %fusion.406 = (f32[32,32,1,128]{3,2,1,0:T(1,128)S(1)}, f32[32,32,1,128]{3,2,1,0:T(1,128)S(1)}, f32[32,32,1,128]{3,2,1,0:T(1,128)S(1)}, f32[32,32,1,128]{3,2,1,0:T(1,128)S(1)}, f32[32,32,1,128]{3,2,1,0:T(1,128)S(1)}) fusion(f32[32,32,4,128]{3,2,1,0:T(4,128)S(1)} %broadcast_select_fusion.5, f32[32,32,4,128]{3,2,1,0:T(4,128)} %reshape.777), kind=kLoop, calls=%fused_computation.432.clone.1 | loop fusion | flops 131072 | bytes 5242880 | tf_op jit(solution)/shard_map/while/body/eval_jaxpr/jvp()/slice | solution.py:114
  194.6 5.7 add_reduce_fusion.2
  212.6 9.8 %multiply_reduce_fusion.35 = (f32[32,32,3]{2,1,0:T(8,128)}, f32[32,32,128]{2,1,0:T(8,128)S(1)}, f32[32,32,3]{2,1,0:T(8,128)}, f32[32,32,128]{2,1,0:T(8,128)S(1)}, f32[32,32,3,128]{3,2,1,0:T(4,128)}) fusion(f32[32,32,4,128]{3,2,1,0:T(4,128)S(1)} %broadcast_select_fusion.5, f32[32,32,128]{2,1,0:T(8,128)S(1)} %broadcast_multiply_fusion.10, ...), kind=kLoop, calls=%fused_computation.217.clone.1 | loop fusion | flops 4057088 | bytes 5853184 | tf_op jit(solution)/shard_map/while/body/eval_jaxpr/transpose(jvp())/reduce_sum | solution.py:116
  222.5 4.5 slice_multiply_fusion.7
  232.0 6.2 scatter_custom_fusion.17
  240.8 98.5 %scatter_fusion = f32[496,4,128]{2,1,0:T(4,128)} fusion(f32[496,4,128]{2,1,0:T(4,128)} %get-tuple-element.1714, s32[1024]{0:T(1024)S(1)} %reshape.776, f32[1024,4,128]{2,1,0:T(4,128)S(1)} %bitcast.483), kind=kCustom, calls=%fused_computation.10.clone.clone.1 | custom fusion | flops 524288 | bytes 6295552 | tf_op jit(solution)/shard_map/while/body/eval_jaxpr/transpose(jvp(jit(_take)))/scatter-add | solution.py:113
  341.8 9.2 %gather_fusion.4 = f32[1024,4,128]{2,1,0:T(4,128)} fusion(f32[496,4,128]{2,1,0:T(4,128)} %get-tuple-element.1743, s32[1024]{0:T(1024)S(1)} %broadcast_clamp_fusion.8), kind=kCustom, calls=%fused_computation.3.clone.clone.1 | custom fusion | bytes 4198400 | tf_op jit(solution)/shard_map/while/body/eval_jaxpr/jvp(jit(_take))/gather | solution.py:113
  351.0 3.2 broadcast_select_fusion.5
  363.7 2.9 reshape.777
  366.7 7.0 %fusion.406 = (f32[32,32,1,128]{3,2,1,0:T(1,128)S(1)}, f32[32,32,1,128]{3,2,1,0:T(1,128)S(1)}, f32[32,32,1,128]{3,2,1,0:T(1,128)S(1)}, f32[32,32,1,128]{3,2,1,0:T(1,128)S(1)}, f32[32,32,1,128]{3,2,1,0:T(1,128)S(1)}) fusion(f32[32,32,4,128]{3,2,1,0:T(4,128)S(1)} %broadcast_select_fusion.5, f32[32,32,4,128]{3,2,1,0:T(4,128)} %reshape.777), kind=kLoop, calls=%fused_computation.432.clone.1 | loop fusion | flops 131072 | bytes 5242880 | tf_op jit(solution)/shard_map/while/body/eval_jaxpr/jvp()/slice | solution.py:114
  374.0 5.7 add_reduce_fusion.2
  392.0 9.8 %multiply_reduce_fusion.35 = (f32[32,32,3]{2,1,0:T(8,128)}, f32[32,32,128]{2,1,0:T(8,128)S(1)}, f32[32,32,3]{2,1,0:T(8,128)}, f32[32,32,128]{2,1,0:T(8,128)S(1)}, f32[32,32,3,128]{3,2,1,0:T(4,128)}) fusion(f32[32,32,4,128]{3,2,1,0:T(4,128)S(1)} %broadcast_select_fusion.5, f32[32,32,128]{2,1,0:T(8,128)S(1)} %broadcast_multiply_fusion.10, ...), kind=kLoop, calls=%fused_computation.217.clone.1 | loop fusion | flops 4057088 | bytes 5853184 | tf_op jit(solution)/shard_map/while/body/eval_jaxpr/transpose(jvp())/reduce_sum | solution.py:116
  401.9 4.5 slice_multiply_fusion.7
  411.4 6.2 scatter_custom_fusion.17
  420.2 97.9 %scatter_fusion = f32[496,4,128]{2,1,0:T(4,128)} fusion(f32[496,4,128]{2,1,0:T(4,128)} %get-tuple-element.1714, s32[1024]{0:T(1024)S(1)} %reshape.776, f32[1024,4,128]{2,1,0:T(4,128)S(1)} %bitcast.483), kind=kCustom, calls=%fused_computation.10.clone.clone.1 | custom fusion | flops 524288 | bytes 6295552 | tf_op jit(solution)/shard_map/while/body/eval_jaxpr/transpose(jvp(jit(_take)))/scatter-add | solution.py:113
  526.6 14.5 %collective-permute-start.13 = (bf16[1,3,3,16,512]{4,3,2,1,0:T(8,128)(2,1)S(1)}, bf16[1,3,3,16,512]{4,3,2,1,0:T(8,128)(2,1)S(1)}, u32[]{:S(2)}, u32[]{:S(2)}) collective-permute-start(bf16[1,3,3,16,512]{4,3,2,1,0:T(8,128)(2,1)S(1)} %slice.367), channel_id=1, source_target_pairs={{32,0},{64,32},{96,64},{128,96},{160,128},{192,160},{224,192},{256... | collective-permute-start | bytes 442376 | tf_op jit(solution)/shard_map/ppermute | solution.py:30
  543.8 3.3 collective-permute-start.15
  551.9 3.3 collective-permute-done.14
  558.4 3.6 collective-permute-start.16
  562.8 12.7 %collective-permute-done.17 = bf16[5,5,1,16,512]{4,3,2,1,0:T(8,128)(2,1)} collective-permute-done((bf16[5,5,1,16,512]{4,3,2,1,0:T(8,128)(2,1)}, bf16[5,5,1,16,512]{4,3,2,1,0:T(8,128)(2,1)}, u32[]{:S(2)}, u32[]{:S(2)}) %collective-permute-start.17) | collective-permute-done | bytes 409632 | tf_op jit(solution)/shard_map/ppermute | solution.py:30
  579.2 48.2 %while.52 = (s32[]{:T(128)}, f32[3,496]{0,1:T(8,128)S(1)}, s32[32,64]{1,0:T(8,128)S(1)}, f32[3,496]{0,1:T(8,128)S(1)}, s32[]{:T(128)}, /*index=5*/bf16[2,8,64]{2...) while((s32[]{:T(128)}, f32[3,496]{0,1:T(8,128)S(1)}, ...), condition=%wide.region_39.42_spmd, body=%wide.region_26.41_spmd.sunk | while | flops 131087152 | bytes 19015908 | solution.py:293
  580.2 2.8 gather_fusion.2
  586.8 2.8 gather_fusion.3
  597.0 6.1 scatter_custom_fusion.15
  621.1 6.1 scatter_custom_fusion.15
  627.8 11.6 %collective-permute-start.19 = (bf16[1,3,3,3,16]{4,2,1,0,3:T(4,128)(2,1)S(1)}, bf16[1,3,3,3,16]{4,2,1,0,3:T(4,128)(2,1)S(1)}, u32[]{:S(2)}, u32[]{:S(2)}) collective-permute-start(bf16[1,3,3,3,16]{4,2,1,0,3:T(4,128)(2,1)S(1)} %get-tuple-element.1297), channel_id=1, source_target_pairs={{32,0},{64,32},{96,64},{128,96},{160,128},{192,160},{224,192},{256... | collective-permute-start | bytes 2600 | tf_op jit(solution)/shard_map/ppermute | solution.py:30
  641.6 13.6 %collective-permute-done.18 = bf16[1,3,3,3,16]{4,2,1,0,3:T(4,128)(2,1)S(1)} collective-permute-done((bf16[1,3,3,3,16]{4,2,1,0,3:T(4,128)(2,1)S(1)}, bf16[1,3,3,3,16]{4,2,1,0,3:T(4,128)(2,1)S(1)}, u32[]{:S(2)}, u32[]{:S(2)}) %collective-permute-start.18) | collective-permute-done | bytes 896 | tf_op jit(solution)/shard_map/ppermute | solution.py:27
  655.3 3.3 collective-permute-start.21
  661.1 3.1 collective-permute-done.20
  666.2 3.9 collective-permute-start.22
  670.7 7.9 %collective-permute-done.22 = bf16[5,5,1,3,16]{4,3,2,1,0:T(4,128)(2,1)S(1)} collective-permute-done((bf16[5,5,1,3,16]{4,3,2,1,0:T(4,128)(2,1)S(1)}, bf16[5,5,1,3,16]{4,3,2,1,0:T(4,128)(2,1)S(1)}, u32[]{:S(2)}, u32[]{:S(2)}) %collective-permute-start.22) | collective-permute-done | bytes 2432 | tf_op jit(solution)/shard_map/ppermute | solution.py:27
  (519 shorter events, 182.7 us)
Async XLA Ops:
  0.6 65.5 %copy-start = (bf16[7,128]{1,0:T(8,128)(2,1)S(1)}, bf16[7,128]{1,0:T(8,128)(2,1)}, u32[]{:S(2)}) copy-start(bf16[7,128]{1,0:T(8,128)(2,1)} %param.29) | copy-start | bytes 5380
  0.6 66.8 %copy-start.14 = (bf16[6,128,128]{2,1,0:T(8,128)(2,1)S(1)}, bf16[6,128,128]{2,1,0:T(8,128)(2,1)}, u32[]{:S(2)}) copy-start(bf16[6,128,128]{2,1,0:T(8,128)(2,1)} %param.33) | copy-start | bytes 589828
  0.7 66.8 %copy-start.13 = (s32[32,64]{1,0:T(8,128)S(1)}, s32[32,64]{1,0:T(8,128)}, u32[]{:S(2)}) copy-start(s32[32,64]{1,0:T(8,128)} %param.27) | copy-start | bytes 24580
  4.9 19.3 %collective-permute-start.1 = (f32[1,1,1,4,16]{4,3,2,1,0:T(4,128)S(1)}, f32[1,1,1,4,16]{4,3,2,1,0:T(4,128)S(1)}, u32[]{:S(2)}, u32[]{:S(2)}) collective-permute-start(f32[1,1,1,4,16]{4,3,2,1,0:T(4,128)S(1)} %maximum_bitcast_fusion), channel_id=1, source_target_pairs={{32,0},{64,32},{96,64},{128,96},{160,128},{192,160},{224,192},{256... | collective-permute-start | bytes 776 | tf_op jit(solution)/shard_map/ppermute | solution.py:30
  22.2 15.7 %collective-permute-start = (f32[1,1,1,4,16]{4,3,2,1,0:T(4,128)S(1)}, f32[1,1,1,4,16]{4,3,2,1,0:T(4,128)S(1)}, u32[]{:S(2)}, u32[]{:S(2)}) collective-permute-start(f32[1,1,1,4,16]{4,3,2,1,0:T(4,128)S(1)} %maximum_bitcast_fusion), channel_id=1, source_target_pairs={{0,32},{32,64},{64,96},{96,128},{128,160},{160,192},{192,224},{224... | collective-permute-start | bytes 776 | tf_op jit(solution)/shard_map/ppermute | solution.py:27
  38.0 6.2 collective-permute-start.3
  40.3 6.5 collective-permute-start.2
  46.8 8.3 %collective-permute-start.5 = (f32[3,3,1,4,16]{4,3,2,1,0:T(4,128)S(1)}, f32[3,3,1,4,16]{4,3,2,1,0:T(4,128)S(1)}, u32[]{:S(2)}, u32[]{:S(2)}) collective-permute-start(f32[3,3,1,4,16]{4,3,2,1,0:T(4,128)S(1)} %pad_maximum_fusion.22), channel_id=1, source_target_pairs={{1,0},{2,1},{3,2},{4,3},{5,4},{6,5},{7,6},{0,7},{9,8},{10,9},{11,1... | collective-permute-start | bytes 6920 | tf_op jit(solution)/shard_map/ppermute | solution.py:30
  52.5 12.3 %collective-permute-start.4 = (f32[3,3,1,4,16]{4,3,2,1,0:T(4,128)S(1)}, f32[3,3,1,4,16]{4,3,2,1,0:T(4,128)S(1)}, u32[]{:S(2)}, u32[]{:S(2)}) collective-permute-start(f32[3,3,1,4,16]{4,3,2,1,0:T(4,128)S(1)} %pad_maximum_fusion.22), channel_id=1, source_target_pairs={{0,1},{1,2},{2,3},{3,4},{4,5},{5,6},{6,7},{7,0},{8,9},{9,10},{10,1... | collective-permute-start | bytes 6920 | tf_op jit(solution)/shard_map/ppermute | solution.py:27
  97.2 46.6 %copy-start.41 = (f32[64]{0:T(128)}, f32[64]{0:T(128)S(1)}, u32[]{:S(2)}) copy-start(f32[64]{0:T(128)S(1)} %get-tuple-element.757) | copy-start | bytes 772
  97.9 4.3 collective-permute-start.7
  99.8 15.9 %collective-permute-start.6 = (bf16[1,1,1,16,512]{4,3,2,1,0:T(8,128)(2,1)S(1)}, bf16[1,1,1,16,512]{4,3,2,1,0:T(8,128)(2,1)S(1)}, u32[]{:S(2)}, u32[]{:S(2)}) collective-permute-start(bf16[1,1,1,16,512]{4,3,2,1,0:T(8,128)(2,1)S(1)} %broadcast_select_fusion.2), channel_id=1, source_target_pairs={{0,32},{32,64},{64,96},{96,128},{128,160},{160,192},{192,224},{224... | collective-permute-start | bytes 49160 | tf_op jit(solution)/shard_map/ppermute | solution.py:27
  115.7 7.1 %collective-permute-start.9 = (bf16[3,1,1,16,512]{4,3,2,1,0:T(8,128)(2,1)S(1)}, bf16[3,1,1,16,512]{4,3,2,1,0:T(8,128)(2,1)S(1)}, u32[]{:S(2)}, u32[]{:S(2)}) collective-permute-start(bf16[3,1,1,16,512]{4,3,2,1,0:T(8,128)(2,1)S(1)} %pad_maximum_fusion.16), channel_id=1, source_target_pairs={{8,0},{16,8},{24,16},{0,24},{9,1},{17,9},{25,17},{1,25},{10,2},{18... | collective-permute-start | bytes 147464 | tf_op jit(solution)/shard_map/ppermute | solution.py:30
  120.9 6.0 collective-permute-start.8
  126.9 7.0 %collective-permute-start.11 = (bf16[3,3,1,16,512]{4,3,2,1,0:T(8,128)(2,1)S(1)}, bf16[3,3,1,16,512]{4,3,2,1,0:T(8,128)(2,1)S(1)}, u32[]{:S(2)}, u32[]{:S(2)}) collective-permute-start(bf16[3,3,1,16,512]{4,3,2,1,0:T(8,128)(2,1)S(1)} %pad_maximum_fusion.8), channel_id=1, source_target_pairs={{1,0},{2,1},{3,2},{4,3},{5,4},{6,5},{7,6},{0,7},{9,8},{10,9},{11,1... | collective-permute-start | bytes 442376 | tf_op jit(solution)/shard_map/ppermute | solution.py:30
  128.8 13.6 %collective-permute-start.10 = (bf16[3,3,1,16,512]{4,3,2,1,0:T(8,128)(2,1)S(1)}, bf16[3,3,1,16,512]{4,3,2,1,0:T(8,128)(2,1)S(1)}, u32[]{:S(2)}, u32[]{:S(2)}) collective-permute-start(bf16[3,3,1,16,512]{4,3,2,1,0:T(8,128)(2,1)S(1)} %pad_maximum_fusion.8), channel_id=1, source_target_pairs={{0,1},{1,2},{2,3},{3,4},{4,5},{5,6},{6,7},{7,0},{8,9},{9,10},{10,1... | collective-permute-start | bytes 442376 | tf_op jit(solution)/shard_map/ppermute | solution.py:27
  178.6 8.6 %copy-start.16 = (f32[32,32]{1,0:T(8,128)}, f32[32,32]{1,0:T(8,128)S(1)}, u32[]{:S(2)}) copy-start(f32[32,32]{1,0:T(8,128)S(1)} %multiply_reduce_fusion.34) | copy-start | bytes 12292 | tf_op jit(solution)/shard_map/while
  212.6 9.8 %copy-start.4 = (f32[32,32,1,128]{3,2,1,0:T(1,128)S(1)}, f32[32,32,1,128]{3,2,1,0:T(1,128)}, u32[]{:S(2)}) copy-start(f32[32,32,1,128]{3,2,1,0:T(1,128)} %copy-done.3) | copy-start | bytes 1572868 | tf_op jit(solution)/shard_map/while
  212.6 9.9 %copy-start.10 = (f32[32,32,128]{2,1,0:T(8,128)S(1)}, f32[32,32,128]{2,1,0:T(8,128)}, u32[]{:S(2)}) copy-start(f32[32,32,128]{2,1,0:T(8,128)} %copy-done.9) | copy-start | bytes 1572868 | tf_op jit(solution)/shard_map/while
  240.8 98.5 %copy-start.22 = (f32[64,128]{1,0:T(8,128)S(1)}, f32[64,128]{1,0:T(8,128)}, u32[]{:S(2)}) copy-start(f32[64,128]{1,0:T(8,128)} %get-tuple-element.1715) | copy-start | bytes 98308 | tf_op jit(solution)/shard_map/while
  240.8 98.5 %copy-start.33 = (f32[32]{0:T(128)S(1)}, f32[32]{0:T(128)}, u32[]{:S(2)}) copy-start(f32[32]{0:T(128)} %copy-done.32) | copy-start | bytes 388 | tf_op jit(solution)/shard_map/while
  240.8 98.5 %copy-start.37 = (f32[128]{0:T(128)S(1)}, f32[128]{0:T(128)}, u32[]{:S(2)}) copy-start(f32[128]{0:T(128)} %copy-done.36) | copy-start | bytes 1540 | tf_op jit(solution)/shard_map/while
  240.8 99.2 %copy-start.20 = (bf16[64,512]{1,0:T(8,128)(2,1)S(1)}, bf16[64,512]{1,0:T(8,128)(2,1)}, u32[]{:S(2)}) copy-start(bf16[64,512]{1,0:T(8,128)(2,1)} %get-tuple-element.1834) | copy-start | bytes 196612 | tf_op jit(solution)/shard_map/while
  358.0 8.6 %copy-start.16 = (f32[32,32]{1,0:T(8,128)}, f32[32,32]{1,0:T(8,128)S(1)}, u32[]{:S(2)}) copy-start(f32[32,32]{1,0:T(8,128)S(1)} %multiply_reduce_fusion.34) | copy-start | bytes 12292 | tf_op jit(solution)/shard_map/while
  392.0 9.8 %copy-start.4 = (f32[32,32,1,128]{3,2,1,0:T(1,128)S(1)}, f32[32,32,1,128]{3,2,1,0:T(1,128)}, u32[]{:S(2)}) copy-start(f32[32,32,1,128]{3,2,1,0:T(1,128)} %copy-done.3) | copy-start | bytes 1572868 | tf_op jit(solution)/shard_map/while
  392.0 9.9 %copy-start.10 = (f32[32,32,128]{2,1,0:T(8,128)S(1)}, f32[32,32,128]{2,1,0:T(8,128)}, u32[]{:S(2)}) copy-start(f32[32,32,128]{2,1,0:T(8,128)} %copy-done.9) | copy-start | bytes 1572868 | tf_op jit(solution)/shard_map/while
  420.2 97.9 %copy-start.22 = (f32[64,128]{1,0:T(8,128)S(1)}, f32[64,128]{1,0:T(8,128)}, u32[]{:S(2)}) copy-start(f32[64,128]{1,0:T(8,128)} %get-tuple-element.1715) | copy-start | bytes 98308 | tf_op jit(solution)/shard_map/while
  420.2 97.9 %copy-start.33 = (f32[32]{0:T(128)S(1)}, f32[32]{0:T(128)}, u32[]{:S(2)}) copy-start(f32[32]{0:T(128)} %copy-done.32) | copy-start | bytes 388 | tf_op jit(solution)/shard_map/while
  420.2 97.9 %copy-start.37 = (f32[128]{0:T(128)S(1)}, f32[128]{0:T(128)}, u32[]{:S(2)}) copy-start(f32[128]{0:T(128)} %copy-done.36) | copy-start | bytes 1540 | tf_op jit(solution)/shard_map/while
  420.2 98.6 %copy-start.20 = (bf16[64,512]{1,0:T(8,128)(2,1)S(1)}, bf16[64,512]{1,0:T(8,128)(2,1)}, u32[]{:S(2)}) copy-start(bf16[64,512]{1,0:T(8,128)(2,1)} %get-tuple-element.1834) | copy-start | bytes 196612 | tf_op jit(solution)/shard_map/while
  524.2 18.1 %collective-permute-start.12 = (bf16[1,3,3,16,512]{4,3,2,1,0:T(8,128)(2,1)S(1)}, bf16[1,3,3,16,512]{4,3,2,1,0:T(8,128)(2,1)}, u32[]{:S(2)}, u32[]{:S(2)}) collective-permute-start(bf16[1,3,3,16,512]{4,3,2,1,0:T(8,128)(2,1)S(1)} %slice.364), channel_id=1, source_target_pairs={{0,32},{32,64},{64,96},{96,128},{128,160},{160,192},{192,224},{224... | collective-permute-start | bytes 442376 | tf_op jit(solution)/shard_map/ppermute | solution.py:27
  526.6 17.1 %collective-permute-start.13 = (bf16[1,3,3,16,512]{4,3,2,1,0:T(8,128)(2,1)S(1)}, bf16[1,3,3,16,512]{4,3,2,1,0:T(8,128)(2,1)S(1)}, u32[]{:S(2)}, u32[]{:S(2)}) collective-permute-start(bf16[1,3,3,16,512]{4,3,2,1,0:T(8,128)(2,1)S(1)} %slice.367), channel_id=1, source_target_pairs={{32,0},{64,32},{96,64},{128,96},{160,128},{192,160},{224,192},{256... | collective-permute-start | bytes 442376 | tf_op jit(solution)/shard_map/ppermute | solution.py:30
  543.8 8.1 %collective-permute-start.15 = (bf16[5,1,3,16,512]{4,3,2,1,0:T(8,128)(2,1)S(1)}, bf16[5,1,3,16,512]{4,3,2,1,0:T(8,128)(2,1)S(1)}, u32[]{:S(2)}, u32[]{:S(2)}) collective-permute-start(bf16[5,1,3,16,512]{4,3,2,1,0:T(8,128)(2,1)S(1)} %get-tuple-element.1289), channel_id=1, source_target_pairs={{8,0},{16,8},{24,16},{0,24},{9,1},{17,9},{25,17},{1,25},{10,2},{18... | collective-permute-start | bytes 737288 | tf_op jit(solution)/shard_map/ppermute | solution.py:30
  547.1 8.1 %collective-permute-start.14 = (bf16[5,1,3,16,512]{4,3,2,1,0:T(8,128)(2,1)S(1)}, bf16[5,1,3,16,512]{4,3,2,1,0:T(8,128)(2,1)S(1)}, u32[]{:S(2)}, u32[]{:S(2)}) collective-permute-start(bf16[5,1,3,16,512]{4,3,2,1,0:T(8,128)(2,1)S(1)} %get-tuple-element.1288), channel_id=1, source_target_pairs={{0,8},{8,16},{16,24},{24,0},{1,9},{9,17},{17,25},{25,1},{2,10},{10... | collective-permute-start | bytes 737288 | tf_op jit(solution)/shard_map/ppermute | solution.py:27
  556.2 19.4 %collective-permute-start.17 = (bf16[5,5,1,16,512]{4,3,2,1,0:T(8,128)(2,1)}, bf16[5,5,1,16,512]{4,3,2,1,0:T(8,128)(2,1)}, u32[]{:S(2)}, u32[]{:S(2)}) collective-permute-start(bf16[5,5,1,16,512]{4,3,2,1,0:T(8,128)(2,1)} %get-tuple-element.1287), channel_id=1, source_target_pairs={{1,0},{2,1},{3,2},{4,3},{5,4},{6,5},{7,6},{0,7},{9,8},{10,9},{11,1... | collective-permute-start | bytes 1228808 | tf_op jit(solution)/shard_map/ppermute | solution.py:30
  558.4 17.1 %collective-permute-start.16 = (bf16[5,5,1,16,512]{4,3,2,1,0:T(8,128)(2,1)}, bf16[5,5,1,16,512]{4,3,2,1,0:T(8,128)(2,1)}, u32[]{:S(2)}, u32[]{:S(2)}) collective-permute-start(bf16[5,5,1,16,512]{4,3,2,1,0:T(8,128)(2,1)} %get-tuple-element.1286), channel_id=1, source_target_pairs={{0,1},{1,2},{2,3},{3,4},{4,5},{5,6},{6,7},{7,0},{8,9},{9,10},{10,1... | collective-permute-start | bytes 1228808 | tf_op jit(solution)/shard_map/ppermute | solution.py:27
  562.8 14.3 %copy-start.39 = (s32[16]{0:T(128)S(1)}, s32[16]{0:T(128)}, u32[]{:S(2)}) copy-start(s32[16]{0:T(128)} %copy-done.38) | copy-start | bytes 196
  562.8 16.4 %copy-start.25 = (bf16[2,8,64]{2,1,0:T(8,128)(2,1)S(1)}, bf16[2,8,64]{2,1,0:T(8,128)(2,1)}, u32[]{:S(2)}) copy-start(bf16[2,8,64]{2,1,0:T(8,128)(2,1)} %get-tuple-element.1822) | copy-start | bytes 6148
  562.8 16.4 %copy-start.27 = (f32[2,128]{1,0:T(2,128)S(1)}, f32[2,128]{1,0:T(2,128)}, u32[]{:S(2)}) copy-start(f32[2,128]{1,0:T(2,128)} %get-tuple-element.1826) | copy-start | bytes 3076
  562.8 16.4 %copy-start.31 = (f32[64]{0:T(128)S(1)}, f32[64]{0:T(128)}, u32[]{:S(2)}) copy-start(f32[64]{0:T(128)} %get-tuple-element.1827) | copy-start | bytes 772
  579.2 90.9 %copy-start.40 = (f32[64]{0:T(128)S(1)}, f32[64]{0:T(128)}, u32[]{:S(2)}) copy-start(f32[64]{0:T(128)} %get-tuple-element.1814) | copy-start | bytes 772
  579.2 90.9 %copy-start.42 = (f32[64]{0:T(128)S(1)}, f32[64]{0:T(128)}, u32[]{:S(2)}) copy-start(f32[64]{0:T(128)} %copy-done.41) | copy-start | bytes 772
  627.8 13.8 %collective-permute-start.19 = (bf16[1,3,3,3,16]{4,2,1,0,3:T(4,128)(2,1)S(1)}, bf16[1,3,3,3,16]{4,2,1,0,3:T(4,128)(2,1)S(1)}, u32[]{:S(2)}, u32[]{:S(2)}) collective-permute-start(bf16[1,3,3,3,16]{4,2,1,0,3:T(4,128)(2,1)S(1)} %get-tuple-element.1297), channel_id=1, source_target_pairs={{32,0},{64,32},{96,64},{128,96},{160,128},{192,160},{224,192},{256... | collective-permute-start | bytes 2600 | tf_op jit(solution)/shard_map/ppermute | solution.py:30
  639.4 15.8 %collective-permute-start.18 = (bf16[1,3,3,3,16]{4,2,1,0,3:T(4,128)(2,1)S(1)}, bf16[1,3,3,3,16]{4,2,1,0,3:T(4,128)(2,1)S(1)}, u32[]{:S(2)}, u32[]{:S(2)}) collective-permute-start(bf16[1,3,3,3,16]{4,2,1,0,3:T(4,128)(2,1)S(1)} %get-tuple-element.1296), channel_id=1, source_target_pairs={{0,32},{32,64},{64,96},{96,128},{128,160},{160,192},{192,224},{224... | collective-permute-start | bytes 2600 | tf_op jit(solution)/shard_map/ppermute | solution.py:27
  655.3 5.9 collective-permute-start.21
  658.6 5.6 collective-permute-start.20
  664.3 6.4 collective-permute-start.23
  666.2 12.3 %collective-permute-start.22 = (bf16[5,5,1,3,16]{4,3,2,1,0:T(4,128)(2,1)S(1)}, bf16[5,5,1,3,16]{4,3,2,1,0:T(4,128)(2,1)S(1)}, u32[]{:S(2)}, u32[]{:S(2)}) collective-permute-start(bf16[5,5,1,3,16]{4,3,2,1,0:T(4,128)(2,1)S(1)} %get-tuple-element.1292), channel_id=1, source_target_pairs={{0,1},{1,2},{2,3},{3,4},{4,5},{5,6},{6,7},{7,0},{8,9},{9,10},{10,1... | collective-permute-start | bytes 7208 | tf_op jit(solution)/shard_map/ppermute | solution.py:27
  (48 other events, 139.2 us)
where the time goes:
time: 693 us; the launch traced here: 680 us
  other arithmetic  327 us (47%)
  starting transfers between devices  103 us (15%)
  waiting for transfers between devices  96.7 us (14%)
  local copies, waits for them, and re-layouts  94 us (14%)
  matrix products  44.3 us (6%)
  loops' own time  13.1 us (2%)
    scatter-add x2, other arithmetic, layer_two(): source = jnp.take(projected, neighbour_rows, axis=0)  196 us
    ppermute x12, waiting for transfers between devices, padded(): lax.ppermute(lax.slice_in_dim(block, block.shape[dim] - width, None, axis...  81.2 us
    ppermute x12, starting transfers between devices, padded(): lax.ppermute(lax.slice_in_dim(block, 0, width, axis=dim), axis, backward)  71.2 us
    ppermute x12, starting transfers between devices, padded(): lax.ppermute(lax.slice_in_dim(block, block.shape[dim] - width, None, axis...  32 us
    scatter-add x4, other arithmetic, pair_terms(): others = jnp.take(positions_all, neighbour_rows, axis=1)  24.5 us
    dot_general x36, matrix products, mixed(): jnp.dot(values, matrix.astype(jnp.float32), precision=lax.Precision.HIGHEST)  20.1 us
    reduce_sum x2, other arithmetic, layer_two(): along_unit = jnp.sum(vector_src * direction, axis=2)  19.5 us
    gather x2, local copies, waits for them, and re-layouts, layer_two(): source = jnp.take(projected, neighbour_rows, axis=0)  18.3 us
  transfers between devices with their start and end apart: 24, of which 14 were waited for; matrix products, arithmetic and copies ran while one was open for 1% of the time, Pallas kernels for 0%

commit v1 on v0

v1 whole, which is shorter than its diff:
```python
import math

import jax
import jax.numpy as jnp
from jax import lax
from jax.experimental import pallas as pl
from jax.experimental.pallas import tpu as pltpu
from jax.sharding import PartitionSpec as P

C = 128
NB = 8
RH = 64
NSPEC = 7
SLOTS = 64
DEPTH = 32
EXPORT = 16
PAIRS = SLOTS * DEPTH
SLAB = 9 * EXPORT
TABLE = 512
LANES = 128
COLUMNS = PAIRS // LANES
DOMAIN_LENGTH = 6.0
CUTOFF = 6.0
SOFTEN = 0.25
NORM = 1.0 / math.sqrt(DEPTH)
AXES = ("gx", "gy", "gz")
F32 = jnp.float32
BF16 = jnp.bfloat16


def dot_nn(a, b):
    return lax.dot_general(a, b, (((1,), (0,)), ((), ())), preferred_element_type=F32)


def dot_nt(a, b):
    return lax.dot_general(a, b, (((1,), (1,)), ((), ())), preferred_element_type=F32)


def dot_tn(a, b):
    return lax.dot_general(a, b, (((0,), (0,)), ((), ())), preferred_element_type=F32)


def iota(shape, dim):
    return lax.broadcasted_iota(jnp.int32, shape, dim)


def column(values, m):
    return values[:, m * LANES : (m + 1) * LANES]


def halves(values):
    high = values.astype(BF16)
    low = (values - high.astype(F32)).astype(BF16)
    return jnp.where(iota(values.shape, 1) % LANES < SLOTS, high.astype(F32), low.astype(F32)).astype(BF16)


def fold(values):
    return values + pltpu.roll(values, SLOTS, 1)


def live_row(count):
    return (iota((1, LANES), 1) % SLOTS < count).astype(F32)


def gather_entries(table, index):
    parts = []
    for m in range(COLUMNS):
        ids = jnp.broadcast_to(column(index, m), (8, LANES))
        low = ids & (LANES - 1)
        high = ids >> 7
        found = jnp.take_along_axis(column(table, 0), low, axis=1)
        for v in range(1, TABLE // LANES):
            found = jnp.where(high == v, jnp.take_along_axis(column(table, v), low, axis=1), found)
        parts.append(found)
    return jnp.concatenate(parts, axis=1)


def sincos_pi(turns):
    whole = jnp.floor(turns + 0.5)
    part = turns - whole
    sign = 1.0 - 2.0 * (whole - 2.0 * jnp.floor(whole * 0.5))
    square = part * part
    sine = 0.0
    cosine = 0.0
    for n in range(6, -1, -1):
        cosine = cosine * square + (-1.0) ** n * math.pi ** (2 * n) / math.factorial(2 * n)
    for n in range(5, -1, -1):
        sine = sine * square + (-1.0) ** n * math.pi ** (2 * n + 1) / math.factorial(2 * n + 1)
    return sine * part * sign, cosine * sign


def geometry(table, index, count, with_slope):
    found = gather_entries(table, index)
    first = column(table, 0)
    centre = jnp.where(iota((8, LANES), 1) < SLOTS, first, pltpu.roll(first, SLOTS, 1))
    centre = jnp.concatenate([centre] * COLUMNS, axis=1)
    rows = iota((8, PAIRS), 0)
    delta = jnp.where(rows < 3, found - centre, 0.0)
    kind = found[3:4, :]
    square = jnp.sum(delta * delta, axis=0, keepdims=True) + SOFTEN
    inverse = lax.rsqrt(square)
    distance = square * inverse
    unit = delta * inverse
    slot = iota((1, PAIRS), 1) % SLOTS
    paired = jnp.where((index != slot) & (slot < count), 1.0, 0.0)
    scaled = jnp.minimum(distance * (1.0 / CUTOFF), 1.0)
    power = scaled * scaled * scaled
    power = power * power
    envelope = 1.0 + power * (-28.0 + scaled * (48.0 - 21.0 * scaled))
    orders = (iota((8, 1), 0) + 1).astype(F32)
    sine, cosine = sincos_pi(orders * scaled)
    weight = envelope * paired * inverse
    basis = (sine * weight).astype(BF16)
    if not with_slope:
        return unit, inverse, kind, basis, None
    rest = 1.0 - scaled
    slope = (-168.0 / CUTOFF) * (power * rest * rest) / jnp.maximum(scaled, 1e-3)
    basis_slope = weight * cosine * (orders * (math.pi / CUTOFF)) + sine * (
        slope * paired * inverse - weight * inverse
    )
    return unit, inverse, kind, basis, basis_slope


def hidden_of(weights, basis):
    before = dot_nn(weights, basis)
    gate = 1.0 / (1.0 + jnp.exp(-before))
    return before, gate


def pair_gradient(unit, inverse, grad_unit, grad_distance):
    along = jnp.sum(grad_unit * unit, axis=0, keepdims=True)
    return inverse * (grad_unit - unit * along) + unit * grad_distance


def stack_rows(rows):
    where = iota((8, rows[0].shape[1]), 0)
    out = jnp.zeros((8, rows[0].shape[1]), F32)
    for r, row in enumerate(rows):
        out = jnp.where(where == r, row, out)
    return out


def start_kernel(exports, positions, species, own, payload, picked):
    own[...] = jnp.zeros_like(own)
    own[0:3, 0:SLOTS] = positions[...]
    own[3:4, 0:SLOTS] = species[...].astype(F32)
    lane = iota((8, LANES), 1) % EXPORT
    row = iota((EXPORT, LANES), 0)
    source = jnp.zeros((8, LANES), jnp.int32)
    pick = jnp.zeros((EXPORT, LANES), jnp.int32)
    for e in range(EXPORT):
        slot = exports[e]
        source = jnp.where(lane == e, slot, source)
        pick = jnp.where(row == e, slot, pick)
    picked[...] = pick
    payload[...] = jnp.take_along_axis(own[...], source, axis=1)


def first_kernel(
    count_ref, own, low, mid, high, index, picked, win_t, wout_t, mix_a, mix_b, mix0_t, emb, emb_t, read_t,
    table, own_rows, outgoing, sums, energy, spread, radial,
):
    count = count_ref[0]
    group = iota((8, LANES), 1) // EXPORT
    rows8 = iota((8, 1), 0)
    tiles = [own[...]] + [jnp.zeros((8, LANES), F32) for _ in range(3)]
    slabs = (low, mid, high)
    for b in range(27):
        oz, oy, ox = b // 9 - 1, b // 3 % 3 - 1, b % 3 - 1
        entry = SLOTS + b * EXPORT
        shift = jnp.where(rows8 == 0, DOMAIN_LENGTH * ox, 0.0)
        shift = jnp.where(rows8 == 1, DOMAIN_LENGTH * oy, shift)
        shift = jnp.where(rows8 == 2, DOMAIN_LENGTH * oz, shift)
        tile = entry // LANES
        at = entry % LANES // EXPORT
        tiles[tile] = jnp.where(group == at, slabs[oz + 1][b % 9] + shift, tiles[tile])
    for v in range(4):
        table[:, v * LANES : (v + 1) * LANES] = tiles[v]
    whole = jnp.concatenate(tiles, axis=1)
    ids = index[...]
    unit, inverse, kind, basis, _ = geometry(whole, ids, count, False)
    before, gate = hidden_of(win_t[...], basis)
    hidden = (before * gate).astype(BF16)
    pe = dot_nt(mix0_t[...], emb[...])
    pe_high = pe.astype(BF16)
    pe_low = (pe - pe_high.astype(F32)).astype(BF16)
    pe_both = jnp.concatenate([pe_high.astype(F32), pe_low.astype(F32)], axis=1).astype(BF16)
    spread[...] = pe_both
    species = (iota((16, PAIRS), 0) % 8 == kind.astype(jnp.int32)).astype(F32).astype(BF16)
    a0 = jnp.zeros((C, LANES), F32)
    a1 = [jnp.zeros((C, LANES), F32) for _ in range(3)]
    for m in range(COLUMNS):
        radial = dot_nn(wout_t[...], column(hidden, m))
        source = dot_nn(pe_both, column(species, m))
        a0 = a0 + radial[:C] * source
        t = radial[C:] * source
        for x in range(3):
            a1[x] = a1[x] + t * column(unit[x : x + 1], m)
    a0 = fold(a0) * NORM
    a1 = [fold(v) * NORM for v in a1]
    for x, v in enumerate([a0] + a1):
        sums[x * C : (x + 1) * C, :] = v
    quad = a1[0] * a1[0] + a1[1] * a1[1] + a1[2] * a1[2]
    own_kind = (iota((8, LANES), 0) == whole[3:4, :LANES].astype(jnp.int32)).astype(F32).astype(BF16)
    own_kind = jnp.where(iota((8, LANES), 1) < SLOTS, own_kind.astype(F32), 0.0).astype(BF16)
    scalar = dot_nn(emb_t[...], own_kind)
    scalar = scalar + dot_nn(mix_a[...], jnp.concatenate([halves(a0), halves(a0 * a0), halves(quad)], axis=0))
    scalar = fold(scalar)
    top = jnp.concatenate([halves(v) for v in a1], axis=1)
    bottom = jnp.concatenate([halves(a0 * v) for v in a1], axis=1)
    vector = dot_nn(mix_b[...], jnp.concatenate([top, bottom], axis=0))
    parts = [scalar] + [fold(column(vector, x)) for x in range(3)]
    features = jnp.concatenate(parts, axis=0).astype(BF16)
    rounded = features[:C].astype(F32)
    row_energy = jnp.sum(scalar * read_t[:, 0:1] + rounded * read_t[:, 1:2], axis=0, keepdims=True)
    energy[...] = row_energy * live_row(count)
    lanes = iota((SLOTS, LANES), 1)
    eye = (lanes == iota((SLOTS, LANES), 0)).astype(F32).astype(BF16)
    chosen = (iota((EXPORT, LANES), 1) == picked[...]).astype(F32).astype(BF16)
    own_rows[...] = dot_nt(eye, features).astype(BF16)
    outgoing[...] = dot_nt(chosen, features).astype(BF16)


def second_kernel(
    count_ref, table, own_rows, low, mid, high, index, win_t, win, wout_t, wout, mix_t, mix_rest, read,
    grad_own, grad_low, grad_mid, grad_high, pair_out, energy,
    feats, projected, onehot, radial, source, grad_radial, grad_source,
):
    count = count_ref[0]
    ids = index[...]
    unit, inverse, _, basis, basis_slope = geometry(table[...], ids, count, True)
    before, gate = hidden_of(win_t[...], basis)
    hidden = (before * gate).astype(BF16)
    feats[0:SLOTS, :] = own_rows[...]
    feats[SLOTS : SLOTS + SLAB, :] = low[...]
    feats[SLOTS + SLAB : SLOTS + 2 * SLAB, :] = mid[...]
    feats[SLOTS + 2 * SLAB : SLOTS + 3 * SLAB, :] = high[...]
    feats[SLOTS + 3 * SLAB :, :] = jnp.zeros((TABLE - SLOTS - 3 * SLAB, 4 * C), BF16)
    for c in range(4):
        projected[c * C : (c + 1) * C, :] = dot_nt(
            mix_t[min(c, 1)], feats[:, c * C : (c + 1) * C]
        ).astype(BF16)
    entry = iota((TABLE, LANES), 0)
    for m in range(COLUMNS):
        onehot[:, m * LANES : (m + 1) * LANES] = (entry == column(ids, m)).astype(F32).astype(BF16)
    units = [[column(unit[x : x + 1], m) for m in range(COLUMNS)] for x in range(3)]
    wide = 2 * LANES
    a0 = jnp.zeros((C, LANES), F32)
    a1 = [jnp.zeros((C, LANES), F32) for _ in range(3)]
    for w in range(PAIRS // wide):
        at = slice(w * wide, (w + 1) * wide)
        radial[:, at] = dot_nn(wout_t[...], hidden[:, at])
        source[:, at] = dot_nn(projected[...], onehot[:, at])
        for m in (2 * w, 2 * w + 1):
            here = slice(m * LANES, (m + 1) * LANES)
            s = source[0:C, here]
            v = [source[(x + 1) * C : (x + 2) * C, here] for x in range(3)]
            u = [units[x][m] for x in range(3)]
            along = v[0] * u[0] + v[1] * u[1] + v[2] * u[2]
            a0 = a0 + radial[0:C, here] * s + radial[3 * C :, here] * along
            t = radial[C : 2 * C, here] * s
            r3 = radial[2 * C : 3 * C, here]
            for x in range(3):
                a1[x] = a1[x] + t * u[x] + r3 * v[x]
    a0 = fold(a0) * NORM
    a1 = [fold(v) * NORM for v in a1]
    quad = a1[0] * a1[0] + a1[1] * a1[1] + a1[2] * a1[2]
    read_high = read[...].astype(BF16)
    read_low = (read[...] - read_high.astype(F32)).astype(BF16)
    rests = dot_nt(mix_rest[...], read_high) + dot_nt(mix_rest[...], read_low)
    m2, m3, m4 = [rests[k * C : (k + 1) * C, 1:2] for k in range(3)]
    live = live_row(count)
    energy[...] = live * jnp.sum(a0 * m2 + a0 * a0 * m3 + quad * m4, axis=0, keepdims=True)
    live = live * NORM
    d0 = (m2 + 2.0 * a0 * m3) * live
    d1 = [2.0 * v * m4 * live for v in a1]
    grad_units = [[], [], []]
    for m in range(COLUMNS):
        here = slice(m * LANES, (m + 1) * LANES)
        s = source[0:C, here]
        v = [source[(x + 1) * C : (x + 2) * C, here] for x in range(3)]
        u = [units[x][m] for x in range(3)]
        r1, r2, r3, r4 = [radial[k * C : (k + 1) * C, here] for k in range(4)]
        along = v[0] * u[0] + v[1] * u[1] + v[2] * u[2]
        slant = d1[0] * u[0] + d1[1] * u[1] + d1[2] * u[2]
        grad_radial[0:C, here] = (d0 * s).astype(BF16)
        grad_radial[C : 2 * C, here] = (s * slant).astype(BF16)
        grad_radial[2 * C : 3 * C, here] = (d1[0] * v[0] + d1[1] * v[1] + d1[2] * v[2]).astype(BF16)
        grad_radial[3 * C :, here] = (d0 * along).astype(BF16)
        grad_source[0:C, here] = (r1 * d0 + r2 * slant).astype(BF16)
        q = d0 * r4
        t = r2 * s
        for x in range(3):
            grad_source[(x + 1) * C : (x + 2) * C, here] = (q * u[x] + r3 * d1[x]).astype(BF16)
            grad_units[x].append(jnp.sum(q * v[x] + t * d1[x], axis=0, keepdims=True))
    grad_unit = stack_rows([jnp.concatenate(g, axis=1) for g in grad_units])
    grad_hidden = dot_nn(wout[...], grad_radial[...])
    grad_before = (grad_hidden * (gate * (1.0 + before * (1.0 - gate)))).astype(BF16)
    grad_basis = dot_nn(win[...], grad_before)
    grad_distance = jnp.sum(grad_basis * basis_slope, axis=0, keepdims=True)
    pair_out[...] = pair_gradient(unit, inverse, grad_unit, grad_distance)
    grad_projected = dot_nt(onehot[...], grad_source[...])
    outs = (grad_low, grad_mid, grad_high)
    live_rows = (iota((SLOTS, 1), 0) < count).astype(F32)
    for c in range(4):
        at = slice(c * C, (c + 1) * C)
        rows = dot_nn(grad_projected[:, at].astype(BF16), mix_t[min(c, 1)])
        mine = rows[0:SLOTS]
        if c == 0:
            mine = mine + live_rows * read[1:2, :]
        grad_own[:, at] = mine
        for k in range(3):
            begin = SLOTS + k * SLAB
            outs[k][:, at] = rows[begin : begin + SLAB].astype(BF16)


def third_kernel(
    count_ref, table, sums, grad_own, back, picked, pair_in, index, win_t, win, wout_t, wout, mix_rest, spread, read_t,
    grad_mine, grad_low, grad_mid, grad_high,
    onehot, grad_radial,
):
    count = count_ref[0]
    ids = index[...]
    unit, inverse, kind, basis, basis_slope = geometry(table[...], ids, count, True)
    before, gate = hidden_of(win_t[...], basis)
    hidden = (before * gate).astype(BF16)
    species = (iota((16, PAIRS), 0) % 8 == kind.astype(jnp.int32)).astype(F32).astype(BF16)
    entry = iota((TABLE, LANES), 0)
    for m in range(COLUMNS):
        onehot[:, m * LANES : (m + 1) * LANES] = (entry == column(ids, m)).astype(F32).astype(BF16)
    mine = grad_own[...]
    mine_high = mine.astype(BF16)
    mine_low = (mine - mine_high.astype(F32)).astype(BF16)
    came = back[...].astype(F32)
    came_high = came.astype(BF16)
    came_low = (came - came_high.astype(F32)).astype(BF16)
    eye = (iota((SLOTS, LANES), 1) % SLOTS == iota((SLOTS, LANES), 0)).astype(F32).astype(BF16)
    chosen = (iota((EXPORT, LANES), 1) % SLOTS == picked[...]).astype(F32).astype(BF16)
    left = jnp.concatenate([mine_high, mine_low, came_high, came_low], axis=0)
    right = jnp.concatenate([eye, eye, chosen, chosen], axis=0)
    grads = dot_tn(left, right)
    live = live_row(count)
    gs = grads[0:C] + read_t[:, 0:1] * live
    gv = [grads[(x + 1) * C : (x + 2) * C] for x in range(3)]
    a0 = sums[0:C, :]
    a1 = [sums[(x + 1) * C : (x + 2) * C, :] for x in range(3)]
    first = fold(dot_nn(mix_rest[0 : 3 * C, :], halves(gs)))
    others = fold_columns(dot_nn(mix_rest[3 * C : 5 * C, :], jnp.concatenate([halves(g) for g in gv], axis=1)))
    straight = [column(others[0:C], x) for x in range(3)]
    crossed = [column(others[C : 2 * C], x) for x in range(3)]
    scale = live * NORM
    d0 = first[0:C] + 2.0 * a0 * first[C : 2 * C]
    for x in range(3):
        d0 = d0 + a1[x] * crossed[x]
    d0 = d0 * scale
    d1 = [(straight[x] + a0 * crossed[x] + 2.0 * a1[x] * first[2 * C : 3 * C]) * scale for x in range(3)]
    grad_units = [[], [], []]
    for m in range(COLUMNS):
        here = slice(m * LANES, (m + 1) * LANES)
        r2 = dot_nn(wout_t[C : 2 * C, :], column(hidden, m))
        source = dot_nn(spread[...], column(species, m))
        u = [column(unit[x : x + 1], m) for x in range(3)]
        slant = d1[0] * u[0] + d1[1] * u[1] + d1[2] * u[2]
        grad_radial[0:C, here] = (d0 * source).astype(BF16)
        grad_radial[C:, here] = (slant * source).astype(BF16)
        q = r2 * source
        for x in range(3):
            grad_units[x].append(jnp.sum(q * d1[x], axis=0, keepdims=True))
    grad_unit = stack_rows([jnp.concatenate(g, axis=1) for g in grad_units])
    grad_hidden = dot_nn(wout[...], grad_radial[...])
    grad_before = (grad_hidden * (gate * (1.0 + before * (1.0 - gate)))).astype(BF16)
    grad_basis = dot_nn(win[...], grad_before)
    grad_distance = jnp.sum(grad_basis * basis_slope, axis=0, keepdims=True)
    pairs = pair_in[...] + pair_gradient(unit, inverse, grad_unit, grad_distance)
    pair_high = pairs.astype(BF16)
    pair_low = (pairs - pair_high.astype(F32)).astype(BF16)
    both = jnp.concatenate([pair_high.astype(F32), pair_low.astype(F32)], axis=0).astype(BF16)
    spread_back = dot_nt(both, onehot[...])
    grads = spread_back[0:8] + spread_back[8:16]
    total = column(pairs, 0)
    for m in range(1, COLUMNS):
        total = total + column(pairs, m)
    grad_mine[...] = column(grads, 0) - fold(total)
    outs = (grad_low, grad_mid, grad_high)
    for b in range(27):
        at = SLOTS + b * EXPORT
        tile = column(grads, at // LANES)
        offset = at % LANES
        if offset:
            tile = pltpu.roll(tile, LANES - offset, 1)
        outs[b // 9][b % 9] = tile


def fold_columns(values):
    count = values.shape[1] // LANES
    return jnp.concatenate([fold(column(values, x)) for x in range(count)], axis=1)


def last_kernel(exports, count_ref, grad_mine, back, energy_one, energy_two, forces, energies):
    lane = iota((8, LANES), 1)
    total = grad_mine[...]
    came = back[...]
    source = jnp.zeros((8, LANES), jnp.int32)
    hit = jnp.zeros((8, LANES), F32)
    for e in range(EXPORT):
        same = lane == exports[e]
        source = jnp.where(same, e, source)
        hit = jnp.where(same, 1.0, hit)
    total = total + jnp.where(hit > 0.5, jnp.take_along_axis(came, source, axis=1), 0.0)
    forces[...] = -total[0:3, 0:SLOTS]
    energies[...] = (live_row(count_ref[0]) * (energy_one[...] + energy_two[...]))[:, 0:SLOTS]


def call(kernel, outs, specs, scratch=(), limit=None, smem=0):
    count = len(specs)
    in_specs = [pl.BlockSpec(memory_space=pltpu.SMEM)] * smem
    in_specs += [pl.BlockSpec(memory_space=pltpu.VMEM)] * (count - smem)
    many = isinstance(outs, (list, tuple))
    return pl.pallas_call(
        kernel,
        out_shape=[jax.ShapeDtypeStruct(s, t) for s, t in outs],
        in_specs=in_specs,
        out_specs=[pl.BlockSpec(memory_space=pltpu.VMEM)] * len(outs),
        scratch_shapes=[pltpu.VMEM(s, t) for s, t in scratch],
        compiler_params=pltpu.CompilerParams(vmem_limit_bytes=limit or (16 << 20)),
    )(*specs)


def domain(x, y, z):
    return (x % 16 * 4 + y % 4) * 8 + z % 8


def moves(step):
    sx, sy, sz = step
    return [
        (domain(x, y, z), domain(x + sx, y + sy, z + sz))
        for x in range(16)
        for y in range(4)
        for z in range(8)
    ]


UP = ((1, 0, 0), (0, 1, 0), (0, 0, 1))
DOWN = ((-1, 0, 0), (0, -1, 0), (0, 0, -1))


def send(value, step):
    return lax.ppermute(value, AXES, moves(step))


def spread_halo(block):
    for axis in range(2):
        low = send(block, UP[axis])
        high = send(block, DOWN[axis])
        block = jnp.concatenate([low, block, high], axis=0)
    return send(block, UP[2]), block, send(block, DOWN[2])


def gather_halo(low, mid, high):
    for axis in (2, 1, 0):
        from_low = send(high, UP[axis])
        from_high = send(low, DOWN[axis])
        block = mid + from_low + from_high
        if axis:
            third = block.shape[0] // 3
            low, mid, high = block[:third], block[third : 2 * third], block[2 * third :]
    return block


def body(
    positions, species, counts, neighbours, exports, embedding, radial_in,
    radial_out_one, radial_out_two, mix_one, mix_two, readout,
):
    own, payload, picked = call(
        start_kernel,
        [((8, LANES), F32), ((8, LANES), F32), ((EXPORT, LANES), jnp.int32)],
        [exports, positions, species.reshape(1, SLOTS)],
        smem=1,
    )
    block = (neighbours - SLOTS) // EXPORT
    turned = block % 3 * 9 + block // 3 % 3 * 3 + block // 9
    moved = SLOTS + turned * EXPORT + neighbours % EXPORT
    index = jnp.where(neighbours < SLOTS, neighbours, moved).reshape(1, PAIRS)
    emb = jnp.concatenate([embedding, jnp.zeros((1, C), BF16)], axis=0)
    emb_t = emb.T
    win_t = jnp.swapaxes(radial_in, 1, 2)
    one_t = radial_out_one.T
    two_t = radial_out_two.T
    mix0_t = mix_one[0].T
    mix_a = mix_one[1:4].reshape(3 * C, C).T
    mix_b = mix_one[4:6].reshape(2 * C, C).T
    mix_back = mix_one[1:6].reshape(5 * C, C)
    mix_two_t = jnp.swapaxes(mix_two[0:2], 1, 2)
    mix_two_rest = mix_two[2:5].reshape(3 * C, C)
    read_t = readout.T
    read = jnp.concatenate([readout, jnp.zeros((6, C), F32)], axis=0)

    low, mid, high = spread_halo(payload[None])
    table, own_rows, outgoing, sums, energy_one, spread = call(
        lambda *refs: first_kernel(*refs, None),
        [
            ((8, TABLE), F32),
            ((SLOTS, 4 * C), BF16),
            ((EXPORT, 4 * C), BF16),
            ((4 * C, LANES), F32),
            ((1, LANES), F32),
            ((C, 16), BF16),
        ],
        [counts, own, low, mid, high, index, picked, win_t[0], one_t, mix_a, mix_b, mix0_t, emb, emb_t, read_t],
        smem=1,
    )
    low, mid, high = spread_halo(outgoing)
    grad_own, grad_low, grad_mid, grad_high, pairs, energy_two = call(
        second_kernel,
        [
            ((SLOTS, 4 * C), F32),
            ((SLAB, 4 * C), BF16),
            ((SLAB, 4 * C), BF16),
            ((SLAB, 4 * C), BF16),
            ((8, PAIRS), F32),
            ((1, LANES), F32),
        ],
        [
            counts, table, own_rows, low, mid, high, index, win_t[1], radial_in[1], two_t, radial_out_two,
            mix_two_t, mix_two_rest, read,
        ],
        scratch=[
            ((TABLE, 4 * C), BF16),
            ((4 * C, TABLE), BF16),
            ((TABLE, PAIRS), BF16),
            ((4 * C, PAIRS), F32),
            ((4 * C, PAIRS), F32),
            ((4 * C, PAIRS), BF16),
            ((4 * C, PAIRS), BF16),
        ],
        limit=48 << 20,
        smem=1,
    )
    back = gather_halo(grad_low, grad_mid, grad_high)
    grad_mine, grad_low, grad_mid, grad_high = call(
        third_kernel,
        [((8, LANES), F32), ((9, 8, LANES), F32), ((9, 8, LANES), F32), ((9, 8, LANES), F32)],
        [
            counts, table, sums, grad_own, back, picked, pairs, index, win_t[0], radial_in[0], one_t,
            radial_out_one, mix_back, spread, read_t,
        ],
        scratch=[((TABLE, PAIRS), BF16), ((2 * C, PAIRS), BF16)],
        limit=32 << 20,
        smem=1,
    )
    back = gather_halo(grad_low, grad_mid, grad_high)
    forces, energies = call(
        last_kernel,
        [((3, SLOTS), F32), ((1, SLOTS), F32)],
        [exports, counts, grad_mine, back[0], energy_one, energy_two],
        smem=2,
    )
    return forces, energies.reshape(SLOTS)


def solution(mesh):
    whole = P()
    split = P(AXES)
    in_specs = (P(None, AXES), split, split, P(None, AXES), split) + (whole,) * 7
    out_specs = (P(None, AXES), split)
    return jax.shard_map(body, mesh=mesh, in_specs=in_specs, out_specs=out_specs, check_vma=False)
```

time: 693 us -> 209 us (0.30)
  the two profiles are of different devices: /device:TPU:8 before, /device:TPU:503 now
where the time goes in v1:
time: 209 us; the launch traced here: 208 us
  starting transfers between devices  114 us (55%)
  waiting for transfers between devices  73.1 us (35%)
  Pallas kernels  13.4 us (6%)
  local copies, waits for them, and re-layouts  6.1 us (3%)
    ppermute x24, starting transfers between devices, send(): return lax.ppermute(value, AXES, moves(step))  114 us
    ppermute x24, waiting for transfers between devices, send(): return lax.ppermute(value, AXES, moves(step))  73.1 us
    pallas_call x5, Pallas kernels, call(): pl.pallas_call(kernel, out_shape=[jax.ShapeDtypeStruct(s, t) for s, t in...  13.4 us
    unnamed x40, local copies, waits for them, and re-layouts  4.2 us
  transfers between devices with their start and end apart: 24, of which 13 were waited for; matrix products, arithmetic and copies ran while one was open for 1% of the time, Pallas kernels for 0%

profile of v1, /device:TPU:503, one launch (start us, length us, event | category | flops | bytes accessed | tf_op | source)
XLA Modules:
  0.0 208.4 jit_solution(12731363306356936844)
XLA Ops:
  0.7 0.6 copy-done.3
  1.3 0.7 copy-done.2
  2.0 0.6 shard_map.131
  2.6 2.6 %collective-permute-start.1 = (f32[1,8,128]{2,1,0:T(8,128)S(1)}, f32[1,8,128]{2,1,0:T(8,128)S(1)}, u32[]{:S(2)}, u32[]{:S(2)}) collective-permute-start(f32[1,8,128]{2,1,0:T(8,128)S(1)} %bitcast.41), channel_id=1, source_target_pairs={{0,480},{1,481},{2,482},{3,483},{4,484},{5,485},{6,486},{7,487},{8... | collective-permute-start | bytes 12296 | tf_op jit(solution)/shard_map/ppermute | solution.py:448
  5.2 13.8 %collective-permute-start = (f32[1,8,128]{2,1,0:T(8,128)S(1)}, f32[1,8,128]{2,1,0:T(8,128)S(1)}, u32[]{:S(2)}, u32[]{:S(2)}) collective-permute-start(f32[1,8,128]{2,1,0:T(8,128)S(1)} %bitcast.42), channel_id=1, source_target_pairs={{0,32},{1,33},{2,34},{3,35},{4,36},{5,37},{6,38},{7,39},{8,40},{9,... | collective-permute-start | bytes 12296 | tf_op jit(solution)/shard_map/ppermute | solution.py:448
  19.1 0.6 collective-permute-done
  19.7 3.0 %collective-permute-start.2 = (f32[3,8,128]{2,1,0:T(8,128)S(1)}, f32[3,8,128]{2,1,0:T(8,128)S(1)}, u32[]{:S(2)}, u32[]{:S(2)}) collective-permute-start(f32[3,8,128]{2,1,0:T(8,128)S(1)} %pad_maximum_fusion), channel_id=1, source_target_pairs={{0,8},{1,9},{2,10},{3,11},{4,12},{5,13},{6,14},{7,15},{8,16},{9,17... | collective-permute-start | bytes 36872 | tf_op jit(solution)/shard_map/ppermute | solution.py:448
  23.0 2.4 %collective-permute-start.3 = (f32[3,8,128]{2,1,0:T(8,128)S(1)}, f32[3,8,128]{2,1,0:T(8,128)S(1)}, u32[]{:S(2)}, u32[]{:S(2)}) collective-permute-start(f32[3,8,128]{2,1,0:T(8,128)S(1)} %pad_maximum_fusion), channel_id=1, source_target_pairs={{0,24},{1,25},{2,26},{3,27},{4,28},{5,29},{6,30},{7,31},{8,0},{9,1... | collective-permute-start | bytes 36872 | tf_op jit(solution)/shard_map/ppermute | solution.py:448
  25.4 2.0 collective-permute-done.3
  27.4 2.6 %collective-permute-start.5 = (f32[9,8,128]{2,1,0:T(8,128)S(1)}, f32[9,8,128]{2,1,0:T(8,128)S(1)}, u32[]{:S(2)}, u32[]{:S(2)}) collective-permute-start(f32[9,8,128]{2,1,0:T(8,128)S(1)} %constant_dynamic-update-slice_fusion.refs_3_), channel_id=1, source_target_pairs={{0,7},{1,0},{2,1},{3,2},{4,3},{5,4},{6,5},{7,6},{8,15},{9,8},{10,9... | collective-permute-start | bytes 110600 | tf_op jit(solution)/shard_map/ppermute | solution.py:448
  30.1 9.3 %collective-permute-start.4 = (f32[9,8,128]{2,1,0:T(8,128)S(1)}, f32[9,8,128]{2,1,0:T(8,128)S(1)}, u32[]{:S(2)}, u32[]{:S(2)}) collective-permute-start(f32[9,8,128]{2,1,0:T(8,128)S(1)} %constant_dynamic-update-slice_fusion.refs_3_), channel_id=1, source_target_pairs={{0,1},{1,2},{2,3},{3,4},{4,5},{5,6},{6,7},{7,0},{8,9},{9,10},{10,1... | collective-permute-start | bytes 110600 | tf_op jit(solution)/shard_map/ppermute | solution.py:448
  40.3 0.6 copy-done.1
  41.1 0.6 copy-done.9
  41.9 0.6 slice-done.2
  42.7 1.6 shard_map.132
  44.3 17.1 %collective-permute-start.6 = (bf16[16,512]{1,0:T(8,128)(2,1)S(1)}, bf16[16,512]{1,0:T(8,128)(2,1)S(1)}, u32[]{:S(2)}, u32[]{:S(2)}) collective-permute-start(bf16[16,512]{1,0:T(8,128)(2,1)S(1)} %get-tuple-element.29), channel_id=1, source_target_pairs={{0,32},{1,33},{2,34},{3,35},{4,36},{5,37},{6,38},{7,39},{8,40},{9,... | collective-permute-start | bytes 49160 | tf_op jit(solution)/shard_map/ppermute | solution.py:448
  61.5 1.9 collective-permute-start.7
  63.4 14.0 %collective-permute-done.7 = bf16[16,512]{1,0:T(8,128)(2,1)S(1)} collective-permute-done((bf16[16,512]{1,0:T(8,128)(2,1)S(1)}, bf16[16,512]{1,0:T(8,128)(2,1)S(1)}, u32[]{:S(2)}, u32[]{:S(2)}) %collective-permute-start.7) | collective-permute-done | bytes 16416 | tf_op jit(solution)/shard_map/ppermute | solution.py:448
  77.5 3.1 %collective-permute-start.8 = (bf16[48,512]{1,0:T(8,128)(2,1)S(1)}, bf16[48,512]{1,0:T(8,128)(2,1)S(1)}, u32[]{:S(2)}, u32[]{:S(2)}) collective-permute-start(bf16[48,512]{1,0:T(8,128)(2,1)S(1)} %constant_dynamic-update-slice_fusion.5), channel_id=1, source_target_pairs={{0,8},{1,9},{2,10},{3,11},{4,12},{5,13},{6,14},{7,15},{8,16},{9,17... | collective-permute-start | bytes 147464 | tf_op jit(solution)/shard_map/ppermute | solution.py:448
  80.6 0.8 slice-done.3
  81.5 0.7 copy-done
  82.3 2.2 %collective-permute-start.9 = (bf16[48,512]{1,0:T(8,128)(2,1)S(1)}, bf16[48,512]{1,0:T(8,128)(2,1)S(1)}, u32[]{:S(2)}, u32[]{:S(2)}) collective-permute-start(bf16[48,512]{1,0:T(8,128)(2,1)S(1)} %constant_dynamic-update-slice_fusion.5), channel_id=1, source_target_pairs={{0,24},{1,25},{2,26},{3,27},{4,28},{5,29},{6,30},{7,31},{8,0},{9,1... | collective-permute-start | bytes 147464 | tf_op jit(solution)/shard_map/ppermute | solution.py:448
  84.6 2.8 %collective-permute-done.9 = bf16[48,512]{1,0:T(8,128)(2,1)S(1)} collective-permute-done((bf16[48,512]{1,0:T(8,128)(2,1)S(1)}, bf16[48,512]{1,0:T(8,128)(2,1)S(1)}, u32[]{:S(2)}, u32[]{:S(2)}) %collective-permute-start.9) | collective-permute-done | bytes 49184 | tf_op jit(solution)/shard_map/ppermute | solution.py:448
  87.5 1.9 collective-permute-start.11
  89.4 10.0 %collective-permute-start.10 = (bf16[144,512]{1,0:T(8,128)(2,1)S(1)}, bf16[144,512]{1,0:T(8,128)(2,1)S(1)}, u32[]{:S(2)}, u32[]{:S(2)}) collective-permute-start(bf16[144,512]{1,0:T(8,128)(2,1)S(1)} %constant_dynamic-update-slice_fusion.8.mid), channel_id=1, source_target_pairs={{0,1},{1,2},{2,3},{3,4},{4,5},{5,6},{6,7},{7,0},{8,9},{9,10},{10,1... | collective-permute-start | bytes 442376 | tf_op jit(solution)/shard_map/ppermute | solution.py:448
  99.4 0.7 collective-permute-done.11.high
  100.1 1.3 collective-permute-done.10.low
  101.4 7.3 %shard_map.133 = (f32[64,512]{1,0:T(8,128)S(1)}, bf16[144,512]{1,0:T(8,128)(2,1)S(1)}, bf16[144,512]{1,0:T(8,128)(2,1)S(1)}, bf16[144,512]{1,0:T(8,128)(2,1)S(1)...) custom-call(s32[1]{0:T(128)S(6)} %copy.48.refs_0_.count_ref, f32[8,512]{1,0:T(8,128)S(1)} %get-tuple-element.26.table, ...), custom_call_target="tpu_custom_call" | custom-call | tf_op jit(solution)/shard_map/pallas_call | solution.py:419
  108.8 10.6 %collective-permute-start.12 = (bf16[144,512]{1,0:T(8,128)(2,1)S(1)}, bf16[144,512]{1,0:T(8,128)(2,1)S(1)}, u32[]{:S(2)}, u32[]{:S(2)}) collective-permute-start(bf16[144,512]{1,0:T(8,128)(2,1)S(1)} %get-tuple-element.32), channel_id=1, source_target_pairs={{0,1},{1,2},{2,3},{3,4},{4,5},{5,6},{6,7},{7,0},{8,9},{9,10},{10,1... | collective-permute-start | bytes 442376 | tf_op jit(solution)/shard_map/ppermute | solution.py:448
  119.3 1.9 collective-permute-start.13
  121.4 10.4 %collective-permute-done.13 = bf16[144,512]{1,0:T(8,128)(2,1)S(1)} collective-permute-done((bf16[144,512]{1,0:T(8,128)(2,1)S(1)}, bf16[144,512]{1,0:T(8,128)(2,1)S(1)}, u32[]{:S(2)}, u32[]{:S(2)}) %collective-permute-start.13) | collective-permute-done | bytes 147488 | tf_op jit(solution)/shard_map/ppermute | solution.py:448
  131.9 3.3 %collective-permute-start.14 = (bf16[48,512]{1,0:T(8,128)(2,1)S(1)}, bf16[48,512]{1,0:T(8,128)(2,1)S(1)}, u32[]{:S(2)}, u32[]{:S(2)}) collective-permute-start(bf16[48,512]{1,0:T(8,128)(2,1)S(1)} %get-tuple-element.44), channel_id=1, source_target_pairs={{0,8},{1,9},{2,10},{3,11},{4,12},{5,13},{6,14},{7,15},{8,16},{9,17... | collective-permute-start | bytes 147464 | tf_op jit(solution)/shard_map/ppermute | solution.py:448
  135.2 2.1 collective-permute-start.15
  137.3 2.7 %collective-permute-done.15 = bf16[48,512]{1,0:T(8,128)(2,1)S(1)} collective-permute-done((bf16[48,512]{1,0:T(8,128)(2,1)S(1)}, bf16[48,512]{1,0:T(8,128)(2,1)S(1)}, u32[]{:S(2)}, u32[]{:S(2)}) %collective-permute-start.15) | collective-permute-done | bytes 49184 | tf_op jit(solution)/shard_map/ppermute | solution.py:448
  140.1 7.1 %collective-permute-start.16 = (bf16[16,512]{1,0:T(8,128)(2,1)S(1)}, bf16[16,512]{1,0:T(8,128)(2,1)S(1)}, u32[]{:S(2)}, u32[]{:S(2)}) collective-permute-start(bf16[16,512]{1,0:T(8,128)(2,1)S(1)} %get-tuple-element.46), channel_id=1, source_target_pairs={{0,32},{1,33},{2,34},{3,35},{4,36},{5,37},{6,38},{7,39},{8,40},{9,... | collective-permute-start | bytes 49160 | tf_op jit(solution)/shard_map/ppermute | solution.py:448
  147.2 2.1 %collective-permute-start.17 = (bf16[16,512]{1,0:T(8,128)(2,1)S(1)}, bf16[16,512]{1,0:T(8,128)(2,1)S(1)}, u32[]{:S(2)}, u32[]{:S(2)}) collective-permute-start(bf16[16,512]{1,0:T(8,128)(2,1)S(1)} %get-tuple-element.47), channel_id=1, source_target_pairs={{0,480},{1,481},{2,482},{3,483},{4,484},{5,485},{6,486},{7,487},{8... | collective-permute-start | bytes 49160 | tf_op jit(solution)/shard_map/ppermute | solution.py:448
  149.4 13.7 %collective-permute-done.17 = bf16[16,512]{1,0:T(8,128)(2,1)S(1)} collective-permute-done((bf16[16,512]{1,0:T(8,128)(2,1)S(1)}, bf16[16,512]{1,0:T(8,128)(2,1)S(1)}, u32[]{:S(2)}, u32[]{:S(2)}) %collective-permute-start.17) | collective-permute-done | bytes 16416 | tf_op jit(solution)/shard_map/ppermute | solution.py:448
  163.1 2.7 %shard_map.134 = (f32[8,128]{1,0:T(8,128)S(1)}, f32[9,8,128]{2,1,0:T(8,128)S(1)}, f32[9,8,128]{2,1,0:T(8,128)S(1)}, f32[9,8,128]{2,1,0:T(8,128)S(1)}) custom-call(s32[1]{0:T(128)S(6)} %copy.48.refs_0_.count_ref, f32[8,512]{1,0:T(8,128)S(1)} %get-tuple-element.26.table, f32[512,128]{1,0:T(8,128)S(1)} %get-tuple-element.27.sums, ...), custom_call_target="tpu_custom_call" | custom-call | tf_op jit(solution)/shard_map/pallas_call | solution.py:419
  165.8 1.9 collective-permute-start.18
  167.8 3.4 %collective-permute-start.19 = (f32[9,8,128]{2,1,0:T(8,128)S(1)}, f32[9,8,128]{2,1,0:T(8,128)S(1)}, u32[]{:S(2)}, u32[]{:S(2)}) collective-permute-start(f32[9,8,128]{2,1,0:T(8,128)S(1)} %get-tuple-element.39), channel_id=1, source_target_pairs={{0,7},{1,0},{2,1},{3,2},{4,3},{5,4},{6,5},{7,6},{8,15},{9,8},{10,9... | collective-permute-start | bytes 110600 | tf_op jit(solution)/shard_map/ppermute | solution.py:448
  171.1 7.9 %collective-permute-done.19 = f32[9,8,128]{2,1,0:T(8,128)S(1)} collective-permute-done((f32[9,8,128]{2,1,0:T(8,128)S(1)}, f32[9,8,128]{2,1,0:T(8,128)S(1)}, u32[]{:S(2)}, u32[]{:S(2)}) %collective-permute-start.19) | collective-permute-done | bytes 36896 | tf_op jit(solution)/shard_map/ppermute | solution.py:448
  179.1 3.4 %collective-permute-start.20 = (f32[3,8,128]{2,1,0:T(8,128)S(1)}, f32[3,8,128]{2,1,0:T(8,128)S(1)}, u32[]{:S(2)}, u32[]{:S(2)}) collective-permute-start(f32[3,8,128]{2,1,0:T(8,128)S(1)} %get-tuple-element.48), channel_id=1, source_target_pairs={{0,8},{1,9},{2,10},{3,11},{4,12},{5,13},{6,14},{7,15},{8,16},{9,17... | collective-permute-start | bytes 36872 | tf_op jit(solution)/shard_map/ppermute | solution.py:448
  182.5 1.9 collective-permute-start.21
  184.4 2.8 %collective-permute-done.21 = f32[3,8,128]{2,1,0:T(8,128)S(1)} collective-permute-done((f32[3,8,128]{2,1,0:T(8,128)S(1)}, f32[3,8,128]{2,1,0:T(8,128)S(1)}, u32[]{:S(2)}, u32[]{:S(2)}) %collective-permute-start.21) | collective-permute-done | bytes 12320 | tf_op jit(solution)/shard_map/ppermute | solution.py:448
  187.2 4.2 %collective-permute-start.22 = (f32[1,8,128]{2,1,0:T(8,128)S(1)}, f32[1,8,128]{2,1,0:T(8,128)S(1)}, u32[]{:S(2)}, u32[]{:S(2)}) collective-permute-start(f32[1,8,128]{2,1,0:T(8,128)S(1)} %get-tuple-element.52), channel_id=1, source_target_pairs={{0,32},{1,33},{2,34},{3,35},{4,36},{5,37},{6,38},{7,39},{8,40},{9,... | collective-permute-start | bytes 12296 | tf_op jit(solution)/shard_map/ppermute | solution.py:448
  191.4 1.9 collective-permute-start.23
  193.4 13.8 %collective-permute-done.23 = f32[1,8,128]{2,1,0:T(8,128)S(1)} collective-permute-done((f32[1,8,128]{2,1,0:T(8,128)S(1)}, f32[1,8,128]{2,1,0:T(8,128)S(1)}, u32[]{:S(2)}, u32[]{:S(2)}) %collective-permute-start.23) | collective-permute-done | bytes 4128 | tf_op jit(solution)/shard_map/ppermute | solution.py:448
  207.2 1.2 shard_map.135
  (78 shorter events, 1.8 us)
Async XLA Ops:
  0.6 0.7 copy-start.3
  0.6 0.7 copy-start.4
  1.3 0.7 copy-start.2
  2.0 17.0 %copy-start.7 = (bf16[2,8,64]{2,1,0:T(8,128)(2,1)S(1)}, bf16[2,8,64]{2,1,0:T(8,128)(2,1)}, u32[]{:S(2)}) copy-start(bf16[2,8,64]{2,1,0:T(8,128)(2,1)} %param.18) | copy-start | bytes 6148
  2.6 16.5 %collective-permute-start.1 = (f32[1,8,128]{2,1,0:T(8,128)S(1)}, f32[1,8,128]{2,1,0:T(8,128)S(1)}, u32[]{:S(2)}, u32[]{:S(2)}) collective-permute-start(f32[1,8,128]{2,1,0:T(8,128)S(1)} %bitcast.41), channel_id=1, source_target_pairs={{0,480},{1,481},{2,482},{3,483},{4,484},{5,485},{6,486},{7,487},{8... | collective-permute-start | bytes 12296 | tf_op jit(solution)/shard_map/ppermute | solution.py:448
  5.2 14.5 %collective-permute-start = (f32[1,8,128]{2,1,0:T(8,128)S(1)}, f32[1,8,128]{2,1,0:T(8,128)S(1)}, u32[]{:S(2)}, u32[]{:S(2)}) collective-permute-start(f32[1,8,128]{2,1,0:T(8,128)S(1)} %bitcast.42), channel_id=1, source_target_pairs={{0,32},{1,33},{2,34},{3,35},{4,36},{5,37},{6,38},{7,39},{8,40},{9,... | collective-permute-start | bytes 12296 | tf_op jit(solution)/shard_map/ppermute | solution.py:448
  19.1 3.7 %copy-start.8 = (s32[32,64]{1,0:T(8,128)S(1)}, s32[32,64]{1,0:T(8,128)}, u32[]{:S(2)}) copy-start(s32[32,64]{1,0:T(8,128)} %param.15) | copy-start | bytes 24580
  19.7 3.1 %copy-start.10 = (bf16[7,128]{1,0:T(8,128)(2,1)S(1)}, bf16[7,128]{1,0:T(8,128)(2,1)}, u32[]{:S(2)}) copy-start(bf16[7,128]{1,0:T(8,128)(2,1)} %param.17) | copy-start | bytes 5380
  19.7 5.6 %collective-permute-start.2 = (f32[3,8,128]{2,1,0:T(8,128)S(1)}, f32[3,8,128]{2,1,0:T(8,128)S(1)}, u32[]{:S(2)}, u32[]{:S(2)}) collective-permute-start(f32[3,8,128]{2,1,0:T(8,128)S(1)} %pad_maximum_fusion), channel_id=1, source_target_pairs={{0,8},{1,9},{2,10},{3,11},{4,12},{5,13},{6,14},{7,15},{8,16},{9,17... | collective-permute-start | bytes 36872 | tf_op jit(solution)/shard_map/ppermute | solution.py:448
  23.0 4.4 %collective-permute-start.3 = (f32[3,8,128]{2,1,0:T(8,128)S(1)}, f32[3,8,128]{2,1,0:T(8,128)S(1)}, u32[]{:S(2)}, u32[]{:S(2)}) collective-permute-start(f32[3,8,128]{2,1,0:T(8,128)S(1)} %pad_maximum_fusion), channel_id=1, source_target_pairs={{0,24},{1,25},{2,26},{3,27},{4,28},{5,29},{6,30},{7,31},{8,0},{9,1... | collective-permute-start | bytes 36872 | tf_op jit(solution)/shard_map/ppermute | solution.py:448
  27.4 15.3 %collective-permute-start.5 = (f32[9,8,128]{2,1,0:T(8,128)S(1)}, f32[9,8,128]{2,1,0:T(8,128)S(1)}, u32[]{:S(2)}, u32[]{:S(2)}) collective-permute-start(f32[9,8,128]{2,1,0:T(8,128)S(1)} %constant_dynamic-update-slice_fusion.refs_3_), channel_id=1, source_target_pairs={{0,7},{1,0},{2,1},{3,2},{4,3},{5,4},{6,5},{7,6},{8,15},{9,8},{10,9... | collective-permute-start | bytes 110600 | tf_op jit(solution)/shard_map/ppermute | solution.py:448
  30.1 12.6 %collective-permute-start.4 = (f32[9,8,128]{2,1,0:T(8,128)S(1)}, f32[9,8,128]{2,1,0:T(8,128)S(1)}, u32[]{:S(2)}, u32[]{:S(2)}) collective-permute-start(f32[9,8,128]{2,1,0:T(8,128)S(1)} %constant_dynamic-update-slice_fusion.refs_3_), channel_id=1, source_target_pairs={{0,1},{1,2},{2,3},{3,4},{4,5},{5,6},{6,7},{7,0},{8,9},{9,10},{10,1... | collective-permute-start | bytes 110600 | tf_op jit(solution)/shard_map/ppermute | solution.py:448
  39.4 0.8 slice-start
  40.2 0.8 copy-start.1
  41.0 0.7 copy-start.9
  41.0 0.9 slice-start.1
  41.7 0.9 slice-start.2
  44.3 36.2 %copy-start.6 = (bf16[5,128,128]{2,1,0:T(8,128)(2,1)S(1)}, bf16[5,128,128]{2,1,0:T(8,128)(2,1)}, u32[]{:S(2)}) copy-start(bf16[5,128,128]{2,1,0:T(8,128)(2,1)} %param.22) | copy-start | bytes 491524
  44.3 19.1 %collective-permute-start.6 = (bf16[16,512]{1,0:T(8,128)(2,1)S(1)}, bf16[16,512]{1,0:T(8,128)(2,1)S(1)}, u32[]{:S(2)}, u32[]{:S(2)}) collective-permute-start(bf16[16,512]{1,0:T(8,128)(2,1)S(1)} %get-tuple-element.29), channel_id=1, source_target_pairs={{0,32},{1,33},{2,34},{3,35},{4,36},{5,37},{6,38},{7,39},{8,40},{9,... | collective-permute-start | bytes 49160 | tf_op jit(solution)/shard_map/ppermute | solution.py:448
  61.5 16.0 %collective-permute-start.7 = (bf16[16,512]{1,0:T(8,128)(2,1)S(1)}, bf16[16,512]{1,0:T(8,128)(2,1)S(1)}, u32[]{:S(2)}, u32[]{:S(2)}) collective-permute-start(bf16[16,512]{1,0:T(8,128)(2,1)S(1)} %get-tuple-element.29), channel_id=1, source_target_pairs={{0,480},{1,481},{2,482},{3,483},{4,484},{5,485},{6,486},{7,487},{8... | collective-permute-start | bytes 49160 | tf_op jit(solution)/shard_map/ppermute | solution.py:448
  77.5 7.1 %collective-permute-start.8 = (bf16[48,512]{1,0:T(8,128)(2,1)S(1)}, bf16[48,512]{1,0:T(8,128)(2,1)S(1)}, u32[]{:S(2)}, u32[]{:S(2)}) collective-permute-start(bf16[48,512]{1,0:T(8,128)(2,1)S(1)} %constant_dynamic-update-slice_fusion.5), channel_id=1, source_target_pairs={{0,8},{1,9},{2,10},{3,11},{4,12},{5,13},{6,14},{7,15},{8,16},{9,17... | collective-permute-start | bytes 147464 | tf_op jit(solution)/shard_map/ppermute | solution.py:448
  80.5 0.8 slice-start.3
  81.4 0.8 copy-start
  82.3 5.1 %collective-permute-start.9 = (bf16[48,512]{1,0:T(8,128)(2,1)S(1)}, bf16[48,512]{1,0:T(8,128)(2,1)S(1)}, u32[]{:S(2)}, u32[]{:S(2)}) collective-permute-start(bf16[48,512]{1,0:T(8,128)(2,1)S(1)} %constant_dynamic-update-slice_fusion.5), channel_id=1, source_target_pairs={{0,24},{1,25},{2,26},{3,27},{4,28},{5,29},{6,30},{7,31},{8,0},{9,1... | collective-permute-start | bytes 147464 | tf_op jit(solution)/shard_map/ppermute | solution.py:448
  87.5 12.6 %collective-permute-start.11 = (bf16[144,512]{1,0:T(8,128)(2,1)S(1)}, bf16[144,512]{1,0:T(8,128)(2,1)S(1)}, u32[]{:S(2)}, u32[]{:S(2)}) collective-permute-start(bf16[144,512]{1,0:T(8,128)(2,1)S(1)} %constant_dynamic-update-slice_fusion.8.mid), channel_id=1, source_target_pairs={{0,7},{1,0},{2,1},{3,2},{4,3},{5,4},{6,5},{7,6},{8,15},{9,8},{10,9... | collective-permute-start | bytes 442376 | tf_op jit(solution)/shard_map/ppermute | solution.py:448
  89.4 12.1 %collective-permute-start.10 = (bf16[144,512]{1,0:T(8,128)(2,1)S(1)}, bf16[144,512]{1,0:T(8,128)(2,1)S(1)}, u32[]{:S(2)}, u32[]{:S(2)}) collective-permute-start(bf16[144,512]{1,0:T(8,128)(2,1)S(1)} %constant_dynamic-update-slice_fusion.8.mid), channel_id=1, source_target_pairs={{0,1},{1,2},{2,3},{3,4},{4,5},{5,6},{6,7},{7,0},{8,9},{9,10},{10,1... | collective-permute-start | bytes 442376 | tf_op jit(solution)/shard_map/ppermute | solution.py:448
  108.8 12.6 %collective-permute-start.12 = (bf16[144,512]{1,0:T(8,128)(2,1)S(1)}, bf16[144,512]{1,0:T(8,128)(2,1)S(1)}, u32[]{:S(2)}, u32[]{:S(2)}) collective-permute-start(bf16[144,512]{1,0:T(8,128)(2,1)S(1)} %get-tuple-element.32), channel_id=1, source_target_pairs={{0,1},{1,2},{2,3},{3,4},{4,5},{5,6},{6,7},{7,0},{8,9},{9,10},{10,1... | collective-permute-start | bytes 442376 | tf_op jit(solution)/shard_map/ppermute | solution.py:448
  119.3 12.5 %collective-permute-start.13 = (bf16[144,512]{1,0:T(8,128)(2,1)S(1)}, bf16[144,512]{1,0:T(8,128)(2,1)S(1)}, u32[]{:S(2)}, u32[]{:S(2)}) collective-permute-start(bf16[144,512]{1,0:T(8,128)(2,1)S(1)} %get-tuple-element.33), channel_id=1, source_target_pairs={{0,7},{1,0},{2,1},{3,2},{4,3},{5,4},{6,5},{7,6},{8,15},{9,8},{10,9... | collective-permute-start | bytes 442376 | tf_op jit(solution)/shard_map/ppermute | solution.py:448
  131.9 17.5 %copy-start.5 = (bf16[6,128,128]{2,1,0:T(8,128)(2,1)S(1)}, bf16[6,128,128]{2,1,0:T(8,128)(2,1)}, u32[]{:S(2)}) copy-start(bf16[6,128,128]{2,1,0:T(8,128)(2,1)} %param.21) | copy-start | bytes 589828
  131.9 5.4 %collective-permute-start.14 = (bf16[48,512]{1,0:T(8,128)(2,1)S(1)}, bf16[48,512]{1,0:T(8,128)(2,1)S(1)}, u32[]{:S(2)}, u32[]{:S(2)}) collective-permute-start(bf16[48,512]{1,0:T(8,128)(2,1)S(1)} %get-tuple-element.44), channel_id=1, source_target_pairs={{0,8},{1,9},{2,10},{3,11},{4,12},{5,13},{6,14},{7,15},{8,16},{9,17... | collective-permute-start | bytes 147464 | tf_op jit(solution)/shard_map/ppermute | solution.py:448
  135.2 4.8 %collective-permute-start.15 = (bf16[48,512]{1,0:T(8,128)(2,1)S(1)}, bf16[48,512]{1,0:T(8,128)(2,1)S(1)}, u32[]{:S(2)}, u32[]{:S(2)}) collective-permute-start(bf16[48,512]{1,0:T(8,128)(2,1)S(1)} %get-tuple-element.45), channel_id=1, source_target_pairs={{0,24},{1,25},{2,26},{3,27},{4,28},{5,29},{6,30},{7,31},{8,0},{9,1... | collective-permute-start | bytes 147464 | tf_op jit(solution)/shard_map/ppermute | solution.py:448
  140.1 9.3 %collective-permute-start.16 = (bf16[16,512]{1,0:T(8,128)(2,1)S(1)}, bf16[16,512]{1,0:T(8,128)(2,1)S(1)}, u32[]{:S(2)}, u32[]{:S(2)}) collective-permute-start(bf16[16,512]{1,0:T(8,128)(2,1)S(1)} %get-tuple-element.46), channel_id=1, source_target_pairs={{0,32},{1,33},{2,34},{3,35},{4,36},{5,37},{6,38},{7,39},{8,40},{9,... | collective-permute-start | bytes 49160 | tf_op jit(solution)/shard_map/ppermute | solution.py:448
  147.2 15.9 %collective-permute-start.17 = (bf16[16,512]{1,0:T(8,128)(2,1)S(1)}, bf16[16,512]{1,0:T(8,128)(2,1)S(1)}, u32[]{:S(2)}, u32[]{:S(2)}) collective-permute-start(bf16[16,512]{1,0:T(8,128)(2,1)S(1)} %get-tuple-element.47), channel_id=1, source_target_pairs={{0,480},{1,481},{2,482},{3,483},{4,484},{5,485},{6,486},{7,487},{8... | collective-permute-start | bytes 49160 | tf_op jit(solution)/shard_map/ppermute | solution.py:448
  165.8 5.3 %collective-permute-start.18 = (f32[9,8,128]{2,1,0:T(8,128)S(1)}, f32[9,8,128]{2,1,0:T(8,128)S(1)}, u32[]{:S(2)}, u32[]{:S(2)}) collective-permute-start(f32[9,8,128]{2,1,0:T(8,128)S(1)} %get-tuple-element.38), channel_id=1, source_target_pairs={{0,1},{1,2},{2,3},{3,4},{4,5},{5,6},{6,7},{7,0},{8,9},{9,10},{10,1... | collective-permute-start | bytes 110600 | tf_op jit(solution)/shard_map/ppermute | solution.py:448
  167.8 11.3 %collective-permute-start.19 = (f32[9,8,128]{2,1,0:T(8,128)S(1)}, f32[9,8,128]{2,1,0:T(8,128)S(1)}, u32[]{:S(2)}, u32[]{:S(2)}) collective-permute-start(f32[9,8,128]{2,1,0:T(8,128)S(1)} %get-tuple-element.39), channel_id=1, source_target_pairs={{0,7},{1,0},{2,1},{3,2},{4,3},{5,4},{6,5},{7,6},{8,15},{9,8},{10,9... | collective-permute-start | bytes 110600 | tf_op jit(solution)/shard_map/ppermute | solution.py:448
  179.1 5.3 %collective-permute-start.20 = (f32[3,8,128]{2,1,0:T(8,128)S(1)}, f32[3,8,128]{2,1,0:T(8,128)S(1)}, u32[]{:S(2)}, u32[]{:S(2)}) collective-permute-start(f32[3,8,128]{2,1,0:T(8,128)S(1)} %get-tuple-element.48), channel_id=1, source_target_pairs={{0,8},{1,9},{2,10},{3,11},{4,12},{5,13},{6,14},{7,15},{8,16},{9,17... | collective-permute-start | bytes 36872 | tf_op jit(solution)/shard_map/ppermute | solution.py:448
  182.5 4.7 %collective-permute-start.21 = (f32[3,8,128]{2,1,0:T(8,128)S(1)}, f32[3,8,128]{2,1,0:T(8,128)S(1)}, u32[]{:S(2)}, u32[]{:S(2)}) collective-permute-start(f32[3,8,128]{2,1,0:T(8,128)S(1)} %get-tuple-element.49), channel_id=1, source_target_pairs={{0,24},{1,25},{2,26},{3,27},{4,28},{5,29},{6,30},{7,31},{8,0},{9,1... | collective-permute-start | bytes 36872 | tf_op jit(solution)/shard_map/ppermute | solution.py:448
  187.2 6.1 %collective-permute-start.22 = (f32[1,8,128]{2,1,0:T(8,128)S(1)}, f32[1,8,128]{2,1,0:T(8,128)S(1)}, u32[]{:S(2)}, u32[]{:S(2)}) collective-permute-start(f32[1,8,128]{2,1,0:T(8,128)S(1)} %get-tuple-element.52), channel_id=1, source_target_pairs={{0,32},{1,33},{2,34},{3,35},{4,36},{5,37},{6,38},{7,39},{8,40},{9,... | collective-permute-start | bytes 12296 | tf_op jit(solution)/shard_map/ppermute | solution.py:448
  191.4 15.7 %collective-permute-start.23 = (f32[1,8,128]{2,1,0:T(8,128)S(1)}, f32[1,8,128]{2,1,0:T(8,128)S(1)}, u32[]{:S(2)}, u32[]{:S(2)}) collective-permute-start(f32[1,8,128]{2,1,0:T(8,128)S(1)} %get-tuple-element.53), channel_id=1, source_target_pairs={{0,480},{1,481},{2,482},{3,483},{4,484},{5,485},{6,486},{7,487},{8... | collective-permute-start | bytes 12296 | tf_op jit(solution)/shard_map/ppermute | solution.py:448

commit v2 on v1

--- a/solution.py
+++ b/solution.py
@@ -102,7 +102,7 @@
     distance = square * inverse
     unit = delta * inverse
     slot = iota((1, PAIRS), 1) % SLOTS
-    paired = jnp.where((index != slot) & (slot < count), 1.0, 0.0)
+    paired = jnp.where(index != slot, jnp.concatenate([live_row(count)] * COLUMNS, axis=1), 0.0)
     scaled = jnp.minimum(distance * (1.0 / CUTOFF), 1.0)
     power = scaled * scaled * scaled
     power = power * power
@@ -121,6 +121,23 @@
     return unit, inverse, kind, basis, basis_slope
 
 
+def split(values):
+    high = values.astype(BF16)
+    return high, (values - high.astype(F32)).astype(BF16)
+
+
+def keep(values):
+    return values.astype(BF16).astype(F32)
+
+
+def grad_distance_of(wout, win, grad_radial, before, gate, basis_slope):
+    half = grad_radial.shape[0] // 2
+    grad_hidden = keep(dot_nn(wout[...], grad_radial[0:half, :]) + dot_nn(wout[...], grad_radial[half:, :]))
+    high, low = split(grad_hidden * (gate * (1.0 + before * (1.0 - gate))))
+    grad_basis = keep(dot_nn(win[...], high) + dot_nn(win[...], low))
+    return jnp.sum(grad_basis * basis_slope, axis=0, keepdims=True)
+
+
 def hidden_of(weights, basis):
     before = dot_nn(weights, basis)
     gate = 1.0 / (1.0 + jnp.exp(-before))
@@ -140,27 +157,25 @@
     return out
 
 
-def start_kernel(exports, positions, species, own, payload, picked):
+def start_kernel(arrived, own, payload, picked, index, count):
     own[...] = jnp.zeros_like(own)
-    own[0:3, 0:SLOTS] = positions[...]
-    own[3:4, 0:SLOTS] = species[...].astype(F32)
-    lane = iota((8, LANES), 1) % EXPORT
-    row = iota((EXPORT, LANES), 0)
-    source = jnp.zeros((8, LANES), jnp.int32)
-    pick = jnp.zeros((EXPORT, LANES), jnp.int32)
-    for e in range(EXPORT):
-        slot = exports[e]
-        source = jnp.where(lane == e, slot, source)
-        pick = jnp.where(row == e, slot, pick)
-    picked[...] = pick
+    own[0:4, 0:SLOTS] = arrived[COLUMNS : COLUMNS + 4, 0:SLOTS]
+    exports = arrived[COLUMNS + 4 : COLUMNS + 5, :]
+    count[...] = arrived[COLUMNS + 5 : COLUMNS + 6, :].astype(jnp.int32)
+    mine = iota((EXPORT, LANES), 1) == iota((EXPORT, LANES), 0)
+    pick = jnp.sum(jnp.where(mine, exports, 0.0), axis=1, keepdims=True)
+    picked[...] = jnp.broadcast_to(pick, (EXPORT, LANES)).astype(jnp.int32)
+    source = jnp.broadcast_to(exports, (8, LANES)).astype(jnp.int32)
     payload[...] = jnp.take_along_axis(own[...], source, axis=1)
+    for m in range(COLUMNS):
+        index[:, m * LANES : (m + 1) * LANES] = arrived[m : m + 1, :].astype(jnp.int32)
 
 
 def first_kernel(
     count_ref, own, low, mid, high, index, picked, win_t, wout_t, mix_a, mix_b, mix0_t, emb, emb_t, read_t,
     table, own_rows, outgoing, sums, energy, spread, radial,
 ):
-    count = count_ref[0]
+    count = count_ref[...]
     group = iota((8, LANES), 1) // EXPORT
     rows8 = iota((8, 1), 0)
     tiles = [own[...]] + [jnp.zeros((8, LANES), F32) for _ in range(3)]
@@ -224,9 +239,9 @@
 def second_kernel(
     count_ref, table, own_rows, low, mid, high, index, win_t, win, wout_t, wout, mix_t, mix_rest, read,
     grad_own, grad_low, grad_mid, grad_high, pair_out, energy,
-    feats, projected, onehot, radial, source, grad_radial, grad_source,
+    feats, turned, onehot, radial, source, grad_radial, grad_source,
 ):
-    count = count_ref[0]
+    count = count_ref[...]
     ids = index[...]
     unit, inverse, _, basis, basis_slope = geometry(table[...], ids, count, True)
     before, gate = hidden_of(win_t[...], basis)
@@ -236,10 +251,9 @@
     feats[SLOTS + SLAB : SLOTS + 2 * SLAB, :] = mid[...]
     feats[SLOTS + 2 * SLAB : SLOTS + 3 * SLAB, :] = high[...]
     feats[SLOTS + 3 * SLAB :, :] = jnp.zeros((TABLE - SLOTS - 3 * SLAB, 4 * C), BF16)
+    eye = (iota((C, C), 0) == iota((C, C), 1)).astype(F32).astype(BF16)
     for c in range(4):
-        projected[c * C : (c + 1) * C, :] = dot_nt(
-            mix_t[min(c, 1)], feats[:, c * C : (c + 1) * C]
-        ).astype(BF16)
+        turned[c * C : (c + 1) * C, :] = dot_nt(eye, feats[:, c * C : (c + 1) * C]).astype(BF16)
     entry = iota((TABLE, LANES), 0)
     for m in range(COLUMNS):
         onehot[:, m * LANES : (m + 1) * LANES] = (entry == column(ids, m)).astype(F32).astype(BF16)
@@ -250,7 +264,9 @@
     for w in range(PAIRS // wide):
         at = slice(w * wide, (w + 1) * wide)
         radial[:, at] = dot_nn(wout_t[...], hidden[:, at])
-        source[:, at] = dot_nn(projected[...], onehot[:, at])
+        picked = dot_nn(turned[...], onehot[:, at]).astype(BF16)
+        for c in range(4):
+            source[c * C : (c + 1) * C, at] = dot_nn(mix_t[min(c, 1)], picked[c * C : (c + 1) * C])
         for m in (2 * w, 2 * w + 1):
             here = slice(m * LANES, (m + 1) * LANES)
             s = source[0:C, here]
@@ -283,10 +299,11 @@
         r1, r2, r3, r4 = [radial[k * C : (k + 1) * C, here] for k in range(4)]
         along = v[0] * u[0] + v[1] * u[1] + v[2] * u[2]
         slant = d1[0] * u[0] + d1[1] * u[1] + d1[2] * u[2]
-        grad_radial[0:C, here] = (d0 * s).astype(BF16)
-        grad_radial[C : 2 * C, here] = (s * slant).astype(BF16)
-        grad_radial[2 * C : 3 * C, here] = (d1[0] * v[0] + d1[1] * v[1] + d1[2] * v[2]).astype(BF16)
-        grad_radial[3 * C :, here] = (d0 * along).astype(BF16)
+        parts = (d0 * s, s * slant, d1[0] * v[0] + d1[1] * v[1] + d1[2] * v[2], d0 * along)
+        for k in range(4):
+            high_part, low_part = split(parts[k])
+            grad_radial[k * C : (k + 1) * C, here] = high_part
+            grad_radial[(k + 4) * C : (k + 5) * C, here] = low_part
         grad_source[0:C, here] = (r1 * d0 + r2 * slant).astype(BF16)
         q = d0 * r4
         t = r2 * s
@@ -294,17 +311,15 @@
             grad_source[(x + 1) * C : (x + 2) * C, here] = (q * u[x] + r3 * d1[x]).astype(BF16)
             grad_units[x].append(jnp.sum(q * v[x] + t * d1[x], axis=0, keepdims=True))
     grad_unit = stack_rows([jnp.concatenate(g, axis=1) for g in grad_units])
-    grad_hidden = dot_nn(wout[...], grad_radial[...])
-    grad_before = (grad_hidden * (gate * (1.0 + before * (1.0 - gate)))).astype(BF16)
-    grad_basis = dot_nn(win[...], grad_before)
-    grad_distance = jnp.sum(grad_basis * basis_slope, axis=0, keepdims=True)
+    grad_distance = grad_distance_of(wout, win, grad_radial, before, gate, basis_slope)
     pair_out[...] = pair_gradient(unit, inverse, grad_unit, grad_distance)
     grad_projected = dot_nt(onehot[...], grad_source[...])
     outs = (grad_low, grad_mid, grad_high)
-    live_rows = (iota((SLOTS, 1), 0) < count).astype(F32)
+    live_rows = (iota((SLOTS, 1), 0) < count[:, 0:1]).astype(F32)
     for c in range(4):
         at = slice(c * C, (c + 1) * C)
-        rows = dot_nn(grad_projected[:, at].astype(BF16), mix_t[min(c, 1)])
+        high_part, low_part = split(grad_projected[:, at])
+        rows = dot_nn(high_part, mix_t[min(c, 1)]) + dot_nn(low_part, mix_t[min(c, 1)])
         mine = rows[0:SLOTS]
         if c == 0:
             mine = mine + live_rows * read[1:2, :]
@@ -319,7 +334,7 @@
     grad_mine, grad_low, grad_mid, grad_high,
     onehot, grad_radial,
 ):
-    count = count_ref[0]
+    count = count_ref[...]
     ids = index[...]
     unit, inverse, kind, basis, basis_slope = geometry(table[...], ids, count, True)
     before, gate = hidden_of(win_t[...], basis)
@@ -361,16 +376,16 @@
         source = dot_nn(spread[...], column(species, m))
         u = [column(unit[x : x + 1], m) for x in range(3)]
         slant = d1[0] * u[0] + d1[1] * u[1] + d1[2] * u[2]
-        grad_radial[0:C, here] = (d0 * source).astype(BF16)
-        grad_radial[C:, here] = (slant * source).astype(BF16)
+        parts = (d0 * source, slant * source)
+        for k in range(2):
+            high_part, low_part = split(parts[k])
+            grad_radial[k * C : (k + 1) * C, here] = high_part
+            grad_radial[(k + 2) * C : (k + 3) * C, here] = low_part
         q = r2 * source
         for x in range(3):
             grad_units[x].append(jnp.sum(q * d1[x], axis=0, keepdims=True))
     grad_unit = stack_rows([jnp.concatenate(g, axis=1) for g in grad_units])
-    grad_hidden = dot_nn(wout[...], grad_radial[...])
-    grad_before = (grad_hidden * (gate * (1.0 + before * (1.0 - gate)))).astype(BF16)
-    grad_basis = dot_nn(win[...], grad_before)
-    grad_distance = jnp.sum(grad_basis * basis_slope, axis=0, keepdims=True)
+    grad_distance = grad_distance_of(wout, win, grad_radial, before, gate, basis_slope)
     pairs = pair_in[...] + pair_gradient(unit, inverse, grad_unit, grad_distance)
     pair_high = pairs.astype(BF16)
     pair_low = (pairs - pair_high.astype(F32)).astype(BF16)
@@ -396,48 +411,45 @@
     return jnp.concatenate([fold(column(values, x)) for x in range(count)], axis=1)
 
 
-def last_kernel(exports, count_ref, grad_mine, back, energy_one, energy_two, forces, energies):
-    lane = iota((8, LANES), 1)
-    total = grad_mine[...]
-    came = back[...]
-    source = jnp.zeros((8, LANES), jnp.int32)
-    hit = jnp.zeros((8, LANES), F32)
-    for e in range(EXPORT):
-        same = lane == exports[e]
-        source = jnp.where(same, e, source)
-        hit = jnp.where(same, 1.0, hit)
-    total = total + jnp.where(hit > 0.5, jnp.take_along_axis(came, source, axis=1), 0.0)
-    forces[...] = -total[0:3, 0:SLOTS]
-    energies[...] = (live_row(count_ref[0]) * (energy_one[...] + energy_two[...]))[:, 0:SLOTS]
-
-
-def call(kernel, outs, specs, scratch=(), limit=None, smem=0):
-    count = len(specs)
-    in_specs = [pl.BlockSpec(memory_space=pltpu.SMEM)] * smem
-    in_specs += [pl.BlockSpec(memory_space=pltpu.VMEM)] * (count - smem)
-    many = isinstance(outs, (list, tuple))
+def last_kernel(count_ref, grad_mine, back, picked, energy_one, energy_two, out):
+    same = iota((EXPORT, LANES), 1) == picked[...]
+    entry = jnp.sum(jnp.where(same, iota((EXPORT, LANES), 0), 0), axis=0, keepdims=True)
+    hit = jnp.sum(same.astype(F32), axis=0, keepdims=True)
+    came = jnp.take_along_axis(back[...], jnp.broadcast_to(entry, (8, LANES)), axis=1)
+    forces = -(grad_mine[...] + came * hit)
+    energies = live_row(count_ref[...]) * (energy_one[...] + energy_two[...])
+    out[...] = jnp.where(iota((8, LANES), 0) == 3, energies, forces)
+
+
+def call(kernel, outs, specs, scratch=(), limit=None):
     return pl.pallas_call(
         kernel,
         out_shape=[jax.ShapeDtypeStruct(s, t) for s, t in outs],
-        in_specs=in_specs,
+        in_specs=[pl.BlockSpec(memory_space=pltpu.VMEM)] * len(specs),
         out_specs=[pl.BlockSpec(memory_space=pltpu.VMEM)] * len(outs),
         scratch_shapes=[pltpu.VMEM(s, t) for s, t in scratch],
         compiler_params=pltpu.CompilerParams(vmem_limit_bytes=limit or (16 << 20)),
     )(*specs)
 
 
-def domain(x, y, z):
-    return (x % 16 * 4 + y % 4) * 8 + z % 8
+DOMAINS = [(x, y, z) for x in range(16) for y in range(4) for z in range(8)]
+
+
+def given(x, y, z):
+    return (x * 4 + y) * 8 + z
+
+
+def seat(x, y, z):
+    x, y, z = x % 16, y % 4, z % 8
+    return given(z // 2 * 4 + x // 8 * 2 + z % 2, y, x % 8)
+
+
+MOVE_IN = [(given(*d), seat(*d)) for d in DOMAINS]
+MOVE_OUT = [(there, here) for here, there in MOVE_IN]
 
 
 def moves(step):
-    sx, sy, sz = step
-    return [
-        (domain(x, y, z), domain(x + sx, y + sy, z + sz))
-        for x in range(16)
-        for y in range(4)
-        for z in range(8)
-    ]
+    return [(seat(*d), seat(*(a + b for a, b in zip(d, step)))) for d in DOMAINS]
 
 
 UP = ((1, 0, 0), (0, 1, 0), (0, 0, 1))
@@ -471,16 +483,33 @@
     positions, species, counts, neighbours, exports, embedding, radial_in,
     radial_out_one, radial_out_two, mix_one, mix_two, readout,
 ):
-    own, payload, picked = call(
-        start_kernel,
-        [((8, LANES), F32), ((8, LANES), F32), ((EXPORT, LANES), jnp.int32)],
-        [exports, positions, species.reshape(1, SLOTS)],
-        smem=1,
-    )
     block = (neighbours - SLOTS) // EXPORT
     turned = block % 3 * 9 + block // 3 % 3 * 3 + block // 9
     moved = SLOTS + turned * EXPORT + neighbours % EXPORT
-    index = jnp.where(neighbours < SLOTS, neighbours, moved).reshape(1, PAIRS)
+    moved = jnp.where(neighbours < SLOTS, neighbours, moved).astype(F32)
+    slots = jnp.concatenate([positions, species.astype(F32)[None]], axis=0)
+    packed = jnp.concatenate(
+        [
+            moved.reshape(COLUMNS, LANES),
+            jnp.pad(slots, ((0, 0), (0, LANES - SLOTS))),
+            jnp.tile(exports.astype(F32), LANES // EXPORT)[None],
+            jnp.broadcast_to(counts.astype(F32)[None], (1, LANES)),
+            jnp.zeros((2, LANES), F32),
+        ],
+        axis=0,
+    )
+    arrived = lax.ppermute(packed, AXES, MOVE_IN)
+    own, payload, picked, index, count = call(
+        start_kernel,
+        [
+            ((8, LANES), F32),
+            ((8, LANES), F32),
+            ((EXPORT, LANES), jnp.int32),
+            ((1, PAIRS), jnp.int32),
+            ((1, LANES), jnp.int32),
+        ],
+        [arrived],
+    )
     emb = jnp.concatenate([embedding, jnp.zeros((1, C), BF16)], axis=0)
     emb_t = emb.T
     win_t = jnp.swapaxes(radial_in, 1, 2)
@@ -506,8 +535,7 @@
             ((1, LANES), F32),
             ((C, 16), BF16),
         ],
-        [counts, own, low, mid, high, index, picked, win_t[0], one_t, mix_a, mix_b, mix0_t, emb, emb_t, read_t],
-        smem=1,
+        [count, own, low, mid, high, index, picked, win_t[0], one_t, mix_a, mix_b, mix0_t, emb, emb_t, read_t],
     )
     low, mid, high = spread_halo(outgoing)
     grad_own, grad_low, grad_mid, grad_high, pairs, energy_two = call(
@@ -521,7 +549,7 @@
             ((1, LANES), F32),
         ],
         [
-            counts, table, own_rows, low, mid, high, index, win_t[1], radial_in[1], two_t, radial_out_two,
+            count, table, own_rows, low, mid, high, index, win_t[1], radial_in[1], two_t, radial_out_two,
             mix_two_t, mix_two_rest, read,
         ],
         scratch=[
@@ -530,32 +558,30 @@
             ((TABLE, PAIRS), BF16),
             ((4 * C, PAIRS), F32),
             ((4 * C, PAIRS), F32),
+            ((8 * C, PAIRS), BF16),
             ((4 * C, PAIRS), BF16),
-            ((4 * C, PAIRS), BF16),
         ],
         limit=48 << 20,
-        smem=1,
     )
     back = gather_halo(grad_low, grad_mid, grad_high)
     grad_mine, grad_low, grad_mid, grad_high = call(
         third_kernel,
         [((8, LANES), F32), ((9, 8, LANES), F32), ((9, 8, LANES), F32), ((9, 8, LANES), F32)],
         [
-            counts, table, sums, grad_own, back, picked, pairs, index, win_t[0], radial_in[0], one_t,
+            count, table, sums, grad_own, back, picked, pairs, index, win_t[0], radial_in[0], one_t,
             radial_out_one, mix_back, spread, read_t,
         ],
-        scratch=[((TABLE, PAIRS), BF16), ((2 * C, PAIRS), BF16)],
+        scratch=[((TABLE, PAIRS), BF16), ((4 * C, PAIRS), BF16)],
         limit=32 << 20,
-        smem=1,
     )
     back = gather_halo(grad_low, grad_mid, grad_high)
-    forces, energies = call(
+    (out,) = call(
         last_kernel,
-        [((3, SLOTS), F32), ((1, SLOTS), F32)],
-        [exports, counts, grad_mine, back[0], energy_one, energy_two],
-        smem=2,
-    )
-    return forces, energies.reshape(SLOTS)
+        [((8, LANES), F32)],
+        [count, grad_mine, back[0], picked, energy_one, energy_two],
+    )
+    out = lax.ppermute(out, AXES, MOVE_OUT)
+    return out[0:3, 0:SLOTS], out[3, 0:SLOTS]
 
 
 def solution(mesh):

time: 209 us -> 149 us (0.71)
  the two profiles are of different devices: /device:TPU:503 before, /device:TPU:15 now
where the time goes in v2:
time: 149 us; the launch traced here: 148 us
  starting transfers between devices  92.5 us (62%)
  waiting for transfers between devices  30 us (20%)
  Pallas kernels  14.3 us (10%)
  local copies, waits for them, and re-layouts  7.98 us (5%)
  between operations  1.82 us (1%)
    ppermute x24, starting transfers between devices, send(): return lax.ppermute(value, AXES, moves(step))  68.3 us
    ppermute x24, waiting for transfers between devices, send(): return lax.ppermute(value, AXES, moves(step))  27.1 us
    pallas_call x5, Pallas kernels, call(): pl.pallas_call(kernel, out_shape=[jax.ShapeDtypeStruct(s, t) for s, t in...  14.3 us
    ppermute x1, starting transfers between devices, body(): arrived = lax.ppermute(packed, AXES, MOVE_IN)  12.5 us
    ppermute x1, starting transfers between devices, body(): out = lax.ppermute(out, AXES, MOVE_OUT)  11.7 us
    unnamed x36, local copies, waits for them, and re-layouts  4.12 us
  transfers between devices with their start and end apart: 26, of which 15 were waited for; matrix products, arithmetic and copies ran while one was open for 1% of the time, Pallas kernels for 0%

profile of v2, /device:TPU:15, one launch (start us, length us, event | category | flops | bytes accessed | tf_op | source)
XLA Modules:
  0.0 148.1 jit_solution(17160913231796341010)
XLA Ops:
  1.3 0.7 convert_bitcast_fusion
  2.0 0.7 convert_element_type.16
  3.5 12.5 %collective-permute-start = (f32[24,128]{1,0:T(8,128)S(1)}, f32[24,128]{1,0:T(8,128)S(1)}, u32[]{:S(2)}, u32[]{:S(2)}) collective-permute-start(f32[24,128]{1,0:T(8,128)S(1)} %concatenate.27), channel_id=1, source_target_pairs={{0,0},{1,32},{2,128},{3,160},{4,256},{5,288},{6,384},{7,416},{8,8}... | collective-permute-start | bytes 36872 | tf_op jit(solution)/shard_map/ppermute | solution.py:501
  16.0 2.2 %collective-permute-done.arrived = f32[24,128]{1,0:T(8,128)S(1)} collective-permute-done((f32[24,128]{1,0:T(8,128)S(1)}, f32[24,128]{1,0:T(8,128)S(1)}, u32[]{:S(2)}, u32[]{:S(2)}) %collective-permute-start) | collective-permute-done | bytes 12320 | tf_op jit(solution)/shard_map/ppermute | solution.py:501
  18.3 1.9 %collective-permute-start.2 = (f32[1,8,128]{2,1,0:T(8,128)S(1)}, f32[1,8,128]{2,1,0:T(8,128)S(1)}, u32[]{:S(2)}, u32[]{:S(2)}) collective-permute-start(f32[1,8,128]{2,1,0:T(8,128)S(1)} %bitcast.44), channel_id=1, source_target_pairs={{0,71},{32,103},{128,199},{160,231},{256,327},{288,359},{384,455},... | collective-permute-start | bytes 12296 | tf_op jit(solution)/shard_map/ppermute | solution.py:460
  20.2 3.4 %collective-permute-start.1 = (f32[1,8,128]{2,1,0:T(8,128)S(1)}, f32[1,8,128]{2,1,0:T(8,128)S(1)}, u32[]{:S(2)}, u32[]{:S(2)}) collective-permute-start(f32[1,8,128]{2,1,0:T(8,128)S(1)} %bitcast.45), channel_id=1, source_target_pairs={{0,1},{32,33},{128,129},{160,161},{256,257},{288,289},{384,385},{4... | collective-permute-start | bytes 12296 | tf_op jit(solution)/shard_map/ppermute | solution.py:460
  23.7 2.1 %collective-permute-done.1 = f32[1,8,128]{2,1,0:T(8,128)S(1)} collective-permute-done((f32[1,8,128]{2,1,0:T(8,128)S(1)}, f32[1,8,128]{2,1,0:T(8,128)S(1)}, u32[]{:S(2)}, u32[]{:S(2)}) %collective-permute-start.1) | collective-permute-done | bytes 4128 | tf_op jit(solution)/shard_map/ppermute | solution.py:460
  25.8 3.2 %collective-permute-start.3 = (f32[3,8,128]{2,1,0:T(8,128)S(1)}, f32[3,8,128]{2,1,0:T(8,128)S(1)}, u32[]{:S(2)}, u32[]{:S(2)}) collective-permute-start(f32[3,8,128]{2,1,0:T(8,128)S(1)} %pad_maximum_fusion), channel_id=1, source_target_pairs={{0,8},{32,40},{128,136},{160,168},{256,264},{288,296},{384,392},{4... | collective-permute-start | bytes 36872 | tf_op jit(solution)/shard_map/ppermute | solution.py:460
  29.0 0.7 copy-done.7
  29.8 2.1 %collective-permute-start.4 = (f32[3,8,128]{2,1,0:T(8,128)S(1)}, f32[3,8,128]{2,1,0:T(8,128)S(1)}, u32[]{:S(2)}, u32[]{:S(2)}) collective-permute-start(f32[3,8,128]{2,1,0:T(8,128)S(1)} %pad_maximum_fusion), channel_id=1, source_target_pairs={{0,24},{32,56},{128,152},{160,184},{256,280},{288,312},{384,408},{... | collective-permute-start | bytes 36872 | tf_op jit(solution)/shard_map/ppermute | solution.py:460
  32.0 2.3 %collective-permute-done.4 = f32[3,8,128]{2,1,0:T(8,128)S(1)} collective-permute-done((f32[3,8,128]{2,1,0:T(8,128)S(1)}, f32[3,8,128]{2,1,0:T(8,128)S(1)}, u32[]{:S(2)}, u32[]{:S(2)}) %collective-permute-start.4) | collective-permute-done | bytes 12320 | tf_op jit(solution)/shard_map/ppermute | solution.py:460
  34.3 3.0 %collective-permute-start.6 = (f32[9,8,128]{2,1,0:T(8,128)S(1)}, f32[9,8,128]{2,1,0:T(8,128)S(1)}, u32[]{:S(2)}, u32[]{:S(2)}) collective-permute-start(f32[9,8,128]{2,1,0:T(8,128)S(1)} %constant_dynamic-update-slice_fusion.refs_3_), channel_id=1, source_target_pairs={{0,416},{32,0},{128,32},{160,128},{256,160},{288,256},{384,288},{4... | collective-permute-start | bytes 110600 | tf_op jit(solution)/shard_map/ppermute | solution.py:460
  37.3 8.8 %collective-permute-start.5 = (f32[9,8,128]{2,1,0:T(8,128)S(1)}, f32[9,8,128]{2,1,0:T(8,128)S(1)}, u32[]{:S(2)}, u32[]{:S(2)}) collective-permute-start(f32[9,8,128]{2,1,0:T(8,128)S(1)} %constant_dynamic-update-slice_fusion.refs_3_), channel_id=1, source_target_pairs={{0,32},{32,128},{128,160},{160,256},{256,288},{288,384},{384,416},... | collective-permute-start | bytes 110600 | tf_op jit(solution)/shard_map/ppermute | solution.py:460
  46.2 0.8 slice-done
  47.1 0.6 copy-done.1
  49.5 1.6 %shard_map.132 = (f32[8,512]{1,0:T(8,128)S(1)}, bf16[64,512]{1,0:T(8,128)(2,1)S(1)}, bf16[16,512]{1,0:T(8,128)(2,1)S(1)}, f32[512,128]{1,0:T(8,128)S(1)}, f32[1,...) custom-call(s32[1,128]{1,0:T(1,128)S(1)} %get-tuple-element.23.refs_0_.count_ref, f32[8,128]{1,0:T(8,128)S(1)} %get-tuple-element.24.refs_1_, ...), custom_call_target="tpu_custom_call" | custom-call | tf_op jit(solution)/shard_map/pallas_call | solution.py:425
  51.1 2.1 %collective-permute-start.7 = (bf16[16,512]{1,0:T(8,128)(2,1)S(1)}, bf16[16,512]{1,0:T(8,128)(2,1)S(1)}, u32[]{:S(2)}, u32[]{:S(2)}) collective-permute-start(bf16[16,512]{1,0:T(8,128)(2,1)S(1)} %get-tuple-element.31), channel_id=1, source_target_pairs={{0,1},{32,33},{128,129},{160,161},{256,257},{288,289},{384,385},{4... | collective-permute-start | bytes 49160 | tf_op jit(solution)/shard_map/ppermute | solution.py:460
  53.1 4.6 %collective-permute-start.8 = (bf16[16,512]{1,0:T(8,128)(2,1)S(1)}, bf16[16,512]{1,0:T(8,128)(2,1)S(1)}, u32[]{:S(2)}, u32[]{:S(2)}) collective-permute-start(bf16[16,512]{1,0:T(8,128)(2,1)S(1)} %get-tuple-element.31), channel_id=1, source_target_pairs={{0,71},{32,103},{128,199},{160,231},{256,327},{288,359},{384,455},... | collective-permute-start | bytes 49160 | tf_op jit(solution)/shard_map/ppermute | solution.py:460
  57.8 0.8 collective-permute-done.8
  58.6 2.9 %collective-permute-start.9 = (bf16[48,512]{1,0:T(8,128)(2,1)S(1)}, bf16[48,512]{1,0:T(8,128)(2,1)S(1)}, u32[]{:S(2)}, u32[]{:S(2)}) collective-permute-start(bf16[48,512]{1,0:T(8,128)(2,1)S(1)} %constant_dynamic-update-slice_fusion.5), channel_id=1, source_target_pairs={{0,8},{32,40},{128,136},{160,168},{256,264},{288,296},{384,392},{4... | collective-permute-start | bytes 147464 | tf_op jit(solution)/shard_map/ppermute | solution.py:460
  61.5 0.8 slice-done.3
  62.5 0.7 copy-done
  63.3 2.4 %collective-permute-start.10 = (bf16[48,512]{1,0:T(8,128)(2,1)S(1)}, bf16[48,512]{1,0:T(8,128)(2,1)S(1)}, u32[]{:S(2)}, u32[]{:S(2)}) collective-permute-start(bf16[48,512]{1,0:T(8,128)(2,1)S(1)} %constant_dynamic-update-slice_fusion.5), channel_id=1, source_target_pairs={{0,24},{32,56},{128,152},{160,184},{256,280},{288,312},{384,408},{... | collective-permute-start | bytes 147464 | tf_op jit(solution)/shard_map/ppermute | solution.py:460
  65.7 2.4 %collective-permute-done.10 = bf16[48,512]{1,0:T(8,128)(2,1)S(1)} collective-permute-done((bf16[48,512]{1,0:T(8,128)(2,1)S(1)}, bf16[48,512]{1,0:T(8,128)(2,1)S(1)}, u32[]{:S(2)}, u32[]{:S(2)}) %collective-permute-start.10) | collective-permute-done | bytes 49184 | tf_op jit(solution)/shard_map/ppermute | solution.py:460
  68.2 3.8 %collective-permute-start.11 = (bf16[144,512]{1,0:T(8,128)(2,1)S(1)}, bf16[144,512]{1,0:T(8,128)(2,1)S(1)}, u32[]{:S(2)}, u32[]{:S(2)}) collective-permute-start(bf16[144,512]{1,0:T(8,128)(2,1)S(1)} %constant_dynamic-update-slice_fusion.8.mid), channel_id=1, source_target_pairs={{0,32},{32,128},{128,160},{160,256},{256,288},{288,384},{384,416},... | collective-permute-start | bytes 442376 | tf_op jit(solution)/shard_map/ppermute | solution.py:460
  72.0 2.8 %collective-permute-done.12.high = bf16[144,512]{1,0:T(8,128)(2,1)S(1)} collective-permute-done((bf16[144,512]{1,0:T(8,128)(2,1)S(1)}, bf16[144,512]{1,0:T(8,128)(2,1)S(1)}, u32[]{:S(2)}, u32[]{:S(2)}) %collective-permute-start.12) | collective-permute-done | bytes 147488 | tf_op jit(solution)/shard_map/ppermute | solution.py:460
  74.8 9.4 %shard_map.133 = (f32[64,512]{1,0:T(8,128)S(1)}, bf16[144,512]{1,0:T(8,128)(2,1)S(1)}, bf16[144,512]{1,0:T(8,128)(2,1)S(1)}, bf16[144,512]{1,0:T(8,128)(2,1)S(1)...) custom-call(s32[1,128]{1,0:T(1,128)S(1)} %get-tuple-element.23.refs_0_.count_ref, f32[8,512]{1,0:T(8,128)S(1)} %get-tuple-element.28.table, ...), custom_call_target="tpu_custom_call" | custom-call | tf_op jit(solution)/shard_map/pallas_call | solution.py:425
  84.1 3.0 %collective-permute-start.13 = (bf16[144,512]{1,0:T(8,128)(2,1)S(1)}, bf16[144,512]{1,0:T(8,128)(2,1)S(1)}, u32[]{:S(2)}, u32[]{:S(2)}) collective-permute-start(bf16[144,512]{1,0:T(8,128)(2,1)S(1)} %get-tuple-element.34), channel_id=1, source_target_pairs={{0,32},{32,128},{128,160},{160,256},{256,288},{288,384},{384,416},... | collective-permute-start | bytes 442376 | tf_op jit(solution)/shard_map/ppermute | solution.py:460
  87.1 2.1 %collective-permute-done.13 = bf16[144,512]{1,0:T(8,128)(2,1)S(1)} collective-permute-done((bf16[144,512]{1,0:T(8,128)(2,1)S(1)}, bf16[144,512]{1,0:T(8,128)(2,1)S(1)}, u32[]{:S(2)}, u32[]{:S(2)}) %collective-permute-start.13) | collective-permute-done | bytes 147488 | tf_op jit(solution)/shard_map/ppermute | solution.py:460
  89.2 3.7 %collective-permute-done.14 = bf16[144,512]{1,0:T(8,128)(2,1)S(1)} collective-permute-done((bf16[144,512]{1,0:T(8,128)(2,1)S(1)}, bf16[144,512]{1,0:T(8,128)(2,1)S(1)}, u32[]{:S(2)}, u32[]{:S(2)}) %collective-permute-start.14) | collective-permute-done | bytes 147488 | tf_op jit(solution)/shard_map/ppermute | solution.py:460
  93.0 3.2 %collective-permute-start.15 = (bf16[48,512]{1,0:T(8,128)(2,1)S(1)}, bf16[48,512]{1,0:T(8,128)(2,1)S(1)}, u32[]{:S(2)}, u32[]{:S(2)}) collective-permute-start(bf16[48,512]{1,0:T(8,128)(2,1)S(1)} %get-tuple-element.44), channel_id=1, source_target_pairs={{0,8},{32,40},{128,136},{160,168},{256,264},{288,296},{384,392},{4... | collective-permute-start | bytes 147464 | tf_op jit(solution)/shard_map/ppermute | solution.py:460
  96.2 2.2 %collective-permute-start.16 = (bf16[48,512]{1,0:T(8,128)(2,1)S(1)}, bf16[48,512]{1,0:T(8,128)(2,1)S(1)}, u32[]{:S(2)}, u32[]{:S(2)}) collective-permute-start(bf16[48,512]{1,0:T(8,128)(2,1)S(1)} %get-tuple-element.45), channel_id=1, source_target_pairs={{0,24},{32,56},{128,152},{160,184},{256,280},{288,312},{384,408},{... | collective-permute-start | bytes 147464 | tf_op jit(solution)/shard_map/ppermute | solution.py:460
  98.4 2.6 %collective-permute-done.16 = bf16[48,512]{1,0:T(8,128)(2,1)S(1)} collective-permute-done((bf16[48,512]{1,0:T(8,128)(2,1)S(1)}, bf16[48,512]{1,0:T(8,128)(2,1)S(1)}, u32[]{:S(2)}, u32[]{:S(2)}) %collective-permute-start.16) | collective-permute-done | bytes 49184 | tf_op jit(solution)/shard_map/ppermute | solution.py:460
  101.0 1.9 %collective-permute-start.17 = (bf16[16,512]{1,0:T(8,128)(2,1)S(1)}, bf16[16,512]{1,0:T(8,128)(2,1)S(1)}, u32[]{:S(2)}, u32[]{:S(2)}) collective-permute-start(bf16[16,512]{1,0:T(8,128)(2,1)S(1)} %get-tuple-element.46), channel_id=1, source_target_pairs={{0,1},{32,33},{128,129},{160,161},{256,257},{288,289},{384,385},{4... | collective-permute-start | bytes 49160 | tf_op jit(solution)/shard_map/ppermute | solution.py:460
  102.9 5.3 %collective-permute-start.18 = (bf16[16,512]{1,0:T(8,128)(2,1)S(1)}, bf16[16,512]{1,0:T(8,128)(2,1)S(1)}, u32[]{:S(2)}, u32[]{:S(2)}) collective-permute-start(bf16[16,512]{1,0:T(8,128)(2,1)S(1)} %get-tuple-element.47), channel_id=1, source_target_pairs={{0,71},{32,103},{128,199},{160,231},{256,327},{288,359},{384,455},... | collective-permute-start | bytes 49160 | tf_op jit(solution)/shard_map/ppermute | solution.py:460
  108.3 0.6 collective-permute-done.18
  108.9 3.2 %shard_map.134 = (f32[8,128]{1,0:T(8,128)S(1)}, f32[9,8,128]{2,1,0:T(8,128)S(1)}, f32[9,8,128]{2,1,0:T(8,128)S(1)}, f32[9,8,128]{2,1,0:T(8,128)S(1)}) custom-call(s32[1,128]{1,0:T(1,128)S(1)} %get-tuple-element.23.refs_0_.count_ref, f32[8,512]{1,0:T(8,128)S(1)} %get-tuple-element.28.table, f32[512,128]{1,0:T(8,128)S(1)} %get-tuple-element.29.sums, ...), custom_call_target="tpu_custom_call" | custom-call | tf_op jit(solution)/shard_map/pallas_call | solution.py:425
  112.1 2.3 %collective-permute-start.19 = (f32[9,8,128]{2,1,0:T(8,128)S(1)}, f32[9,8,128]{2,1,0:T(8,128)S(1)}, u32[]{:S(2)}, u32[]{:S(2)}) collective-permute-start(f32[9,8,128]{2,1,0:T(8,128)S(1)} %get-tuple-element.40), channel_id=1, source_target_pairs={{0,32},{32,128},{128,160},{160,256},{256,288},{288,384},{384,416},... | collective-permute-start | bytes 110600 | tf_op jit(solution)/shard_map/ppermute | solution.py:460
  114.4 1.1 collective-permute-done.19
  115.5 3.5 %collective-permute-done.20 = f32[9,8,128]{2,1,0:T(8,128)S(1)} collective-permute-done((f32[9,8,128]{2,1,0:T(8,128)S(1)}, f32[9,8,128]{2,1,0:T(8,128)S(1)}, u32[]{:S(2)}, u32[]{:S(2)}) %collective-permute-start.20) | collective-permute-done | bytes 36896 | tf_op jit(solution)/shard_map/ppermute | solution.py:460
  119.0 3.2 %collective-permute-start.21 = (f32[3,8,128]{2,1,0:T(8,128)S(1)}, f32[3,8,128]{2,1,0:T(8,128)S(1)}, u32[]{:S(2)}, u32[]{:S(2)}) collective-permute-start(f32[3,8,128]{2,1,0:T(8,128)S(1)} %get-tuple-element.48), channel_id=1, source_target_pairs={{0,8},{32,40},{128,136},{160,168},{256,264},{288,296},{384,392},{4... | collective-permute-start | bytes 36872 | tf_op jit(solution)/shard_map/ppermute | solution.py:460
  122.2 2.1 %collective-permute-start.22 = (f32[3,8,128]{2,1,0:T(8,128)S(1)}, f32[3,8,128]{2,1,0:T(8,128)S(1)}, u32[]{:S(2)}, u32[]{:S(2)}) collective-permute-start(f32[3,8,128]{2,1,0:T(8,128)S(1)} %get-tuple-element.49), channel_id=1, source_target_pairs={{0,24},{32,56},{128,152},{160,184},{256,280},{288,312},{384,408},{... | collective-permute-start | bytes 36872 | tf_op jit(solution)/shard_map/ppermute | solution.py:460
  124.3 2.4 %collective-permute-done.22 = f32[3,8,128]{2,1,0:T(8,128)S(1)} collective-permute-done((f32[3,8,128]{2,1,0:T(8,128)S(1)}, f32[3,8,128]{2,1,0:T(8,128)S(1)}, u32[]{:S(2)}, u32[]{:S(2)}) %collective-permute-start.22) | collective-permute-done | bytes 12320 | tf_op jit(solution)/shard_map/ppermute | solution.py:460
  126.7 1.9 %collective-permute-start.23 = (f32[1,8,128]{2,1,0:T(8,128)S(1)}, f32[1,8,128]{2,1,0:T(8,128)S(1)}, u32[]{:S(2)}, u32[]{:S(2)}) collective-permute-start(f32[1,8,128]{2,1,0:T(8,128)S(1)} %get-tuple-element.52), channel_id=1, source_target_pairs={{0,1},{32,33},{128,129},{160,161},{256,257},{288,289},{384,385},{4... | collective-permute-start | bytes 12296 | tf_op jit(solution)/shard_map/ppermute | solution.py:460
  128.6 5.1 %collective-permute-start.24 = (f32[1,8,128]{2,1,0:T(8,128)S(1)}, f32[1,8,128]{2,1,0:T(8,128)S(1)}, u32[]{:S(2)}, u32[]{:S(2)}) collective-permute-start(f32[1,8,128]{2,1,0:T(8,128)S(1)} %get-tuple-element.53), channel_id=1, source_target_pairs={{0,71},{32,103},{128,199},{160,231},{256,327},{288,359},{384,455},... | collective-permute-start | bytes 12296 | tf_op jit(solution)/shard_map/ppermute | solution.py:460
  133.8 0.7 collective-permute-done.24
  134.6 11.7 %collective-permute-start.25 = (f32[8,128]{1,0:T(8,128)S(1)}, f32[8,128]{1,0:T(8,128)S(1)}, u32[]{:S(2)}, u32[]{:S(2)}) collective-permute-start(f32[8,128]{1,0:T(8,128)S(1)} %shard_map.135), channel_id=1, source_target_pairs={{0,0},{32,1},{128,2},{160,3},{256,4},{288,5},{384,6},{416,7},{8,8}... | collective-permute-start | bytes 12296 | tf_op jit(solution)/shard_map/ppermute | solution.py:583
  146.3 0.7 collective-permute-done.25
  (88 shorter events, 4.7 us)
Async XLA Ops:
  0.6 2.1 %copy-start.5 = (s32[32,64]{1,0:T(8,128)S(1)}, s32[32,64]{1,0:T(8,128)}, u32[]{:S(2)}) copy-start(s32[32,64]{1,0:T(8,128)} %param.15) | copy-start | bytes 24580
  2.8 0.7 copy-start.8
  3.5 14.7 %collective-permute-start = (f32[24,128]{1,0:T(8,128)S(1)}, f32[24,128]{1,0:T(8,128)S(1)}, u32[]{:S(2)}, u32[]{:S(2)}) collective-permute-start(f32[24,128]{1,0:T(8,128)S(1)} %concatenate.27), channel_id=1, source_target_pairs={{0,0},{1,32},{2,128},{3,160},{4,256},{5,288},{6,384},{7,416},{8,8}... | collective-permute-start | bytes 36872 | tf_op jit(solution)/shard_map/ppermute | solution.py:501
  18.2 5.4 %copy-start.4 = (bf16[2,8,64]{2,1,0:T(8,128)(2,1)S(1)}, bf16[2,8,64]{2,1,0:T(8,128)(2,1)}, u32[]{:S(2)}) copy-start(bf16[2,8,64]{2,1,0:T(8,128)(2,1)} %param.18) | copy-start | bytes 6148
  18.3 5.4 %collective-permute-start.2 = (f32[1,8,128]{2,1,0:T(8,128)S(1)}, f32[1,8,128]{2,1,0:T(8,128)S(1)}, u32[]{:S(2)}, u32[]{:S(2)}) collective-permute-start(f32[1,8,128]{2,1,0:T(8,128)S(1)} %bitcast.44), channel_id=1, source_target_pairs={{0,71},{32,103},{128,199},{160,231},{256,327},{288,359},{384,455},... | collective-permute-start | bytes 12296 | tf_op jit(solution)/shard_map/ppermute | solution.py:460
  20.2 5.6 %collective-permute-start.1 = (f32[1,8,128]{2,1,0:T(8,128)S(1)}, f32[1,8,128]{2,1,0:T(8,128)S(1)}, u32[]{:S(2)}, u32[]{:S(2)}) collective-permute-start(f32[1,8,128]{2,1,0:T(8,128)S(1)} %bitcast.45), channel_id=1, source_target_pairs={{0,1},{32,33},{128,129},{160,161},{256,257},{288,289},{384,385},{4... | collective-permute-start | bytes 12296 | tf_op jit(solution)/shard_map/ppermute | solution.py:460
  25.8 6.1 %collective-permute-start.3 = (f32[3,8,128]{2,1,0:T(8,128)S(1)}, f32[3,8,128]{2,1,0:T(8,128)S(1)}, u32[]{:S(2)}, u32[]{:S(2)}) collective-permute-start(f32[3,8,128]{2,1,0:T(8,128)S(1)} %pad_maximum_fusion), channel_id=1, source_target_pairs={{0,8},{32,40},{128,136},{160,168},{256,264},{288,296},{384,392},{4... | collective-permute-start | bytes 36872 | tf_op jit(solution)/shard_map/ppermute | solution.py:460
  29.0 0.7 copy-start.7
  29.8 4.4 %collective-permute-start.4 = (f32[3,8,128]{2,1,0:T(8,128)S(1)}, f32[3,8,128]{2,1,0:T(8,128)S(1)}, u32[]{:S(2)}, u32[]{:S(2)}) collective-permute-start(f32[3,8,128]{2,1,0:T(8,128)S(1)} %pad_maximum_fusion), channel_id=1, source_target_pairs={{0,24},{32,56},{128,152},{160,184},{256,280},{288,312},{384,408},{... | collective-permute-start | bytes 36872 | tf_op jit(solution)/shard_map/ppermute | solution.py:460
  34.3 15.2 %collective-permute-start.6 = (f32[9,8,128]{2,1,0:T(8,128)S(1)}, f32[9,8,128]{2,1,0:T(8,128)S(1)}, u32[]{:S(2)}, u32[]{:S(2)}) collective-permute-start(f32[9,8,128]{2,1,0:T(8,128)S(1)} %constant_dynamic-update-slice_fusion.refs_3_), channel_id=1, source_target_pairs={{0,416},{32,0},{128,32},{160,128},{256,160},{288,256},{384,288},{4... | collective-permute-start | bytes 110600 | tf_op jit(solution)/shard_map/ppermute | solution.py:460
  37.3 12.2 %collective-permute-start.5 = (f32[9,8,128]{2,1,0:T(8,128)S(1)}, f32[9,8,128]{2,1,0:T(8,128)S(1)}, u32[]{:S(2)}, u32[]{:S(2)}) collective-permute-start(f32[9,8,128]{2,1,0:T(8,128)S(1)} %constant_dynamic-update-slice_fusion.refs_3_), channel_id=1, source_target_pairs={{0,32},{32,128},{128,160},{160,256},{256,288},{288,384},{384,416},... | collective-permute-start | bytes 110600 | tf_op jit(solution)/shard_map/ppermute | solution.py:460
  46.2 0.8 slice-start
  47.0 0.8 copy-start.1
  47.7 0.7 copy-start.6
  47.7 0.9 slice-start.1
  48.4 0.9 slice-start.2
  51.1 10.4 %copy-start.3 = (bf16[5,128,128]{2,1,0:T(8,128)(2,1)S(1)}, bf16[5,128,128]{2,1,0:T(8,128)(2,1)}, u32[]{:S(2)}) copy-start(bf16[5,128,128]{2,1,0:T(8,128)(2,1)} %param.22) | copy-start | bytes 491524
  51.1 6.6 %collective-permute-start.7 = (bf16[16,512]{1,0:T(8,128)(2,1)S(1)}, bf16[16,512]{1,0:T(8,128)(2,1)S(1)}, u32[]{:S(2)}, u32[]{:S(2)}) collective-permute-start(bf16[16,512]{1,0:T(8,128)(2,1)S(1)} %get-tuple-element.31), channel_id=1, source_target_pairs={{0,1},{32,33},{128,129},{160,161},{256,257},{288,289},{384,385},{4... | collective-permute-start | bytes 49160 | tf_op jit(solution)/shard_map/ppermute | solution.py:460
  53.1 5.4 %collective-permute-start.8 = (bf16[16,512]{1,0:T(8,128)(2,1)S(1)}, bf16[16,512]{1,0:T(8,128)(2,1)S(1)}, u32[]{:S(2)}, u32[]{:S(2)}) collective-permute-start(bf16[16,512]{1,0:T(8,128)(2,1)S(1)} %get-tuple-element.31), channel_id=1, source_target_pairs={{0,71},{32,103},{128,199},{160,231},{256,327},{288,359},{384,455},... | collective-permute-start | bytes 49160 | tf_op jit(solution)/shard_map/ppermute | solution.py:460
  58.6 7.1 %collective-permute-start.9 = (bf16[48,512]{1,0:T(8,128)(2,1)S(1)}, bf16[48,512]{1,0:T(8,128)(2,1)S(1)}, u32[]{:S(2)}, u32[]{:S(2)}) collective-permute-start(bf16[48,512]{1,0:T(8,128)(2,1)S(1)} %constant_dynamic-update-slice_fusion.5), channel_id=1, source_target_pairs={{0,8},{32,40},{128,136},{160,168},{256,264},{288,296},{384,392},{4... | collective-permute-start | bytes 147464 | tf_op jit(solution)/shard_map/ppermute | solution.py:460
  61.5 0.8 slice-start.3
  62.3 0.8 copy-start
  63.3 4.8 %collective-permute-start.10 = (bf16[48,512]{1,0:T(8,128)(2,1)S(1)}, bf16[48,512]{1,0:T(8,128)(2,1)S(1)}, u32[]{:S(2)}, u32[]{:S(2)}) collective-permute-start(bf16[48,512]{1,0:T(8,128)(2,1)S(1)} %constant_dynamic-update-slice_fusion.5), channel_id=1, source_target_pairs={{0,24},{32,56},{128,152},{160,184},{256,280},{288,312},{384,408},{... | collective-permute-start | bytes 147464 | tf_op jit(solution)/shard_map/ppermute | solution.py:460
  68.2 6.6 %collective-permute-start.12 = (bf16[144,512]{1,0:T(8,128)(2,1)S(1)}, bf16[144,512]{1,0:T(8,128)(2,1)S(1)}, u32[]{:S(2)}, u32[]{:S(2)}) collective-permute-start(bf16[144,512]{1,0:T(8,128)(2,1)S(1)} %constant_dynamic-update-slice_fusion.8.mid), channel_id=1, source_target_pairs={{0,416},{32,0},{128,32},{160,128},{256,160},{288,256},{384,288},{4... | collective-permute-start | bytes 442376 | tf_op jit(solution)/shard_map/ppermute | solution.py:460
  68.2 6.6 %collective-permute-start.11 = (bf16[144,512]{1,0:T(8,128)(2,1)S(1)}, bf16[144,512]{1,0:T(8,128)(2,1)S(1)}, u32[]{:S(2)}, u32[]{:S(2)}) collective-permute-start(bf16[144,512]{1,0:T(8,128)(2,1)S(1)} %constant_dynamic-update-slice_fusion.8.mid), channel_id=1, source_target_pairs={{0,32},{32,128},{128,160},{160,256},{256,288},{288,384},{384,416},... | collective-permute-start | bytes 442376 | tf_op jit(solution)/shard_map/ppermute | solution.py:460
  84.1 5.1 %collective-permute-start.13 = (bf16[144,512]{1,0:T(8,128)(2,1)S(1)}, bf16[144,512]{1,0:T(8,128)(2,1)S(1)}, u32[]{:S(2)}, u32[]{:S(2)}) collective-permute-start(bf16[144,512]{1,0:T(8,128)(2,1)S(1)} %get-tuple-element.34), channel_id=1, source_target_pairs={{0,32},{32,128},{128,160},{160,256},{256,288},{288,384},{384,416},... | collective-permute-start | bytes 442376 | tf_op jit(solution)/shard_map/ppermute | solution.py:460
  87.1 5.8 %collective-permute-start.14 = (bf16[144,512]{1,0:T(8,128)(2,1)S(1)}, bf16[144,512]{1,0:T(8,128)(2,1)S(1)}, u32[]{:S(2)}, u32[]{:S(2)}) collective-permute-start(bf16[144,512]{1,0:T(8,128)(2,1)S(1)} %get-tuple-element.35), channel_id=1, source_target_pairs={{0,416},{32,0},{128,32},{160,128},{256,160},{288,256},{384,288},{4... | collective-permute-start | bytes 442376 | tf_op jit(solution)/shard_map/ppermute | solution.py:460
  92.9 15.3 %copy-start.2 = (bf16[6,128,128]{2,1,0:T(8,128)(2,1)S(1)}, bf16[6,128,128]{2,1,0:T(8,128)(2,1)}, u32[]{:S(2)}) copy-start(bf16[6,128,128]{2,1,0:T(8,128)(2,1)} %param.21) | copy-start | bytes 589828
  93.0 5.4 %collective-permute-start.15 = (bf16[48,512]{1,0:T(8,128)(2,1)S(1)}, bf16[48,512]{1,0:T(8,128)(2,1)S(1)}, u32[]{:S(2)}, u32[]{:S(2)}) collective-permute-start(bf16[48,512]{1,0:T(8,128)(2,1)S(1)} %get-tuple-element.44), channel_id=1, source_target_pairs={{0,8},{32,40},{128,136},{160,168},{256,264},{288,296},{384,392},{4... | collective-permute-start | bytes 147464 | tf_op jit(solution)/shard_map/ppermute | solution.py:460
  96.2 4.8 %collective-permute-start.16 = (bf16[48,512]{1,0:T(8,128)(2,1)S(1)}, bf16[48,512]{1,0:T(8,128)(2,1)S(1)}, u32[]{:S(2)}, u32[]{:S(2)}) collective-permute-start(bf16[48,512]{1,0:T(8,128)(2,1)S(1)} %get-tuple-element.45), channel_id=1, source_target_pairs={{0,24},{32,56},{128,152},{160,184},{256,280},{288,312},{384,408},{... | collective-permute-start | bytes 147464 | tf_op jit(solution)/shard_map/ppermute | solution.py:460
  101.0 7.3 %collective-permute-start.17 = (bf16[16,512]{1,0:T(8,128)(2,1)S(1)}, bf16[16,512]{1,0:T(8,128)(2,1)S(1)}, u32[]{:S(2)}, u32[]{:S(2)}) collective-permute-start(bf16[16,512]{1,0:T(8,128)(2,1)S(1)} %get-tuple-element.46), channel_id=1, source_target_pairs={{0,1},{32,33},{128,129},{160,161},{256,257},{288,289},{384,385},{4... | collective-permute-start | bytes 49160 | tf_op jit(solution)/shard_map/ppermute | solution.py:460
  102.9 6.0 %collective-permute-start.18 = (bf16[16,512]{1,0:T(8,128)(2,1)S(1)}, bf16[16,512]{1,0:T(8,128)(2,1)S(1)}, u32[]{:S(2)}, u32[]{:S(2)}) collective-permute-start(bf16[16,512]{1,0:T(8,128)(2,1)S(1)} %get-tuple-element.47), channel_id=1, source_target_pairs={{0,71},{32,103},{128,199},{160,231},{256,327},{288,359},{384,455},... | collective-permute-start | bytes 49160 | tf_op jit(solution)/shard_map/ppermute | solution.py:460
  112.1 3.4 %collective-permute-start.19 = (f32[9,8,128]{2,1,0:T(8,128)S(1)}, f32[9,8,128]{2,1,0:T(8,128)S(1)}, u32[]{:S(2)}, u32[]{:S(2)}) collective-permute-start(f32[9,8,128]{2,1,0:T(8,128)S(1)} %get-tuple-element.40), channel_id=1, source_target_pairs={{0,32},{32,128},{128,160},{160,256},{256,288},{288,384},{384,416},... | collective-permute-start | bytes 110600 | tf_op jit(solution)/shard_map/ppermute | solution.py:460
  114.4 4.6 %collective-permute-start.20 = (f32[9,8,128]{2,1,0:T(8,128)S(1)}, f32[9,8,128]{2,1,0:T(8,128)S(1)}, u32[]{:S(2)}, u32[]{:S(2)}) collective-permute-start(f32[9,8,128]{2,1,0:T(8,128)S(1)} %get-tuple-element.41), channel_id=1, source_target_pairs={{0,416},{32,0},{128,32},{160,128},{256,160},{288,256},{384,288},{4... | collective-permute-start | bytes 110600 | tf_op jit(solution)/shard_map/ppermute | solution.py:460
  119.0 5.3 %collective-permute-start.21 = (f32[3,8,128]{2,1,0:T(8,128)S(1)}, f32[3,8,128]{2,1,0:T(8,128)S(1)}, u32[]{:S(2)}, u32[]{:S(2)}) collective-permute-start(f32[3,8,128]{2,1,0:T(8,128)S(1)} %get-tuple-element.48), channel_id=1, source_target_pairs={{0,8},{32,40},{128,136},{160,168},{256,264},{288,296},{384,392},{4... | collective-permute-start | bytes 36872 | tf_op jit(solution)/shard_map/ppermute | solution.py:460
  122.2 4.4 %collective-permute-start.22 = (f32[3,8,128]{2,1,0:T(8,128)S(1)}, f32[3,8,128]{2,1,0:T(8,128)S(1)}, u32[]{:S(2)}, u32[]{:S(2)}) collective-permute-start(f32[3,8,128]{2,1,0:T(8,128)S(1)} %get-tuple-element.49), channel_id=1, source_target_pairs={{0,24},{32,56},{128,152},{160,184},{256,280},{288,312},{384,408},{... | collective-permute-start | bytes 36872 | tf_op jit(solution)/shard_map/ppermute | solution.py:460
  126.7 7.1 %collective-permute-start.23 = (f32[1,8,128]{2,1,0:T(8,128)S(1)}, f32[1,8,128]{2,1,0:T(8,128)S(1)}, u32[]{:S(2)}, u32[]{:S(2)}) collective-permute-start(f32[1,8,128]{2,1,0:T(8,128)S(1)} %get-tuple-element.52), channel_id=1, source_target_pairs={{0,1},{32,33},{128,129},{160,161},{256,257},{288,289},{384,385},{4... | collective-permute-start | bytes 12296 | tf_op jit(solution)/shard_map/ppermute | solution.py:460
  128.6 5.9 %collective-permute-start.24 = (f32[1,8,128]{2,1,0:T(8,128)S(1)}, f32[1,8,128]{2,1,0:T(8,128)S(1)}, u32[]{:S(2)}, u32[]{:S(2)}) collective-permute-start(f32[1,8,128]{2,1,0:T(8,128)S(1)} %get-tuple-element.53), channel_id=1, source_target_pairs={{0,71},{32,103},{128,199},{160,231},{256,327},{288,359},{384,455},... | collective-permute-start | bytes 12296 | tf_op jit(solution)/shard_map/ppermute | solution.py:460
  134.6 12.5 %collective-permute-start.25 = (f32[8,128]{1,0:T(8,128)S(1)}, f32[8,128]{1,0:T(8,128)S(1)}, u32[]{:S(2)}, u32[]{:S(2)}) collective-permute-start(f32[8,128]{1,0:T(8,128)S(1)} %shard_map.135), channel_id=1, source_target_pairs={{0,0},{32,1},{128,2},{160,3},{256,4},{288,5},{384,6},{416,7},{8,8}... | collective-permute-start | bytes 12296 | tf_op jit(solution)/shard_map/ppermute | solution.py:583

commit v3 on v2

--- a/solution.py
+++ b/solution.py
@@ -89,18 +89,16 @@
     return sine * part * sign, cosine * sign
 
 
-def geometry(table, index, count, with_slope):
+def geometry(table, index, count):
     found = gather_entries(table, index)
     first = column(table, 0)
     centre = jnp.where(iota((8, LANES), 1) < SLOTS, first, pltpu.roll(first, SLOTS, 1))
     centre = jnp.concatenate([centre] * COLUMNS, axis=1)
     rows = iota((8, PAIRS), 0)
     delta = jnp.where(rows < 3, found - centre, 0.0)
-    kind = found[3:4, :]
     square = jnp.sum(delta * delta, axis=0, keepdims=True) + SOFTEN
     inverse = lax.rsqrt(square)
     distance = square * inverse
-    unit = delta * inverse
     slot = iota((1, PAIRS), 1) % SLOTS
     paired = jnp.where(index != slot, jnp.concatenate([live_row(count)] * COLUMNS, axis=1), 0.0)
     scaled = jnp.minimum(distance * (1.0 / CUTOFF), 1.0)
@@ -111,14 +109,21 @@
     sine, cosine = sincos_pi(orders * scaled)
     weight = envelope * paired * inverse
     basis = (sine * weight).astype(BF16)
-    if not with_slope:
-        return unit, inverse, kind, basis, None
     rest = 1.0 - scaled
     slope = (-168.0 / CUTOFF) * (power * rest * rest) / jnp.maximum(scaled, 1e-3)
     basis_slope = weight * cosine * (orders * (math.pi / CUTOFF)) + sine * (
         slope * paired * inverse - weight * inverse
     )
-    return unit, inverse, kind, basis, basis_slope
+    facts = jnp.where(rows == 3, inverse, jnp.where(rows == 4, found[3:4, :], delta * inverse))
+    return facts, basis, basis_slope
+
+
+def unit_of(facts):
+    return jnp.where(iota((8, PAIRS), 0) < 3, facts, 0.0)
+
+
+def species_of(facts):
+    return (iota((16, PAIRS), 0) % 8 == facts[4:5, :].astype(jnp.int32)).astype(F32).astype(BF16)
 
 
 def split(values):
@@ -134,7 +139,7 @@
     half = grad_radial.shape[0] // 2
     grad_hidden = keep(dot_nn(wout[...], grad_radial[0:half, :]) + dot_nn(wout[...], grad_radial[half:, :]))
     high, low = split(grad_hidden * (gate * (1.0 + before * (1.0 - gate))))
-    grad_basis = keep(dot_nn(win[...], high) + dot_nn(win[...], low))
+    grad_basis = keep(dot_nn(win, high) + dot_nn(win, low))
     return jnp.sum(grad_basis * basis_slope, axis=0, keepdims=True)
 
 
@@ -157,23 +162,88 @@
     return out
 
 
-def start_kernel(arrived, own, payload, picked, index, count):
-    own[...] = jnp.zeros_like(own)
-    own[0:4, 0:SLOTS] = arrived[COLUMNS : COLUMNS + 4, 0:SLOTS]
+def flip(matrix):
+    size = matrix.shape[1]
+    eye = (iota((size, size), 0) == iota((size, size), 1)).astype(F32).astype(BF16)
+    return dot_nt(eye, matrix).astype(BF16)
+
+
+def weights_kernel(
+    embedding, radial_in, radial_out_one, radial_out_two, mix_one, mix_two, readout,
+    emb_t, win_t, one_t, two_t, mix_a, mix_b, mix_two_t, spread, read_t, rests,
+):
+    emb = jnp.concatenate([embedding[...].astype(F32), jnp.zeros((1, C), F32)], axis=0).astype(BF16)
+    emb_t[...] = flip(emb)
+    for t in range(2):
+        win_t[t] = flip(radial_in[t])
+        mix_two_t[t] = flip(mix_two[t])
+    one_t[...] = flip(radial_out_one[...])
+    two_t[...] = flip(radial_out_two[...])
+    for k in range(3):
+        mix_a[:, k * C : (k + 1) * C] = flip(mix_one[k + 1])
+    for k in range(2):
+        mix_b[:, k * C : (k + 1) * C] = flip(mix_one[k + 4])
+    pe_high, pe_low = split(dot_nt(flip(mix_one[0]), emb))
+    spread[...] = jnp.concatenate([pe_high.astype(F32), pe_low.astype(F32)], axis=1).astype(BF16)
+    read = jnp.concatenate([readout[...], jnp.zeros((LANES - 2, C), F32)], axis=0)
+    read_t[...] = read.T
+    read_high, read_low = split(read[0:16])
+    for k in range(3):
+        rests[k * C : (k + 1) * C, :] = dot_nt(mix_two[k + 2], read_high) + dot_nt(mix_two[k + 2], read_low)
+
+
+def renamed(index):
+    block = (index - SLOTS) >> 4
+    nines = (block * 57) >> 9
+    threes = (block * 11) >> 5
+    turned = (block - threes * 3) * 9 + (threes - nines * 3) * 3 + nines
+    return jnp.where(index < SLOTS, index, SLOTS + turned * EXPORT + (index & (EXPORT - 1))).astype(F32)
+
+
+def pack_kernel(exports, counts, positions, species, neighbours, packed, payload, picked, count):
+    even = renamed(neighbours[pl.ds(0, COLUMNS, stride=2), :])
+    odd = renamed(neighbours[pl.ds(1, COLUMNS, stride=2), :])
+    lane = iota((8, LANES), 1) % EXPORT
+    row = iota((EXPORT, LANES), 0)
+    source = jnp.zeros((8, LANES), jnp.int32)
+    pick = jnp.zeros((EXPORT, LANES), jnp.int32)
+    for e in range(EXPORT):
+        slot = exports[e]
+        source = jnp.where(lane == e, slot, source)
+        pick = jnp.where(row == e, slot, pick)
+    picked[...] = pick
+    count[...] = jnp.full((1, LANES), counts[0], jnp.int32)
+    packed[...] = jnp.zeros_like(packed)
+    packed[0:COLUMNS, :] = jnp.concatenate([even, odd], axis=1)
+    packed[COLUMNS : COLUMNS + 3, 0:SLOTS] = positions[...]
+    packed[COLUMNS + 3 : COLUMNS + 4, 0:SLOTS] = species[...].astype(F32)
+    packed[COLUMNS + 4 : COLUMNS + 5, :] = source[0:1, :].astype(F32)
+    packed[COLUMNS + 5 : COLUMNS + 6, :] = jnp.full((1, LANES), counts[0], jnp.int32).astype(F32)
+    whole = packed[COLUMNS : COLUMNS + 8, :]
+    whole = jnp.where(iota((8, LANES), 0) < 4, whole, 0.0)
+    payload[...] = jnp.take_along_axis(whole, source, axis=1)
+
+
+def unpack_kernel(arrived, low, high, own, block, picked, index, count):
+    whole = arrived[COLUMNS : COLUMNS + 8, :]
+    whole = jnp.where(iota((8, LANES), 0) < 4, whole, 0.0)
+    own[...] = whole
     exports = arrived[COLUMNS + 4 : COLUMNS + 5, :]
     count[...] = arrived[COLUMNS + 5 : COLUMNS + 6, :].astype(jnp.int32)
     mine = iota((EXPORT, LANES), 1) == iota((EXPORT, LANES), 0)
     pick = jnp.sum(jnp.where(mine, exports, 0.0), axis=1, keepdims=True)
     picked[...] = jnp.broadcast_to(pick, (EXPORT, LANES)).astype(jnp.int32)
     source = jnp.broadcast_to(exports, (8, LANES)).astype(jnp.int32)
-    payload[...] = jnp.take_along_axis(own[...], source, axis=1)
+    block[0] = low[...]
+    block[1] = jnp.take_along_axis(whole, source, axis=1)
+    block[2] = high[...]
     for m in range(COLUMNS):
         index[:, m * LANES : (m + 1) * LANES] = arrived[m : m + 1, :].astype(jnp.int32)
 
 
 def first_kernel(
-    count_ref, own, low, mid, high, index, picked, win_t, wout_t, mix_a, mix_b, mix0_t, emb, emb_t, read_t,
-    table, own_rows, outgoing, sums, energy, spread, radial,
+    count_ref, own, low, mid, high, index, picked, win_t, wout_t, mix_a, mix_b, spread, emb_t, read_t,
+    facts_out, basis_out, slope_out, own_rows, outgoing, sums, energy,
 ):
     count = count_ref[...]
     group = iota((8, LANES), 1) // EXPORT
@@ -189,28 +259,23 @@
         tile = entry // LANES
         at = entry % LANES // EXPORT
         tiles[tile] = jnp.where(group == at, slabs[oz + 1][b % 9] + shift, tiles[tile])
-    for v in range(4):
-        table[:, v * LANES : (v + 1) * LANES] = tiles[v]
     whole = jnp.concatenate(tiles, axis=1)
-    ids = index[...]
-    unit, inverse, kind, basis, _ = geometry(whole, ids, count, False)
-    before, gate = hidden_of(win_t[...], basis)
+    facts, basis, basis_slope = geometry(whole, index[...], count)
+    facts_out[...] = facts
+    basis_out[...] = basis
+    slope_out[...] = basis_slope
+    before, gate = hidden_of(win_t[0], basis)
     hidden = (before * gate).astype(BF16)
-    pe = dot_nt(mix0_t[...], emb[...])
-    pe_high = pe.astype(BF16)
-    pe_low = (pe - pe_high.astype(F32)).astype(BF16)
-    pe_both = jnp.concatenate([pe_high.astype(F32), pe_low.astype(F32)], axis=1).astype(BF16)
-    spread[...] = pe_both
-    species = (iota((16, PAIRS), 0) % 8 == kind.astype(jnp.int32)).astype(F32).astype(BF16)
+    species = species_of(facts)
     a0 = jnp.zeros((C, LANES), F32)
     a1 = [jnp.zeros((C, LANES), F32) for _ in range(3)]
     for m in range(COLUMNS):
         radial = dot_nn(wout_t[...], column(hidden, m))
-        source = dot_nn(pe_both, column(species, m))
+        source = dot_nn(spread[...], column(species, m))
         a0 = a0 + radial[:C] * source
         t = radial[C:] * source
         for x in range(3):
-            a1[x] = a1[x] + t * column(unit[x : x + 1], m)
+            a1[x] = a1[x] + t * column(facts[x : x + 1], m)
     a0 = fold(a0) * NORM
     a1 = [fold(v) * NORM for v in a1]
     for x, v in enumerate([a0] + a1):
@@ -237,14 +302,15 @@
 
 
 def second_kernel(
-    count_ref, table, own_rows, low, mid, high, index, win_t, win, wout_t, wout, mix_t, mix_rest, read,
+    count_ref, facts_ref, basis, slope, own_rows, low, mid, high, index, win_t, win, wout_t, wout, mix_t, rests, read,
     grad_own, grad_low, grad_mid, grad_high, pair_out, energy,
     feats, turned, onehot, radial, source, grad_radial, grad_source,
 ):
     count = count_ref[...]
     ids = index[...]
-    unit, inverse, _, basis, basis_slope = geometry(table[...], ids, count, True)
-    before, gate = hidden_of(win_t[...], basis)
+    facts = facts_ref[...]
+    unit, inverse = unit_of(facts), facts[3:4, :]
+    before, gate = hidden_of(win_t[1], basis[...])
     hidden = (before * gate).astype(BF16)
     feats[0:SLOTS, :] = own_rows[...]
     feats[SLOTS : SLOTS + SLAB, :] = low[...]
@@ -281,9 +347,6 @@
     a0 = fold(a0) * NORM
     a1 = [fold(v) * NORM for v in a1]
     quad = a1[0] * a1[0] + a1[1] * a1[1] + a1[2] * a1[2]
-    read_high = read[...].astype(BF16)
-    read_low = (read[...] - read_high.astype(F32)).astype(BF16)
-    rests = dot_nt(mix_rest[...], read_high) + dot_nt(mix_rest[...], read_low)
     m2, m3, m4 = [rests[k * C : (k + 1) * C, 1:2] for k in range(3)]
     live = live_row(count)
     energy[...] = live * jnp.sum(a0 * m2 + a0 * a0 * m3 + quad * m4, axis=0, keepdims=True)
@@ -311,7 +374,7 @@
             grad_source[(x + 1) * C : (x + 2) * C, here] = (q * u[x] + r3 * d1[x]).astype(BF16)
             grad_units[x].append(jnp.sum(q * v[x] + t * d1[x], axis=0, keepdims=True))
     grad_unit = stack_rows([jnp.concatenate(g, axis=1) for g in grad_units])
-    grad_distance = grad_distance_of(wout, win, grad_radial, before, gate, basis_slope)
+    grad_distance = grad_distance_of(wout, win[1], grad_radial, before, gate, slope[...])
     pair_out[...] = pair_gradient(unit, inverse, grad_unit, grad_distance)
     grad_projected = dot_nt(onehot[...], grad_source[...])
     outs = (grad_low, grad_mid, grad_high)
@@ -330,16 +393,18 @@
 
 
 def third_kernel(
-    count_ref, table, sums, grad_own, back, picked, pair_in, index, win_t, win, wout_t, wout, mix_rest, spread, read_t,
+    count_ref, facts_ref, basis, slope, sums, grad_own, back, picked, pair_in, index, energy_one, energy_two,
+    win_t, win, wout_t, wout, mix_one, spread, read_t,
     grad_mine, grad_low, grad_mid, grad_high,
     onehot, grad_radial,
 ):
     count = count_ref[...]
     ids = index[...]
-    unit, inverse, kind, basis, basis_slope = geometry(table[...], ids, count, True)
-    before, gate = hidden_of(win_t[...], basis)
+    facts = facts_ref[...]
+    unit, inverse = unit_of(facts), facts[3:4, :]
+    before, gate = hidden_of(win_t[0], basis[...])
     hidden = (before * gate).astype(BF16)
-    species = (iota((16, PAIRS), 0) % 8 == kind.astype(jnp.int32)).astype(F32).astype(BF16)
+    species = species_of(facts)
     entry = iota((TABLE, LANES), 0)
     for m in range(COLUMNS):
         onehot[:, m * LANES : (m + 1) * LANES] = (entry == column(ids, m)).astype(F32).astype(BF16)
@@ -359,8 +424,10 @@
     gv = [grads[(x + 1) * C : (x + 2) * C] for x in range(3)]
     a0 = sums[0:C, :]
     a1 = [sums[(x + 1) * C : (x + 2) * C, :] for x in range(3)]
-    first = fold(dot_nn(mix_rest[0 : 3 * C, :], halves(gs)))
-    others = fold_columns(dot_nn(mix_rest[3 * C : 5 * C, :], jnp.concatenate([halves(g) for g in gv], axis=1)))
+    scalar_parts = halves(gs)
+    vector_parts = jnp.concatenate([halves(g) for g in gv], axis=1)
+    first = jnp.concatenate([fold(dot_nn(mix_one[k], scalar_parts)) for k in (1, 2, 3)], axis=0)
+    others = jnp.concatenate([fold_columns(dot_nn(mix_one[k], vector_parts)) for k in (4, 5)], axis=0)
     straight = [column(others[0:C], x) for x in range(3)]
     crossed = [column(others[C : 2 * C], x) for x in range(3)]
     scale = live * NORM
@@ -385,7 +452,7 @@
         for x in range(3):
             grad_units[x].append(jnp.sum(q * d1[x], axis=0, keepdims=True))
     grad_unit = stack_rows([jnp.concatenate(g, axis=1) for g in grad_units])
-    grad_distance = grad_distance_of(wout, win, grad_radial, before, gate, basis_slope)
+    grad_distance = grad_distance_of(wout, win[0], grad_radial, before, gate, slope[...])
     pairs = pair_in[...] + pair_gradient(unit, inverse, grad_unit, grad_distance)
     pair_high = pairs.astype(BF16)
     pair_low = (pairs - pair_high.astype(F32)).astype(BF16)
@@ -395,7 +462,8 @@
     total = column(pairs, 0)
     for m in range(1, COLUMNS):
         total = total + column(pairs, m)
-    grad_mine[...] = column(grads, 0) - fold(total)
+    energies = live * (energy_one[...] + energy_two[...])
+    grad_mine[...] = jnp.where(iota((8, LANES), 0) == 3, energies, column(grads, 0) - fold(total))
     outs = (grad_low, grad_mid, grad_high)
     for b in range(27):
         at = SLOTS + b * EXPORT
@@ -411,24 +479,28 @@
     return jnp.concatenate([fold(column(values, x)) for x in range(count)], axis=1)
 
 
-def last_kernel(count_ref, grad_mine, back, picked, energy_one, energy_two, out):
+def last_kernel(count, main, from_low, from_high, picked, forces, energies):
     same = iota((EXPORT, LANES), 1) == picked[...]
     entry = jnp.sum(jnp.where(same, iota((EXPORT, LANES), 0), 0), axis=0, keepdims=True)
     hit = jnp.sum(same.astype(F32), axis=0, keepdims=True)
-    came = jnp.take_along_axis(back[...], jnp.broadcast_to(entry, (8, LANES)), axis=1)
-    forces = -(grad_mine[...] + came * hit)
-    energies = live_row(count_ref[...]) * (energy_one[...] + energy_two[...])
-    out[...] = jnp.where(iota((8, LANES), 0) == 3, energies, forces)
-
-
-def call(kernel, outs, specs, scratch=(), limit=None):
+    back = main[8:16, :] + from_low[...] + from_high[...]
+    came = jnp.take_along_axis(back, jnp.broadcast_to(entry, (8, LANES)), axis=1)
+    total = main[0:8, :] + came * hit
+    forces[...] = -total[0:3, 0:SLOTS]
+    energies[...] = (main[3:4, :] * live_row(count[...]))[:, 0:SLOTS]
+
+
+def call(kernel, outs, specs, scratch=(), limit=None, smem=0, cost=None):
+    in_specs = [pl.BlockSpec(memory_space=pltpu.SMEM)] * smem
+    in_specs += [pl.BlockSpec(memory_space=pltpu.VMEM)] * (len(specs) - smem)
     return pl.pallas_call(
         kernel,
         out_shape=[jax.ShapeDtypeStruct(s, t) for s, t in outs],
-        in_specs=[pl.BlockSpec(memory_space=pltpu.VMEM)] * len(specs),
+        in_specs=in_specs,
         out_specs=[pl.BlockSpec(memory_space=pltpu.VMEM)] * len(outs),
         scratch_shapes=[pltpu.VMEM(s, t) for s, t in scratch],
         compiler_params=pltpu.CompilerParams(vmem_limit_bytes=limit or (16 << 20)),
+        cost_estimate=cost,
     )(*specs)
 
 
@@ -444,8 +516,12 @@
     return given(z // 2 * 4 + x // 8 * 2 + z % 2, y, x % 8)
 
 
-MOVE_IN = [(given(*d), seat(*d)) for d in DOMAINS]
-MOVE_OUT = [(there, here) for here, there in MOVE_IN]
+def move_in(step):
+    return [(given(x, y, z), seat(x + step, y, z)) for x, y, z in DOMAINS]
+
+
+def move_out(step):
+    return [(seat(x, y, z), given((x + step) % 16, y, z)) for x, y, z in DOMAINS]
 
 
 def moves(step):
@@ -460,16 +536,16 @@
     return lax.ppermute(value, AXES, moves(step))
 
 
-def spread_halo(block):
-    for axis in range(2):
+def spread_halo(block, first=0):
+    for axis in range(first, 2):
         low = send(block, UP[axis])
         high = send(block, DOWN[axis])
         block = jnp.concatenate([low, block, high], axis=0)
     return send(block, UP[2]), block, send(block, DOWN[2])
 
 
-def gather_halo(low, mid, high):
-    for axis in (2, 1, 0):
+def gather_halo(low, mid, high, last=0):
+    for axis in range(2, last - 1, -1):
         from_low = send(high, UP[axis])
         from_high = send(low, DOWN[axis])
         block = mid + from_low + from_high
@@ -483,59 +559,63 @@
     positions, species, counts, neighbours, exports, embedding, radial_in,
     radial_out_one, radial_out_two, mix_one, mix_two, readout,
 ):
-    block = (neighbours - SLOTS) // EXPORT
-    turned = block % 3 * 9 + block // 3 % 3 * 3 + block // 9
-    moved = SLOTS + turned * EXPORT + neighbours % EXPORT
-    moved = jnp.where(neighbours < SLOTS, neighbours, moved).astype(F32)
-    slots = jnp.concatenate([positions, species.astype(F32)[None]], axis=0)
-    packed = jnp.concatenate(
+    packed, payload, picked_here, count_here = call(
+        pack_kernel,
+        [((24, LANES), F32), ((8, LANES), F32), ((EXPORT, LANES), jnp.int32), ((1, LANES), jnp.int32)],
+        [exports, counts, positions, species.reshape(1, SLOTS), neighbours],
+        smem=2,
+    )
+    emb_t, win_t, one_t, two_t, mix_a, mix_b, mix_two_t, spread, read_t, rests = call(
+        weights_kernel,
         [
-            moved.reshape(COLUMNS, LANES),
-            jnp.pad(slots, ((0, 0), (0, LANES - SLOTS))),
-            jnp.tile(exports.astype(F32), LANES // EXPORT)[None],
-            jnp.broadcast_to(counts.astype(F32)[None], (1, LANES)),
-            jnp.zeros((2, LANES), F32),
+            ((C, 8), BF16),
+            ((2, RH, NB), BF16),
+            ((2 * C, RH), BF16),
+            ((4 * C, RH), BF16),
+            ((C, 3 * C), BF16),
+            ((C, 2 * C), BF16),
+            ((2, C, C), BF16),
+            ((C, 16), BF16),
+            ((C, LANES), F32),
+            ((3 * C, 16), F32),
         ],
-        axis=0,
-    )
-    arrived = lax.ppermute(packed, AXES, MOVE_IN)
-    own, payload, picked, index, count = call(
-        start_kernel,
+        [embedding, radial_in, radial_out_one, radial_out_two, mix_one, mix_two, readout],
+        cost=pl.CostEstimate(flops=200_000_000, bytes_accessed=2_000_000, transcendentals=0),
+    )
+    arrived = lax.ppermute(packed, AXES, move_in(0))
+    low = lax.ppermute(payload, AXES, move_in(1))
+    high = lax.ppermute(payload, AXES, move_in(-1))
+    (
+        arrived, low, high, emb_t, win_t, one_t, two_t, mix_a, mix_b, mix_two_t, spread, read_t, rests,
+        radial_in, radial_out_one, radial_out_two, mix_one, readout,
+    ) = lax.optimization_barrier((
+        arrived, low, high, emb_t, win_t, one_t, two_t, mix_a, mix_b, mix_two_t, spread, read_t, rests,
+        radial_in, radial_out_one, radial_out_two, mix_one, readout,
+    ))
+    own, block, picked, index, count = call(
+        unpack_kernel,
         [
             ((8, LANES), F32),
-            ((8, LANES), F32),
+            ((3, 8, LANES), F32),
             ((EXPORT, LANES), jnp.int32),
             ((1, PAIRS), jnp.int32),
             ((1, LANES), jnp.int32),
         ],
-        [arrived],
-    )
-    emb = jnp.concatenate([embedding, jnp.zeros((1, C), BF16)], axis=0)
-    emb_t = emb.T
-    win_t = jnp.swapaxes(radial_in, 1, 2)
-    one_t = radial_out_one.T
-    two_t = radial_out_two.T
-    mix0_t = mix_one[0].T
-    mix_a = mix_one[1:4].reshape(3 * C, C).T
-    mix_b = mix_one[4:6].reshape(2 * C, C).T
-    mix_back = mix_one[1:6].reshape(5 * C, C)
-    mix_two_t = jnp.swapaxes(mix_two[0:2], 1, 2)
-    mix_two_rest = mix_two[2:5].reshape(3 * C, C)
-    read_t = readout.T
-    read = jnp.concatenate([readout, jnp.zeros((6, C), F32)], axis=0)
-
-    low, mid, high = spread_halo(payload[None])
-    table, own_rows, outgoing, sums, energy_one, spread = call(
-        lambda *refs: first_kernel(*refs, None),
+        [arrived, low, high],
+    )
+    low, mid, high = spread_halo(block, 1)
+    facts, basis, slope, own_rows, outgoing, sums, energy_one = call(
+        first_kernel,
         [
-            ((8, TABLE), F32),
+            ((8, PAIRS), F32),
+            ((8, PAIRS), BF16),
+            ((8, PAIRS), F32),
             ((SLOTS, 4 * C), BF16),
             ((EXPORT, 4 * C), BF16),
             ((4 * C, LANES), F32),
             ((1, LANES), F32),
-            ((C, 16), BF16),
         ],
-        [count, own, low, mid, high, index, picked, win_t[0], one_t, mix_a, mix_b, mix0_t, emb, emb_t, read_t],
+        [count, own, low, mid, high, index, picked, win_t, one_t, mix_a, mix_b, spread, emb_t, read_t],
     )
     low, mid, high = spread_halo(outgoing)
     grad_own, grad_low, grad_mid, grad_high, pairs, energy_two = call(
@@ -549,8 +629,8 @@
             ((1, LANES), F32),
         ],
         [
-            count, table, own_rows, low, mid, high, index, win_t[1], radial_in[1], two_t, radial_out_two,
-            mix_two_t, mix_two_rest, read,
+            count, facts, basis, slope, own_rows, low, mid, high, index, win_t, radial_in, two_t,
+            radial_out_two, mix_two_t, rests, readout,
         ],
         scratch=[
             ((TABLE, 4 * C), BF16),
@@ -568,20 +648,22 @@
         third_kernel,
         [((8, LANES), F32), ((9, 8, LANES), F32), ((9, 8, LANES), F32), ((9, 8, LANES), F32)],
         [
-            count, table, sums, grad_own, back, picked, pairs, index, win_t[0], radial_in[0], one_t,
-            radial_out_one, mix_back, spread, read_t,
+            count, facts, basis, slope, sums, grad_own, back, picked, pairs, index, energy_one, energy_two,
+            win_t, radial_in, one_t, radial_out_one, mix_one, spread, read_t,
         ],
         scratch=[((TABLE, PAIRS), BF16), ((4 * C, PAIRS), BF16)],
         limit=32 << 20,
     )
-    back = gather_halo(grad_low, grad_mid, grad_high)
-    (out,) = call(
+    block = gather_halo(grad_low, grad_mid, grad_high, 1)
+    main = lax.ppermute(jnp.concatenate([grad_mine, block[1]], axis=0), AXES, move_out(0))
+    from_low = lax.ppermute(block[2], AXES, move_out(1))
+    from_high = lax.ppermute(block[0], AXES, move_out(-1))
+    forces, energies = call(
         last_kernel,
-        [((8, LANES), F32)],
-        [count, grad_mine, back[0], picked, energy_one, energy_two],
-    )
-    out = lax.ppermute(out, AXES, MOVE_OUT)
-    return out[0:3, 0:SLOTS], out[3, 0:SLOTS]
+        [((3, SLOTS), F32), ((1, SLOTS), F32)],
+        [count_here, main, from_low, from_high, picked_here],
+    )
+    return forces, energies.reshape(SLOTS)
 
 
 def solution(mesh):

time: 149 us -> 158 us (1.060)
  the two profiles are of different devices: /device:TPU:15 before, /device:TPU:29 now
where the time goes in v3:
time: 158 us; the launch traced here: 157 us
  starting transfers between devices  87.6 us (55%)
  waiting for transfers between devices  47 us (30%)
  Pallas kernels  16.1 us (10%)
  local copies, waits for them, and re-layouts  4.89 us (3%)
  between operations  1.71 us (1%)
    ppermute x20, starting transfers between devices, send(): return lax.ppermute(value, AXES, moves(step))  46.7 us
    ppermute x20, waiting for transfers between devices, send(): return lax.ppermute(value, AXES, moves(step))  26.8 us
    pallas_call x7, Pallas kernels, call(): pl.pallas_call(kernel, out_shape=[jax.ShapeDtypeStruct(s, t) for s, t in...  16.1 us
    ppermute x1, starting transfers between devices, body(): high = lax.ppermute(payload, AXES, move_in(-1))  16.1 us
    ppermute x1, starting transfers between devices, body(): lax.ppermute(jnp.concatenate([grad_mine, block[1]], axis=0), AXES, move_o...  13 us
    ppermute x1, waiting for transfers between devices, body(): from_low = lax.ppermute(block[2], AXES, move_out(1))  7.89 us
    ppermute x1, waiting for transfers between devices, body(): from_high = lax.ppermute(block[0], AXES, move_out(-1))  6.23 us
    ppermute x1, starting transfers between devices, body(): from_high = lax.ppermute(block[0], AXES, move_out(-1))  6.08 us
  transfers between devices with their start and end apart: 26, of which 17 were waited for; matrix products, arithmetic and copies ran while one was open for 0% of the time, Pallas kernels for 0%

profile of v3, /device:TPU:29, one launch (start us, length us, event | category | flops | bytes accessed | tf_op | source)
XLA Modules:
  0.0 157.4 jit_solution(17170543625032478732)
XLA Ops:
  2.0 0.7 copy-done.7
  2.7 0.6 shard_map.131
  3.3 16.1 %collective-permute-start.2 = (f32[8,128]{1,0:T(8,128)S(1)}, f32[8,128]{1,0:T(8,128)S(1)}, u32[]{:S(2)}, u32[]{:S(2)}) collective-permute-start(f32[8,128]{1,0:T(8,128)S(1)} %get-tuple-element.60), channel_id=1, source_target_pairs={{0,71},{1,103},{2,199},{3,231},{4,327},{5,359},{6,455},{7,487},{8,... | collective-permute-start | bytes 12296 | tf_op jit(solution)/shard_map/ppermute | solution.py:587
  19.4 1.9 %collective-permute-start.1 = (f32[8,128]{1,0:T(8,128)S(1)}, f32[8,128]{1,0:T(8,128)S(1)}, u32[]{:S(2)}, u32[]{:S(2)}) collective-permute-start(f32[8,128]{1,0:T(8,128)S(1)} %get-tuple-element.60), channel_id=1, source_target_pairs={{0,1},{1,33},{2,129},{3,161},{4,257},{5,289},{6,385},{7,417},{8,9}... | collective-permute-start | bytes 12296 | tf_op jit(solution)/shard_map/ppermute | solution.py:586
  21.3 1.9 %collective-permute-start = (f32[24,128]{1,0:T(8,128)S(1)}, f32[24,128]{1,0:T(8,128)S(1)}, u32[]{:S(2)}, u32[]{:S(2)}) collective-permute-start(f32[24,128]{1,0:T(8,128)S(1)} %get-tuple-element.59), channel_id=1, source_target_pairs={{0,0},{1,32},{2,128},{3,160},{4,256},{5,288},{6,384},{7,416},{8,8}... | collective-permute-start | bytes 36872 | tf_op jit(solution)/shard_map/ppermute | solution.py:585
  23.3 0.9 copy-done
  24.2 0.8 copy-done.2
  25.1 0.8 copy-done.4
  25.8 0.9 copy-done.12
  26.7 0.7 shard_map.132
  27.7 5.9 %collective-permute-done.arrived = f32[24,128]{1,0:T(8,128)S(1)} collective-permute-done((f32[24,128]{1,0:T(8,128)S(1)}, f32[24,128]{1,0:T(8,128)S(1)}, u32[]{:S(2)}, u32[]{:S(2)}) %collective-permute-start) | collective-permute-done | bytes 12320 | tf_op jit(solution)/shard_map/ppermute | solution.py:585
  33.7 1.9 %collective-permute-start.3 = (f32[3,8,128]{2,1,0:T(8,128)S(1)}, f32[3,8,128]{2,1,0:T(8,128)S(1)}, u32[]{:S(2)}, u32[]{:S(2)}) collective-permute-start(f32[3,8,128]{2,1,0:T(8,128)S(1)} %get-tuple-element.76), channel_id=1, source_target_pairs={{0,8},{32,40},{128,136},{160,168},{256,264},{288,296},{384,392},{4... | collective-permute-start | bytes 36872 | tf_op jit(solution)/shard_map/ppermute | solution.py:536
  35.6 3.4 %collective-permute-start.4 = (f32[3,8,128]{2,1,0:T(8,128)S(1)}, f32[3,8,128]{2,1,0:T(8,128)S(1)}, u32[]{:S(2)}, u32[]{:S(2)}) collective-permute-start(f32[3,8,128]{2,1,0:T(8,128)S(1)} %get-tuple-element.76), channel_id=1, source_target_pairs={{0,24},{32,56},{128,152},{160,184},{256,280},{288,312},{384,408},{... | collective-permute-start | bytes 36872 | tf_op jit(solution)/shard_map/ppermute | solution.py:536
  39.0 2.2 %collective-permute-done.4 = f32[3,8,128]{2,1,0:T(8,128)S(1)} collective-permute-done((f32[3,8,128]{2,1,0:T(8,128)S(1)}, f32[3,8,128]{2,1,0:T(8,128)S(1)}, u32[]{:S(2)}, u32[]{:S(2)}) %collective-permute-start.4) | collective-permute-done | bytes 12320 | tf_op jit(solution)/shard_map/ppermute | solution.py:536
  41.3 2.4 %collective-permute-start.6 = (f32[9,8,128]{2,1,0:T(8,128)S(1)}, f32[9,8,128]{2,1,0:T(8,128)S(1)}, u32[]{:S(2)}, u32[]{:S(2)}) collective-permute-start(f32[9,8,128]{2,1,0:T(8,128)S(1)} %constant_dynamic-update-slice_fusion.mid), channel_id=1, source_target_pairs={{0,416},{32,0},{128,32},{160,128},{256,160},{288,256},{384,288},{4... | collective-permute-start | bytes 110600 | tf_op jit(solution)/shard_map/ppermute | solution.py:536
  43.7 1.5 collective-permute-done.6.high
  45.2 1.5 shard_map.134
  46.8 3.7 %collective-permute-start.7 = (bf16[16,512]{1,0:T(8,128)(2,1)S(1)}, bf16[16,512]{1,0:T(8,128)(2,1)S(1)}, u32[]{:S(2)}, u32[]{:S(2)}) collective-permute-start(bf16[16,512]{1,0:T(8,128)(2,1)S(1)} %get-tuple-element.91), channel_id=1, source_target_pairs={{0,1},{32,33},{128,129},{160,161},{256,257},{288,289},{384,385},{4... | collective-permute-start | bytes 49160 | tf_op jit(solution)/shard_map/ppermute | solution.py:536
  50.5 2.8 %collective-permute-start.8 = (bf16[16,512]{1,0:T(8,128)(2,1)S(1)}, bf16[16,512]{1,0:T(8,128)(2,1)S(1)}, u32[]{:S(2)}, u32[]{:S(2)}) collective-permute-start(bf16[16,512]{1,0:T(8,128)(2,1)S(1)} %get-tuple-element.91), channel_id=1, source_target_pairs={{0,71},{32,103},{128,199},{160,231},{256,327},{288,359},{384,455},... | collective-permute-start | bytes 49160 | tf_op jit(solution)/shard_map/ppermute | solution.py:536
  53.3 1.6 %collective-permute-done.8 = bf16[16,512]{1,0:T(8,128)(2,1)S(1)} collective-permute-done((bf16[16,512]{1,0:T(8,128)(2,1)S(1)}, bf16[16,512]{1,0:T(8,128)(2,1)S(1)}, u32[]{:S(2)}, u32[]{:S(2)}) %collective-permute-start.8) | collective-permute-done | bytes 16416 | tf_op jit(solution)/shard_map/ppermute | solution.py:536
  55.0 2.0 %collective-permute-start.9 = (bf16[48,512]{1,0:T(8,128)(2,1)S(1)}, bf16[48,512]{1,0:T(8,128)(2,1)S(1)}, u32[]{:S(2)}, u32[]{:S(2)}) collective-permute-start(bf16[48,512]{1,0:T(8,128)(2,1)S(1)} %constant_dynamic-update-slice_fusion.3), channel_id=1, source_target_pairs={{0,8},{32,40},{128,136},{160,168},{256,264},{288,296},{384,392},{4... | collective-permute-start | bytes 147464 | tf_op jit(solution)/shard_map/ppermute | solution.py:536
  57.0 3.3 %collective-permute-start.10 = (bf16[48,512]{1,0:T(8,128)(2,1)S(1)}, bf16[48,512]{1,0:T(8,128)(2,1)S(1)}, u32[]{:S(2)}, u32[]{:S(2)}) collective-permute-start(bf16[48,512]{1,0:T(8,128)(2,1)S(1)} %constant_dynamic-update-slice_fusion.3), channel_id=1, source_target_pairs={{0,24},{32,56},{128,152},{160,184},{256,280},{288,312},{384,408},{... | collective-permute-start | bytes 147464 | tf_op jit(solution)/shard_map/ppermute | solution.py:536
  60.3 2.7 %collective-permute-done.10 = bf16[48,512]{1,0:T(8,128)(2,1)S(1)} collective-permute-done((bf16[48,512]{1,0:T(8,128)(2,1)S(1)}, bf16[48,512]{1,0:T(8,128)(2,1)S(1)}, u32[]{:S(2)}, u32[]{:S(2)}) %collective-permute-start.10) | collective-permute-done | bytes 49184 | tf_op jit(solution)/shard_map/ppermute | solution.py:536
  63.0 5.0 %collective-permute-start.12 = (bf16[144,512]{1,0:T(8,128)(2,1)S(1)}, bf16[144,512]{1,0:T(8,128)(2,1)S(1)}, u32[]{:S(2)}, u32[]{:S(2)}) collective-permute-start(bf16[144,512]{1,0:T(8,128)(2,1)S(1)} %constant_dynamic-update-slice_fusion.6.mid), channel_id=1, source_target_pairs={{0,416},{32,0},{128,32},{160,128},{256,160},{288,256},{384,288},{4... | collective-permute-start | bytes 442376 | tf_op jit(solution)/shard_map/ppermute | solution.py:536
  68.0 3.1 %collective-permute-done.12.high = bf16[144,512]{1,0:T(8,128)(2,1)S(1)} collective-permute-done((bf16[144,512]{1,0:T(8,128)(2,1)S(1)}, bf16[144,512]{1,0:T(8,128)(2,1)S(1)}, u32[]{:S(2)}, u32[]{:S(2)}) %collective-permute-start.12) | collective-permute-done | bytes 147488 | tf_op jit(solution)/shard_map/ppermute | solution.py:536
  71.2 9.5 %shard_map.135 = (f32[64,512]{1,0:T(8,128)S(1)}, bf16[144,512]{1,0:T(8,128)(2,1)S(1)}, bf16[144,512]{1,0:T(8,128)(2,1)S(1)}, bf16[144,512]{1,0:T(8,128)(2,1)S(1)...) custom-call(s32[1,128]{1,0:T(1,128)S(1)} %get-tuple-element.74.count_ref, f32[8,2048]{1,0:T(8,128)S(1)} %get-tuple-element.86.facts_ref, ...), custom_call_target="tpu_custom_call" | custom-call | tf_op jit(solution)/shard_map/pallas_call | solution.py:496
  80.6 1.5 collective-permute-start.13
  82.1 2.1 %collective-permute-done.13 = bf16[144,512]{1,0:T(8,128)(2,1)S(1)} collective-permute-done((bf16[144,512]{1,0:T(8,128)(2,1)S(1)}, bf16[144,512]{1,0:T(8,128)(2,1)S(1)}, u32[]{:S(2)}, u32[]{:S(2)}) %collective-permute-start.13) | collective-permute-done | bytes 147488 | tf_op jit(solution)/shard_map/ppermute | solution.py:536
  84.2 3.0 %collective-permute-done.14 = bf16[144,512]{1,0:T(8,128)(2,1)S(1)} collective-permute-done((bf16[144,512]{1,0:T(8,128)(2,1)S(1)}, bf16[144,512]{1,0:T(8,128)(2,1)S(1)}, u32[]{:S(2)}, u32[]{:S(2)}) %collective-permute-start.14) | collective-permute-done | bytes 147488 | tf_op jit(solution)/shard_map/ppermute | solution.py:536
  87.3 2.1 %collective-permute-start.15 = (bf16[48,512]{1,0:T(8,128)(2,1)S(1)}, bf16[48,512]{1,0:T(8,128)(2,1)S(1)}, u32[]{:S(2)}, u32[]{:S(2)}) collective-permute-start(bf16[48,512]{1,0:T(8,128)(2,1)S(1)} %get-tuple-element.114), channel_id=1, source_target_pairs={{0,8},{32,40},{128,136},{160,168},{256,264},{288,296},{384,392},{4... | collective-permute-start | bytes 147464 | tf_op jit(solution)/shard_map/ppermute | solution.py:536
  89.4 3.3 %collective-permute-start.16 = (bf16[48,512]{1,0:T(8,128)(2,1)S(1)}, bf16[48,512]{1,0:T(8,128)(2,1)S(1)}, u32[]{:S(2)}, u32[]{:S(2)}) collective-permute-start(bf16[48,512]{1,0:T(8,128)(2,1)S(1)} %get-tuple-element.115), channel_id=1, source_target_pairs={{0,24},{32,56},{128,152},{160,184},{256,280},{288,312},{384,408},{... | collective-permute-start | bytes 147464 | tf_op jit(solution)/shard_map/ppermute | solution.py:536
  92.9 3.1 %collective-permute-done.16 = bf16[48,512]{1,0:T(8,128)(2,1)S(1)} collective-permute-done((bf16[48,512]{1,0:T(8,128)(2,1)S(1)}, bf16[48,512]{1,0:T(8,128)(2,1)S(1)}, u32[]{:S(2)}, u32[]{:S(2)}) %collective-permute-start.16) | collective-permute-done | bytes 49184 | tf_op jit(solution)/shard_map/ppermute | solution.py:536
  96.0 1.9 %collective-permute-start.17 = (bf16[16,512]{1,0:T(8,128)(2,1)S(1)}, bf16[16,512]{1,0:T(8,128)(2,1)S(1)}, u32[]{:S(2)}, u32[]{:S(2)}) collective-permute-start(bf16[16,512]{1,0:T(8,128)(2,1)S(1)} %get-tuple-element.116), channel_id=1, source_target_pairs={{0,1},{32,33},{128,129},{160,161},{256,257},{288,289},{384,385},{4... | collective-permute-start | bytes 49160 | tf_op jit(solution)/shard_map/ppermute | solution.py:536
  98.0 5.3 %collective-permute-start.18 = (bf16[16,512]{1,0:T(8,128)(2,1)S(1)}, bf16[16,512]{1,0:T(8,128)(2,1)S(1)}, u32[]{:S(2)}, u32[]{:S(2)}) collective-permute-start(bf16[16,512]{1,0:T(8,128)(2,1)S(1)} %get-tuple-element.117), channel_id=1, source_target_pairs={{0,71},{32,103},{128,199},{160,231},{256,327},{288,359},{384,455},... | collective-permute-start | bytes 49160 | tf_op jit(solution)/shard_map/ppermute | solution.py:536
  103.3 0.7 collective-permute-done.18
  104.0 3.0 %shard_map.136 = (f32[8,128]{1,0:T(8,128)S(1)}, f32[9,8,128]{2,1,0:T(8,128)S(1)}, f32[9,8,128]{2,1,0:T(8,128)S(1)}, f32[9,8,128]{2,1,0:T(8,128)S(1)}) custom-call(s32[1,128]{1,0:T(1,128)S(1)} %get-tuple-element.74.count_ref, f32[8,2048]{1,0:T(8,128)S(1)} %get-tuple-element.86.facts_ref, bf16[8,2048]{1,0:T(8,128)(2,1)S(1)} %get-tuple-element.87.basis, ...), custom_call_target="tpu_custom_call" | custom-call | tf_op jit(solution)/shard_map/pallas_call | solution.py:496
  107.0 2.7 %collective-permute-start.19 = (f32[9,8,128]{2,1,0:T(8,128)S(1)}, f32[9,8,128]{2,1,0:T(8,128)S(1)}, u32[]{:S(2)}, u32[]{:S(2)}) collective-permute-start(f32[9,8,128]{2,1,0:T(8,128)S(1)} %get-tuple-element.109), channel_id=1, source_target_pairs={{0,32},{32,128},{128,160},{160,256},{256,288},{288,384},{384,416},... | collective-permute-start | bytes 110600 | tf_op jit(solution)/shard_map/ppermute | solution.py:536
  109.7 1.1 collective-permute-done.19
  110.8 3.2 %collective-permute-done.20 = f32[9,8,128]{2,1,0:T(8,128)S(1)} collective-permute-done((f32[9,8,128]{2,1,0:T(8,128)S(1)}, f32[9,8,128]{2,1,0:T(8,128)S(1)}, u32[]{:S(2)}, u32[]{:S(2)}) %collective-permute-start.20) | collective-permute-done | bytes 36896 | tf_op jit(solution)/shard_map/ppermute | solution.py:536
  114.0 1.9 %collective-permute-start.21 = (f32[3,8,128]{2,1,0:T(8,128)S(1)}, f32[3,8,128]{2,1,0:T(8,128)S(1)}, u32[]{:S(2)}, u32[]{:S(2)}) collective-permute-start(f32[3,8,128]{2,1,0:T(8,128)S(1)} %get-tuple-element.118), channel_id=1, source_target_pairs={{0,8},{32,40},{128,136},{160,168},{256,264},{288,296},{384,392},{4... | collective-permute-start | bytes 36872 | tf_op jit(solution)/shard_map/ppermute | solution.py:536
  115.9 3.4 %collective-permute-start.22 = (f32[3,8,128]{2,1,0:T(8,128)S(1)}, f32[3,8,128]{2,1,0:T(8,128)S(1)}, u32[]{:S(2)}, u32[]{:S(2)}) collective-permute-start(f32[3,8,128]{2,1,0:T(8,128)S(1)} %get-tuple-element.119), channel_id=1, source_target_pairs={{0,24},{32,56},{128,152},{160,184},{256,280},{288,312},{384,408},{... | collective-permute-start | bytes 36872 | tf_op jit(solution)/shard_map/ppermute | solution.py:536
  119.3 2.3 %collective-permute-done.22 = f32[3,8,128]{2,1,0:T(8,128)S(1)} collective-permute-done((f32[3,8,128]{2,1,0:T(8,128)S(1)}, f32[3,8,128]{2,1,0:T(8,128)S(1)}, u32[]{:S(2)}, u32[]{:S(2)}) %collective-permute-start.22) | collective-permute-done | bytes 12320 | tf_op jit(solution)/shard_map/ppermute | solution.py:536
  121.6 13.0 %collective-permute-start.23 = (f32[16,128]{1,0:T(8,128)S(1)}, f32[16,128]{1,0:T(8,128)S(1)}, u32[]{:S(2)}, u32[]{:S(2)}) collective-permute-start(f32[16,128]{1,0:T(8,128)S(1)} %pad_maximum_fusion), channel_id=1, source_target_pairs={{0,0},{32,1},{128,2},{160,3},{256,4},{288,5},{384,6},{416,7},{8,8}... | collective-permute-start | bytes 24584 | tf_op jit(solution)/shard_map/ppermute | solution.py:658
  134.6 6.1 %collective-permute-start.25 = (f32[8,128]{1,0:T(8,128)S(1)}, f32[8,128]{1,0:T(8,128)S(1)}, u32[]{:S(2)}, u32[]{:S(2)}) collective-permute-start(f32[8,128]{1,0:T(8,128)S(1)} %get-tuple-element.120), channel_id=1, source_target_pairs={{0,480},{32,481},{128,482},{160,483},{256,484},{288,485},{384,486}... | collective-permute-start | bytes 12296 | tf_op jit(solution)/shard_map/ppermute | solution.py:660
  140.7 1.9 %collective-permute-start.24 = (f32[8,128]{1,0:T(8,128)S(1)}, f32[8,128]{1,0:T(8,128)S(1)}, u32[]{:S(2)}, u32[]{:S(2)}) collective-permute-start(f32[8,128]{1,0:T(8,128)S(1)} %get-tuple-element.121), channel_id=1, source_target_pairs={{0,32},{32,33},{128,34},{160,35},{256,36},{288,37},{384,38},{416,3... | collective-permute-start | bytes 12296 | tf_op jit(solution)/shard_map/ppermute | solution.py:659
  142.6 6.2 %collective-permute-done.25.from_high = f32[8,128]{1,0:T(8,128)S(1)} collective-permute-done((f32[8,128]{1,0:T(8,128)S(1)}, f32[8,128]{1,0:T(8,128)S(1)}, u32[]{:S(2)}, u32[]{:S(2)}) %collective-permute-start.25) | collective-permute-done | bytes 4128 | tf_op jit(solution)/shard_map/ppermute | solution.py:660
  148.8 7.9 %collective-permute-done.24.from_low = f32[8,128]{1,0:T(8,128)S(1)} collective-permute-done((f32[8,128]{1,0:T(8,128)S(1)}, f32[8,128]{1,0:T(8,128)S(1)}, u32[]{:S(2)}, u32[]{:S(2)}) %collective-permute-start.24) | collective-permute-done | bytes 4128 | tf_op jit(solution)/shard_map/ppermute | solution.py:659
  156.7 0.7 shard_map.137
  (60 shorter events, 1.4 us)
Async XLA Ops:
  0.6 0.7 copy-start.8
  1.3 0.7 copy-start.10
  1.3 0.7 copy-start.11
  2.0 0.7 copy-start.7
  2.7 20.6 %copy-start.6 = (bf16[2,8,64]{2,1,0:T(8,128)(2,1)S(1)}, bf16[2,8,64]{2,1,0:T(8,128)(2,1)}, u32[]{:S(2)}) copy-start(bf16[2,8,64]{2,1,0:T(8,128)(2,1)} %win.1) | copy-start | bytes 6148
  3.3 19.9 %copy-start.13 = (bf16[7,128]{1,0:T(8,128)(2,1)S(1)}, bf16[7,128]{1,0:T(8,128)(2,1)}, u32[]{:S(2)}) copy-start(bf16[7,128]{1,0:T(8,128)(2,1)} %embedding.1) | copy-start | bytes 5380
  3.3 20.0 %copy-start.9 = (f32[2,128]{1,0:T(2,128)S(1)}, f32[2,128]{1,0:T(2,128)}, u32[]{:S(2)}) copy-start(f32[2,128]{1,0:T(2,128)} %read) | copy-start | bytes 3076
  3.3 24.2 %collective-permute-start.2 = (f32[8,128]{1,0:T(8,128)S(1)}, f32[8,128]{1,0:T(8,128)S(1)}, u32[]{:S(2)}, u32[]{:S(2)}) collective-permute-start(f32[8,128]{1,0:T(8,128)S(1)} %get-tuple-element.60), channel_id=1, source_target_pairs={{0,71},{1,103},{2,199},{3,231},{4,327},{5,359},{6,455},{7,487},{8,... | collective-permute-start | bytes 12296 | tf_op jit(solution)/shard_map/ppermute | solution.py:587
  19.4 8.3 %collective-permute-start.1 = (f32[8,128]{1,0:T(8,128)S(1)}, f32[8,128]{1,0:T(8,128)S(1)}, u32[]{:S(2)}, u32[]{:S(2)}) collective-permute-start(f32[8,128]{1,0:T(8,128)S(1)} %get-tuple-element.60), channel_id=1, source_target_pairs={{0,1},{1,33},{2,129},{3,161},{4,257},{5,289},{6,385},{7,417},{8,9}... | collective-permute-start | bytes 12296 | tf_op jit(solution)/shard_map/ppermute | solution.py:586
  21.3 12.3 %collective-permute-start = (f32[24,128]{1,0:T(8,128)S(1)}, f32[24,128]{1,0:T(8,128)S(1)}, u32[]{:S(2)}, u32[]{:S(2)}) collective-permute-start(f32[24,128]{1,0:T(8,128)S(1)} %get-tuple-element.59), channel_id=1, source_target_pairs={{0,0},{1,32},{2,128},{3,160},{4,256},{5,288},{6,384},{7,416},{8,8}... | collective-permute-start | bytes 36872 | tf_op jit(solution)/shard_map/ppermute | solution.py:585
  23.3 0.9 copy-start
  24.2 0.8 copy-start.2
  25.1 0.8 copy-start.4
  25.8 0.9 copy-start.12
  33.7 5.3 %collective-permute-start.3 = (f32[3,8,128]{2,1,0:T(8,128)S(1)}, f32[3,8,128]{2,1,0:T(8,128)S(1)}, u32[]{:S(2)}, u32[]{:S(2)}) collective-permute-start(f32[3,8,128]{2,1,0:T(8,128)S(1)} %get-tuple-element.76), channel_id=1, source_target_pairs={{0,8},{32,40},{128,136},{160,168},{256,264},{288,296},{384,392},{4... | collective-permute-start | bytes 36872 | tf_op jit(solution)/shard_map/ppermute | solution.py:536
  35.6 5.7 %collective-permute-start.4 = (f32[3,8,128]{2,1,0:T(8,128)S(1)}, f32[3,8,128]{2,1,0:T(8,128)S(1)}, u32[]{:S(2)}, u32[]{:S(2)}) collective-permute-start(f32[3,8,128]{2,1,0:T(8,128)S(1)} %get-tuple-element.76), channel_id=1, source_target_pairs={{0,24},{32,56},{128,152},{160,184},{256,280},{288,312},{384,408},{... | collective-permute-start | bytes 36872 | tf_op jit(solution)/shard_map/ppermute | solution.py:536
  41.3 4.0 %collective-permute-start.6 = (f32[9,8,128]{2,1,0:T(8,128)S(1)}, f32[9,8,128]{2,1,0:T(8,128)S(1)}, u32[]{:S(2)}, u32[]{:S(2)}) collective-permute-start(f32[9,8,128]{2,1,0:T(8,128)S(1)} %constant_dynamic-update-slice_fusion.mid), channel_id=1, source_target_pairs={{0,416},{32,0},{128,32},{160,128},{256,160},{288,256},{384,288},{4... | collective-permute-start | bytes 110600 | tf_op jit(solution)/shard_map/ppermute | solution.py:536
  43.7 1.6 collective-permute-start.5
  46.8 6.5 %collective-permute-start.7 = (bf16[16,512]{1,0:T(8,128)(2,1)S(1)}, bf16[16,512]{1,0:T(8,128)(2,1)S(1)}, u32[]{:S(2)}, u32[]{:S(2)}) collective-permute-start(bf16[16,512]{1,0:T(8,128)(2,1)S(1)} %get-tuple-element.91), channel_id=1, source_target_pairs={{0,1},{32,33},{128,129},{160,161},{256,257},{288,289},{384,385},{4... | collective-permute-start | bytes 49160 | tf_op jit(solution)/shard_map/ppermute | solution.py:536
  50.5 4.5 %collective-permute-start.8 = (bf16[16,512]{1,0:T(8,128)(2,1)S(1)}, bf16[16,512]{1,0:T(8,128)(2,1)S(1)}, u32[]{:S(2)}, u32[]{:S(2)}) collective-permute-start(bf16[16,512]{1,0:T(8,128)(2,1)S(1)} %get-tuple-element.91), channel_id=1, source_target_pairs={{0,71},{32,103},{128,199},{160,231},{256,327},{288,359},{384,455},... | collective-permute-start | bytes 49160 | tf_op jit(solution)/shard_map/ppermute | solution.py:536
  55.0 5.3 %collective-permute-start.9 = (bf16[48,512]{1,0:T(8,128)(2,1)S(1)}, bf16[48,512]{1,0:T(8,128)(2,1)S(1)}, u32[]{:S(2)}, u32[]{:S(2)}) collective-permute-start(bf16[48,512]{1,0:T(8,128)(2,1)S(1)} %constant_dynamic-update-slice_fusion.3), channel_id=1, source_target_pairs={{0,8},{32,40},{128,136},{160,168},{256,264},{288,296},{384,392},{4... | collective-permute-start | bytes 147464 | tf_op jit(solution)/shard_map/ppermute | solution.py:536
  57.0 6.0 %collective-permute-start.10 = (bf16[48,512]{1,0:T(8,128)(2,1)S(1)}, bf16[48,512]{1,0:T(8,128)(2,1)S(1)}, u32[]{:S(2)}, u32[]{:S(2)}) collective-permute-start(bf16[48,512]{1,0:T(8,128)(2,1)S(1)} %constant_dynamic-update-slice_fusion.3), channel_id=1, source_target_pairs={{0,24},{32,56},{128,152},{160,184},{256,280},{288,312},{384,408},{... | collective-permute-start | bytes 147464 | tf_op jit(solution)/shard_map/ppermute | solution.py:536
  60.3 10.9 %copy-start.3 = (bf16[64,512]{1,0:T(8,128)(2,1)S(1)}, bf16[64,512]{1,0:T(8,128)(2,1)}, u32[]{:S(2)}) copy-start(bf16[64,512]{1,0:T(8,128)(2,1)} %wout) | copy-start | bytes 196612
  63.0 8.2 %collective-permute-start.12 = (bf16[144,512]{1,0:T(8,128)(2,1)S(1)}, bf16[144,512]{1,0:T(8,128)(2,1)S(1)}, u32[]{:S(2)}, u32[]{:S(2)}) collective-permute-start(bf16[144,512]{1,0:T(8,128)(2,1)S(1)} %constant_dynamic-update-slice_fusion.6.mid), channel_id=1, source_target_pairs={{0,416},{32,0},{128,32},{160,128},{256,160},{288,256},{384,288},{4... | collective-permute-start | bytes 442376 | tf_op jit(solution)/shard_map/ppermute | solution.py:536
  68.0 3.1 %collective-permute-start.11 = (bf16[144,512]{1,0:T(8,128)(2,1)S(1)}, bf16[144,512]{1,0:T(8,128)(2,1)S(1)}, u32[]{:S(2)}, u32[]{:S(2)}) collective-permute-start(bf16[144,512]{1,0:T(8,128)(2,1)S(1)} %constant_dynamic-update-slice_fusion.6.mid), channel_id=1, source_target_pairs={{0,32},{32,128},{128,160},{160,256},{256,288},{288,384},{384,416},... | collective-permute-start | bytes 442376 | tf_op jit(solution)/shard_map/ppermute | solution.py:536
  80.6 3.6 %collective-permute-start.13 = (bf16[144,512]{1,0:T(8,128)(2,1)S(1)}, bf16[144,512]{1,0:T(8,128)(2,1)S(1)}, u32[]{:S(2)}, u32[]{:S(2)}) collective-permute-start(bf16[144,512]{1,0:T(8,128)(2,1)S(1)} %get-tuple-element.100), channel_id=1, source_target_pairs={{0,32},{32,128},{128,160},{160,256},{256,288},{288,384},{384,416},... | collective-permute-start | bytes 442376 | tf_op jit(solution)/shard_map/ppermute | solution.py:536
  82.1 5.1 %collective-permute-start.14 = (bf16[144,512]{1,0:T(8,128)(2,1)S(1)}, bf16[144,512]{1,0:T(8,128)(2,1)S(1)}, u32[]{:S(2)}, u32[]{:S(2)}) collective-permute-start(bf16[144,512]{1,0:T(8,128)(2,1)S(1)} %get-tuple-element.101), channel_id=1, source_target_pairs={{0,416},{32,0},{128,32},{160,128},{256,160},{288,256},{384,288},{4... | collective-permute-start | bytes 442376 | tf_op jit(solution)/shard_map/ppermute | solution.py:536
  87.2 16.7 %copy-start.1 = (bf16[6,128,128]{2,1,0:T(8,128)(2,1)S(1)}, bf16[6,128,128]{2,1,0:T(8,128)(2,1)}, u32[]{:S(2)}) copy-start(bf16[6,128,128]{2,1,0:T(8,128)(2,1)} %mix_one.2) | copy-start | bytes 589828
  87.3 5.6 %collective-permute-start.15 = (bf16[48,512]{1,0:T(8,128)(2,1)S(1)}, bf16[48,512]{1,0:T(8,128)(2,1)S(1)}, u32[]{:S(2)}, u32[]{:S(2)}) collective-permute-start(bf16[48,512]{1,0:T(8,128)(2,1)S(1)} %get-tuple-element.114), channel_id=1, source_target_pairs={{0,8},{32,40},{128,136},{160,168},{256,264},{288,296},{384,392},{4... | collective-permute-start | bytes 147464 | tf_op jit(solution)/shard_map/ppermute | solution.py:536
  89.4 6.6 %collective-permute-start.16 = (bf16[48,512]{1,0:T(8,128)(2,1)S(1)}, bf16[48,512]{1,0:T(8,128)(2,1)S(1)}, u32[]{:S(2)}, u32[]{:S(2)}) collective-permute-start(bf16[48,512]{1,0:T(8,128)(2,1)S(1)} %get-tuple-element.115), channel_id=1, source_target_pairs={{0,24},{32,56},{128,152},{160,184},{256,280},{288,312},{384,408},{... | collective-permute-start | bytes 147464 | tf_op jit(solution)/shard_map/ppermute | solution.py:536
  96.0 7.2 %collective-permute-start.17 = (bf16[16,512]{1,0:T(8,128)(2,1)S(1)}, bf16[16,512]{1,0:T(8,128)(2,1)S(1)}, u32[]{:S(2)}, u32[]{:S(2)}) collective-permute-start(bf16[16,512]{1,0:T(8,128)(2,1)S(1)} %get-tuple-element.116), channel_id=1, source_target_pairs={{0,1},{32,33},{128,129},{160,161},{256,257},{288,289},{384,385},{4... | collective-permute-start | bytes 49160 | tf_op jit(solution)/shard_map/ppermute | solution.py:536
  98.0 6.0 %copy-start.5 = (bf16[64,256]{1,0:T(8,128)(2,1)S(1)}, bf16[64,256]{1,0:T(8,128)(2,1)}, u32[]{:S(2)}) copy-start(bf16[64,256]{1,0:T(8,128)(2,1)} %wout.1) | copy-start | bytes 98308
  98.0 6.0 %collective-permute-start.18 = (bf16[16,512]{1,0:T(8,128)(2,1)S(1)}, bf16[16,512]{1,0:T(8,128)(2,1)S(1)}, u32[]{:S(2)}, u32[]{:S(2)}) collective-permute-start(bf16[16,512]{1,0:T(8,128)(2,1)S(1)} %get-tuple-element.117), channel_id=1, source_target_pairs={{0,71},{32,103},{128,199},{160,231},{256,327},{288,359},{384,455},... | collective-permute-start | bytes 49160 | tf_op jit(solution)/shard_map/ppermute | solution.py:536
  107.0 3.8 %collective-permute-start.19 = (f32[9,8,128]{2,1,0:T(8,128)S(1)}, f32[9,8,128]{2,1,0:T(8,128)S(1)}, u32[]{:S(2)}, u32[]{:S(2)}) collective-permute-start(f32[9,8,128]{2,1,0:T(8,128)S(1)} %get-tuple-element.109), channel_id=1, source_target_pairs={{0,32},{32,128},{128,160},{160,256},{256,288},{288,384},{384,416},... | collective-permute-start | bytes 110600 | tf_op jit(solution)/shard_map/ppermute | solution.py:536
  109.7 4.3 %collective-permute-start.20 = (f32[9,8,128]{2,1,0:T(8,128)S(1)}, f32[9,8,128]{2,1,0:T(8,128)S(1)}, u32[]{:S(2)}, u32[]{:S(2)}) collective-permute-start(f32[9,8,128]{2,1,0:T(8,128)S(1)} %get-tuple-element.110), channel_id=1, source_target_pairs={{0,416},{32,0},{128,32},{160,128},{256,160},{288,256},{384,288},{4... | collective-permute-start | bytes 110600 | tf_op jit(solution)/shard_map/ppermute | solution.py:536
  114.0 5.3 %collective-permute-start.21 = (f32[3,8,128]{2,1,0:T(8,128)S(1)}, f32[3,8,128]{2,1,0:T(8,128)S(1)}, u32[]{:S(2)}, u32[]{:S(2)}) collective-permute-start(f32[3,8,128]{2,1,0:T(8,128)S(1)} %get-tuple-element.118), channel_id=1, source_target_pairs={{0,8},{32,40},{128,136},{160,168},{256,264},{288,296},{384,392},{4... | collective-permute-start | bytes 36872 | tf_op jit(solution)/shard_map/ppermute | solution.py:536
  115.9 5.7 %collective-permute-start.22 = (f32[3,8,128]{2,1,0:T(8,128)S(1)}, f32[3,8,128]{2,1,0:T(8,128)S(1)}, u32[]{:S(2)}, u32[]{:S(2)}) collective-permute-start(f32[3,8,128]{2,1,0:T(8,128)S(1)} %get-tuple-element.119), channel_id=1, source_target_pairs={{0,24},{32,56},{128,152},{160,184},{256,280},{288,312},{384,408},{... | collective-permute-start | bytes 36872 | tf_op jit(solution)/shard_map/ppermute | solution.py:536
  121.6 35.1 %collective-permute-start.23 = (f32[16,128]{1,0:T(8,128)S(1)}, f32[16,128]{1,0:T(8,128)S(1)}, u32[]{:S(2)}, u32[]{:S(2)}) collective-permute-start(f32[16,128]{1,0:T(8,128)S(1)} %pad_maximum_fusion), channel_id=1, source_target_pairs={{0,0},{32,1},{128,2},{160,3},{256,4},{288,5},{384,6},{416,7},{8,8}... | collective-permute-start | bytes 24584 | tf_op jit(solution)/shard_map/ppermute | solution.py:658
  134.6 14.2 %collective-permute-start.25 = (f32[8,128]{1,0:T(8,128)S(1)}, f32[8,128]{1,0:T(8,128)S(1)}, u32[]{:S(2)}, u32[]{:S(2)}) collective-permute-start(f32[8,128]{1,0:T(8,128)S(1)} %get-tuple-element.120), channel_id=1, source_target_pairs={{0,480},{32,481},{128,482},{160,483},{256,484},{288,485},{384,486}... | collective-permute-start | bytes 12296 | tf_op jit(solution)/shard_map/ppermute | solution.py:660
  140.7 16.0 %collective-permute-start.24 = (f32[8,128]{1,0:T(8,128)S(1)}, f32[8,128]{1,0:T(8,128)S(1)}, u32[]{:S(2)}, u32[]{:S(2)}) collective-permute-start(f32[8,128]{1,0:T(8,128)S(1)} %get-tuple-element.121), channel_id=1, source_target_pairs={{0,32},{32,33},{128,34},{160,35},{256,36},{288,37},{384,38},{416,3... | collective-permute-start | bytes 12296 | tf_op jit(solution)/shard_map/ppermute | solution.py:659

commit v4 on v3

--- a/solution.py
+++ b/solution.py
@@ -168,10 +168,32 @@
     return dot_nt(eye, matrix).astype(BF16)
 
 
+def fetch(pairs, semaphores):
+    copies = [pltpu.make_async_copy(there, here, semaphores.at[k]) for k, (there, here) in enumerate(pairs)]
+    for copy in copies:
+        copy.start()
+    for copy in copies:
+        copy.wait()
+
+
 def weights_kernel(
-    embedding, radial_in, radial_out_one, radial_out_two, mix_one, mix_two, readout,
+    embedding_far, radial_in_far, radial_out_one_far, radial_out_two_far, mix_one_far, mix_two_far, readout_far,
+    radial_in, radial_out_one, radial_out_two, mix_one, readout,
     emb_t, win_t, one_t, two_t, mix_a, mix_b, mix_two_t, spread, read_t, rests,
+    embedding, mix_two, semaphores,
 ):
+    fetch(
+        (
+            (mix_one_far, mix_one),
+            (mix_two_far, mix_two),
+            (radial_out_two_far, radial_out_two),
+            (radial_out_one_far, radial_out_one),
+            (radial_in_far, radial_in),
+            (embedding_far, embedding),
+            (readout_far, readout),
+        ),
+        semaphores,
+    )
     emb = jnp.concatenate([embedding[...].astype(F32), jnp.zeros((1, C), F32)], axis=0).astype(BF16)
     emb_t[...] = flip(emb)
     for t in range(2):
@@ -200,31 +222,34 @@
     return jnp.where(index < SLOTS, index, SLOTS + turned * EXPORT + (index & (EXPORT - 1))).astype(F32)
 
 
-def pack_kernel(exports, counts, positions, species, neighbours, packed, payload, picked, count):
+def pack_kernel(
+    counts, exports_far, positions_far, species_far, neighbours_far, packed,
+    exports, positions, species, neighbours, semaphores,
+):
+    fetch(
+        (
+            (neighbours_far, neighbours),
+            (positions_far, positions),
+            (species_far, species),
+            (exports_far, exports),
+        ),
+        semaphores,
+    )
     even = renamed(neighbours[pl.ds(0, COLUMNS, stride=2), :])
     odd = renamed(neighbours[pl.ds(1, COLUMNS, stride=2), :])
-    lane = iota((8, LANES), 1) % EXPORT
-    row = iota((EXPORT, LANES), 0)
-    source = jnp.zeros((8, LANES), jnp.int32)
-    pick = jnp.zeros((EXPORT, LANES), jnp.int32)
+    lane = iota((1, LANES), 1) % EXPORT
+    source = jnp.zeros((1, LANES), jnp.int32)
     for e in range(EXPORT):
-        slot = exports[e]
-        source = jnp.where(lane == e, slot, source)
-        pick = jnp.where(row == e, slot, pick)
-    picked[...] = pick
-    count[...] = jnp.full((1, LANES), counts[0], jnp.int32)
+        source = jnp.where(lane == e, exports[e], source)
     packed[...] = jnp.zeros_like(packed)
     packed[0:COLUMNS, :] = jnp.concatenate([even, odd], axis=1)
     packed[COLUMNS : COLUMNS + 3, 0:SLOTS] = positions[...]
     packed[COLUMNS + 3 : COLUMNS + 4, 0:SLOTS] = species[...].astype(F32)
-    packed[COLUMNS + 4 : COLUMNS + 5, :] = source[0:1, :].astype(F32)
+    packed[COLUMNS + 4 : COLUMNS + 5, :] = source.astype(F32)
     packed[COLUMNS + 5 : COLUMNS + 6, :] = jnp.full((1, LANES), counts[0], jnp.int32).astype(F32)
-    whole = packed[COLUMNS : COLUMNS + 8, :]
-    whole = jnp.where(iota((8, LANES), 0) < 4, whole, 0.0)
-    payload[...] = jnp.take_along_axis(whole, source, axis=1)
-
-
-def unpack_kernel(arrived, low, high, own, block, picked, index, count):
+
+
+def unpack_kernel(arrived, own, payload, picked, index, count):
     whole = arrived[COLUMNS : COLUMNS + 8, :]
     whole = jnp.where(iota((8, LANES), 0) < 4, whole, 0.0)
     own[...] = whole
@@ -234,11 +259,32 @@
     pick = jnp.sum(jnp.where(mine, exports, 0.0), axis=1, keepdims=True)
     picked[...] = jnp.broadcast_to(pick, (EXPORT, LANES)).astype(jnp.int32)
     source = jnp.broadcast_to(exports, (8, LANES)).astype(jnp.int32)
-    block[0] = low[...]
-    block[1] = jnp.take_along_axis(whole, source, axis=1)
-    block[2] = high[...]
+    payload[0] = jnp.take_along_axis(whole, source, axis=1)
     for m in range(COLUMNS):
         index[:, m * LANES : (m + 1) * LANES] = arrived[m : m + 1, :].astype(jnp.int32)
+
+
+def side_kernel(
+    facts_ref, basis, index, win_t, one_t, spread,
+    onehot, before_one, gate_one, before_two, gate_two, source, slanted,
+):
+    ids = index[...]
+    entry = iota((TABLE, LANES), 0)
+    for m in range(COLUMNS):
+        onehot[:, m * LANES : (m + 1) * LANES] = (entry == column(ids, m)).astype(F32).astype(BF16)
+    before, gate = hidden_of(win_t[1], basis[...])
+    before_two[...] = before
+    gate_two[...] = gate
+    before, gate = hidden_of(win_t[0], basis[...])
+    before_one[...] = before
+    gate_one[...] = gate
+    hidden = (before * gate).astype(BF16)
+    species = species_of(facts_ref[...])
+    for m in range(COLUMNS):
+        here = slice(m * LANES, (m + 1) * LANES)
+        found = dot_nn(spread[...], column(species, m))
+        source[:, here] = found
+        slanted[:, here] = found * dot_nn(one_t[C : 2 * C, :], column(hidden, m))
 
 
 def first_kernel(
@@ -302,15 +348,15 @@
 
 
 def second_kernel(
-    count_ref, facts_ref, basis, slope, own_rows, low, mid, high, index, win_t, win, wout_t, wout, mix_t, rests, read,
+    count_ref, facts_ref, slope, onehot, before_two, gate_two, own_rows, low, mid, high,
+    win, wout_t, wout, mix_t, rests, read,
     grad_own, grad_low, grad_mid, grad_high, pair_out, energy,
-    feats, turned, onehot, radial, source, grad_radial, grad_source,
+    feats, turned, radial, source, grad_radial, grad_source,
 ):
     count = count_ref[...]
-    ids = index[...]
     facts = facts_ref[...]
     unit, inverse = unit_of(facts), facts[3:4, :]
-    before, gate = hidden_of(win_t[1], basis[...])
+    before, gate = before_two[...], gate_two[...]
     hidden = (before * gate).astype(BF16)
     feats[0:SLOTS, :] = own_rows[...]
     feats[SLOTS : SLOTS + SLAB, :] = low[...]
@@ -320,9 +366,6 @@
     eye = (iota((C, C), 0) == iota((C, C), 1)).astype(F32).astype(BF16)
     for c in range(4):
         turned[c * C : (c + 1) * C, :] = dot_nt(eye, feats[:, c * C : (c + 1) * C]).astype(BF16)
-    entry = iota((TABLE, LANES), 0)
-    for m in range(COLUMNS):
-        onehot[:, m * LANES : (m + 1) * LANES] = (entry == column(ids, m)).astype(F32).astype(BF16)
     units = [[column(unit[x : x + 1], m) for m in range(COLUMNS)] for x in range(3)]
     wide = 2 * LANES
     a0 = jnp.zeros((C, LANES), F32)
@@ -393,21 +436,15 @@
 
 
 def third_kernel(
-    count_ref, facts_ref, basis, slope, sums, grad_own, back, picked, pair_in, index, energy_one, energy_two,
-    win_t, win, wout_t, wout, mix_one, spread, read_t,
+    count_ref, facts_ref, slope, onehot, before_one, gate_one, sources, slanted, sums, grad_own, back, picked,
+    pair_in, energy_one, energy_two, win, wout, mix_one, read_t,
     grad_mine, grad_low, grad_mid, grad_high,
-    onehot, grad_radial,
+    grad_radial,
 ):
     count = count_ref[...]
-    ids = index[...]
     facts = facts_ref[...]
     unit, inverse = unit_of(facts), facts[3:4, :]
-    before, gate = hidden_of(win_t[0], basis[...])
-    hidden = (before * gate).astype(BF16)
-    species = species_of(facts)
-    entry = iota((TABLE, LANES), 0)
-    for m in range(COLUMNS):
-        onehot[:, m * LANES : (m + 1) * LANES] = (entry == column(ids, m)).astype(F32).astype(BF16)
+    before, gate = before_one[...], gate_one[...]
     mine = grad_own[...]
     mine_high = mine.astype(BF16)
     mine_low = (mine - mine_high.astype(F32)).astype(BF16)
@@ -439,8 +476,7 @@
     grad_units = [[], [], []]
     for m in range(COLUMNS):
         here = slice(m * LANES, (m + 1) * LANES)
-        r2 = dot_nn(wout_t[C : 2 * C, :], column(hidden, m))
-        source = dot_nn(spread[...], column(species, m))
+        source = sources[:, here]
         u = [column(unit[x : x + 1], m) for x in range(3)]
         slant = d1[0] * u[0] + d1[1] * u[1] + d1[2] * u[2]
         parts = (d0 * source, slant * source)
@@ -448,7 +484,7 @@
             high_part, low_part = split(parts[k])
             grad_radial[k * C : (k + 1) * C, here] = high_part
             grad_radial[(k + 2) * C : (k + 3) * C, here] = low_part
-        q = r2 * source
+        q = slanted[:, here]
         for x in range(3):
             grad_units[x].append(jnp.sum(q * d1[x], axis=0, keepdims=True))
     grad_unit = stack_rows([jnp.concatenate(g, axis=1) for g in grad_units])
@@ -479,26 +515,31 @@
     return jnp.concatenate([fold(column(values, x)) for x in range(count)], axis=1)
 
 
-def last_kernel(count, main, from_low, from_high, picked, forces, energies):
+def last_kernel(grad_mine, back, picked, out):
     same = iota((EXPORT, LANES), 1) == picked[...]
     entry = jnp.sum(jnp.where(same, iota((EXPORT, LANES), 0), 0), axis=0, keepdims=True)
     hit = jnp.sum(same.astype(F32), axis=0, keepdims=True)
-    back = main[8:16, :] + from_low[...] + from_high[...]
-    came = jnp.take_along_axis(back, jnp.broadcast_to(entry, (8, LANES)), axis=1)
-    total = main[0:8, :] + came * hit
-    forces[...] = -total[0:3, 0:SLOTS]
-    energies[...] = (main[3:4, :] * live_row(count[...]))[:, 0:SLOTS]
-
-
-def call(kernel, outs, specs, scratch=(), limit=None, smem=0, cost=None):
-    in_specs = [pl.BlockSpec(memory_space=pltpu.SMEM)] * smem
-    in_specs += [pl.BlockSpec(memory_space=pltpu.VMEM)] * (len(specs) - smem)
+    came = jnp.take_along_axis(back[...], jnp.broadcast_to(entry, (8, LANES)), axis=1)
+    mine = grad_mine[...]
+    out[...] = jnp.where(iota((8, LANES), 0) == 3, mine, -(mine + came * hit))
+
+
+def finish_kernel(out, forces, energies):
+    forces[...] = out[0:3, 0:SLOTS]
+    energies[...] = out[3:4, 0:SLOTS]
+
+
+def call(kernel, outs, specs, scratch=(), limit=None, far=False, cost=None):
+    spaces = [pltpu.HBM if far else pltpu.VMEM] * len(specs)
+    if far:
+        spaces = [space if v.size > 1 else pltpu.SMEM for space, v in zip(spaces, specs)]
+        specs = [pltpu.with_memory_space_constraint(v, pltpu.HBM) if v.size > 1 else v for v in specs]
     return pl.pallas_call(
         kernel,
         out_shape=[jax.ShapeDtypeStruct(s, t) for s, t in outs],
-        in_specs=in_specs,
+        in_specs=[pl.BlockSpec(memory_space=space) for space in spaces],
         out_specs=[pl.BlockSpec(memory_space=pltpu.VMEM)] * len(outs),
-        scratch_shapes=[pltpu.VMEM(s, t) for s, t in scratch],
+        scratch_shapes=[s if not isinstance(s, tuple) else pltpu.VMEM(*s) for s in scratch],
         compiler_params=pltpu.CompilerParams(vmem_limit_bytes=limit or (16 << 20)),
         cost_estimate=cost,
     )(*specs)
@@ -512,16 +553,12 @@
 
 
 def seat(x, y, z):
-    x, y, z = x % 16, y % 4, z % 8
+    x, y, z = (1 - x) % 16, y % 4, (z + 5) % 8
     return given(z // 2 * 4 + x // 8 * 2 + z % 2, y, x % 8)
 
 
-def move_in(step):
-    return [(given(x, y, z), seat(x + step, y, z)) for x, y, z in DOMAINS]
-
-
-def move_out(step):
-    return [(seat(x, y, z), given((x + step) % 16, y, z)) for x, y, z in DOMAINS]
+MOVE_IN = [(given(*d), seat(*d)) for d in DOMAINS]
+MOVE_OUT = [(there, here) for here, there in MOVE_IN]
 
 
 def moves(step):
@@ -536,16 +573,16 @@
     return lax.ppermute(value, AXES, moves(step))
 
 
-def spread_halo(block, first=0):
-    for axis in range(first, 2):
+def spread_halo(block):
+    for axis in range(2):
         low = send(block, UP[axis])
         high = send(block, DOWN[axis])
         block = jnp.concatenate([low, block, high], axis=0)
     return send(block, UP[2]), block, send(block, DOWN[2])
 
 
-def gather_halo(low, mid, high, last=0):
-    for axis in range(2, last - 1, -1):
+def gather_halo(low, mid, high):
+    for axis in (2, 1, 0):
         from_low = send(high, UP[axis])
         from_high = send(low, DOWN[axis])
         block = mid + from_low + from_high
@@ -559,15 +596,27 @@
     positions, species, counts, neighbours, exports, embedding, radial_in,
     radial_out_one, radial_out_two, mix_one, mix_two, readout,
 ):
-    packed, payload, picked_here, count_here = call(
+    (packed,) = call(
         pack_kernel,
-        [((24, LANES), F32), ((8, LANES), F32), ((EXPORT, LANES), jnp.int32), ((1, LANES), jnp.int32)],
-        [exports, counts, positions, species.reshape(1, SLOTS), neighbours],
-        smem=2,
-    )
-    emb_t, win_t, one_t, two_t, mix_a, mix_b, mix_two_t, spread, read_t, rests = call(
+        [((24, LANES), F32)],
+        [counts, exports, positions, species.reshape(1, SLOTS), neighbours],
+        scratch=[
+            pltpu.SMEM((EXPORT,), jnp.int32),
+            ((3, SLOTS), F32),
+            ((1, SLOTS), jnp.int32),
+            ((DEPTH, SLOTS), jnp.int32),
+            pltpu.SemaphoreType.DMA((4,)),
+        ],
+        far=True,
+    )
+    weights = call(
         weights_kernel,
         [
+            ((2, NB, RH), BF16),
+            ((RH, 2 * C), BF16),
+            ((RH, 4 * C), BF16),
+            ((6, C, C), BF16),
+            ((2, C), F32),
             ((C, 8), BF16),
             ((2, RH, NB), BF16),
             ((2 * C, RH), BF16),
@@ -580,30 +629,28 @@
             ((3 * C, 16), F32),
         ],
         [embedding, radial_in, radial_out_one, radial_out_two, mix_one, mix_two, readout],
+        scratch=[((NSPEC, C), BF16), ((5, C, C), BF16), pltpu.SemaphoreType.DMA((7,))],
+        far=True,
         cost=pl.CostEstimate(flops=200_000_000, bytes_accessed=2_000_000, transcendentals=0),
     )
-    arrived = lax.ppermute(packed, AXES, move_in(0))
-    low = lax.ppermute(payload, AXES, move_in(1))
-    high = lax.ppermute(payload, AXES, move_in(-1))
+    arrived = lax.ppermute(packed, AXES, MOVE_IN)
+    arrived, *weights = lax.optimization_barrier((arrived, *weights))
     (
-        arrived, low, high, emb_t, win_t, one_t, two_t, mix_a, mix_b, mix_two_t, spread, read_t, rests,
         radial_in, radial_out_one, radial_out_two, mix_one, readout,
-    ) = lax.optimization_barrier((
-        arrived, low, high, emb_t, win_t, one_t, two_t, mix_a, mix_b, mix_two_t, spread, read_t, rests,
-        radial_in, radial_out_one, radial_out_two, mix_one, readout,
-    ))
-    own, block, picked, index, count = call(
+        emb_t, win_t, one_t, two_t, mix_a, mix_b, mix_two_t, spread, read_t, rests,
+    ) = weights
+    own, payload, picked, index, count = call(
         unpack_kernel,
         [
             ((8, LANES), F32),
-            ((3, 8, LANES), F32),
+            ((1, 8, LANES), F32),
             ((EXPORT, LANES), jnp.int32),
             ((1, PAIRS), jnp.int32),
             ((1, LANES), jnp.int32),
         ],
-        [arrived, low, high],
-    )
-    low, mid, high = spread_halo(block, 1)
+        [arrived],
+    )
+    low, mid, high = spread_halo(payload)
     facts, basis, slope, own_rows, outgoing, sums, energy_one = call(
         first_kernel,
         [
@@ -617,6 +664,20 @@
         ],
         [count, own, low, mid, high, index, picked, win_t, one_t, mix_a, mix_b, spread, emb_t, read_t],
     )
+    onehot, before_one, gate_one, before_two, gate_two, source, slanted = call(
+        side_kernel,
+        [
+            ((TABLE, PAIRS), BF16),
+            ((RH, PAIRS), F32),
+            ((RH, PAIRS), F32),
+            ((RH, PAIRS), F32),
+            ((RH, PAIRS), F32),
+            ((C, PAIRS), F32),
+            ((C, PAIRS), F32),
+        ],
+        [facts, basis, index, win_t, one_t, spread],
+        cost=pl.CostEstimate(flops=500_000_000, bytes_accessed=6_000_000, transcendentals=0),
+    )
     low, mid, high = spread_halo(outgoing)
     grad_own, grad_low, grad_mid, grad_high, pairs, energy_two = call(
         second_kernel,
@@ -629,40 +690,34 @@
             ((1, LANES), F32),
         ],
         [
-            count, facts, basis, slope, own_rows, low, mid, high, index, win_t, radial_in, two_t,
+            count, facts, slope, onehot, before_two, gate_two, own_rows, low, mid, high, radial_in, two_t,
             radial_out_two, mix_two_t, rests, readout,
         ],
         scratch=[
             ((TABLE, 4 * C), BF16),
             ((4 * C, TABLE), BF16),
-            ((TABLE, PAIRS), BF16),
             ((4 * C, PAIRS), F32),
             ((4 * C, PAIRS), F32),
             ((8 * C, PAIRS), BF16),
             ((4 * C, PAIRS), BF16),
         ],
-        limit=48 << 20,
+        limit=36 << 20,
     )
     back = gather_halo(grad_low, grad_mid, grad_high)
     grad_mine, grad_low, grad_mid, grad_high = call(
         third_kernel,
         [((8, LANES), F32), ((9, 8, LANES), F32), ((9, 8, LANES), F32), ((9, 8, LANES), F32)],
         [
-            count, facts, basis, slope, sums, grad_own, back, picked, pairs, index, energy_one, energy_two,
-            win_t, radial_in, one_t, radial_out_one, mix_one, spread, read_t,
-        ],
-        scratch=[((TABLE, PAIRS), BF16), ((4 * C, PAIRS), BF16)],
-        limit=32 << 20,
-    )
-    block = gather_halo(grad_low, grad_mid, grad_high, 1)
-    main = lax.ppermute(jnp.concatenate([grad_mine, block[1]], axis=0), AXES, move_out(0))
-    from_low = lax.ppermute(block[2], AXES, move_out(1))
-    from_high = lax.ppermute(block[0], AXES, move_out(-1))
-    forces, energies = call(
-        last_kernel,
-        [((3, SLOTS), F32), ((1, SLOTS), F32)],
-        [count_here, main, from_low, from_high, picked_here],
-    )
+            count, facts, slope, onehot, before_one, gate_one, source, slanted, sums, grad_own, back, picked,
+            pairs, energy_one, energy_two, radial_in, radial_out_one, mix_one, read_t,
+        ],
+        scratch=[((4 * C, PAIRS), BF16)],
+        limit=24 << 20,
+    )
+    back = gather_halo(grad_low, grad_mid, grad_high)
+    (out,) = call(last_kernel, [((8, LANES), F32)], [grad_mine, back[0], picked])
+    out = lax.ppermute(out, AXES, MOVE_OUT)
+    forces, energies = call(finish_kernel, [((3, SLOTS), F32), ((1, SLOTS), F32)], [out])
     return forces, energies.reshape(SLOTS)
 
 

time: 158 us -> 141 us (0.89)
  the two profiles are of different devices: /device:TPU:29 before, /device:TPU:8 now
where the time goes in v4:
time: 141 us; the launch traced here: 139 us
  starting transfers between devices  72.3 us (51%)
  waiting for transfers between devices  46 us (33%)
  Pallas kernels  18.5 us (13%)
  between operations  1.69 us (1%)
    ppermute x24, starting transfers between devices, send(): return lax.ppermute(value, AXES, moves(step))  64.7 us
    ppermute x24, waiting for transfers between devices, send(): return lax.ppermute(value, AXES, moves(step))  40.6 us
    pallas_call x9, Pallas kernels, call(): pl.pallas_call(kernel, out_shape=[jax.ShapeDtypeStruct(s, t) for s, t in...  18.5 us
    ppermute x1, starting transfers between devices, body(): arrived = lax.ppermute(packed, AXES, MOVE_IN)  5.73 us
    ppermute x1, waiting for transfers between devices, body(): out = lax.ppermute(out, AXES, MOVE_OUT)  5.4 us
  transfers between devices with their start and end apart: 26, of which 16 were waited for; matrix products, arithmetic and copies ran while one was open for 0% of the time, Pallas kernels for 3%

profile of v4, /device:TPU:8, one launch (start us, length us, event | category | flops | bytes accessed | tf_op | source)
XLA Modules:
  0.0 138.6 jit_solution(16787898234754971065)
XLA Ops:
  1.3 0.9 shard_map.131
  2.2 5.7 %collective-permute-start = (f32[24,128]{1,0:T(8,128)S(1)}, f32[24,128]{1,0:T(8,128)S(1)}, u32[]{:S(2)}, u32[]{:S(2)}) collective-permute-start(f32[24,128]{1,0:T(8,128)S(1)} %shard_map.131), channel_id=1, source_target_pairs={{0,289},{1,385},{2,417},{3,1},{4,33},{5,129},{6,161},{7,257},{8,29... | collective-permute-start | bytes 36872 | tf_op jit(solution)/shard_map/ppermute | solution.py:636
  7.9 1.8 %shard_map.132 = (bf16[2,8,64]{2,1,0:T(8,128)(2,1)S(1)}, bf16[64,256]{1,0:T(8,128)(2,1)S(1)}, bf16[64,512]{1,0:T(8,128)(2,1)S(1)}, bf16[6,128,128]{2,1,0:T(8,128...) custom-call(bf16[7,128]{1,0:T(8,128)(2,1)} %embedding_far.1, ...), custom_call_target="tpu_custom_call" | custom-call | flops 200000000 | bytes 2000000 | tf_op jit(solution)/shard_map/pallas_call | solution.py:537
  9.8 0.1 shard_map.133
  9.9 13.3 %collective-permute-start.1 = (f32[1,8,128]{2,1,0:T(8,128)S(1)}, f32[1,8,128]{2,1,0:T(8,128)S(1)}, u32[]{:S(2)}, u32[]{:S(2)}) collective-permute-start(f32[1,8,128]{2,1,0:T(8,128)S(1)} %get-tuple-element.82), channel_id=1, source_target_pairs={{289,288},{385,384},{417,416},{1,0},{33,32},{129,128},{161,160},{2... | collective-permute-start | bytes 12296 | tf_op jit(solution)/shard_map/ppermute | solution.py:573
  23.2 1.9 %collective-permute-start.2 = (f32[1,8,128]{2,1,0:T(8,128)S(1)}, f32[1,8,128]{2,1,0:T(8,128)S(1)}, u32[]{:S(2)}, u32[]{:S(2)}) collective-permute-start(f32[1,8,128]{2,1,0:T(8,128)S(1)} %get-tuple-element.82), channel_id=1, source_target_pairs={{289,290},{385,386},{417,418},{1,2},{33,34},{129,130},{161,162},{2... | collective-permute-start | bytes 12296 | tf_op jit(solution)/shard_map/ppermute | solution.py:573
  25.2 4.8 %collective-permute-done.2 = f32[1,8,128]{2,1,0:T(8,128)S(1)} collective-permute-done((f32[1,8,128]{2,1,0:T(8,128)S(1)}, f32[1,8,128]{2,1,0:T(8,128)S(1)}, u32[]{:S(2)}, u32[]{:S(2)}) %collective-permute-start.2) | collective-permute-done | bytes 4128 | tf_op jit(solution)/shard_map/ppermute | solution.py:573
  29.9 3.5 %collective-permute-start.3 = (f32[3,8,128]{2,1,0:T(8,128)S(1)}, f32[3,8,128]{2,1,0:T(8,128)S(1)}, u32[]{:S(2)}, u32[]{:S(2)}) collective-permute-start(f32[3,8,128]{2,1,0:T(8,128)S(1)} %constant_dynamic-update-slice_fusion), channel_id=1, source_target_pairs={{289,297},{385,393},{417,425},{1,9},{33,41},{129,137},{161,169},{2... | collective-permute-start | bytes 36872 | tf_op jit(solution)/shard_map/ppermute | solution.py:573
  33.4 2.4 %collective-permute-start.4 = (f32[3,8,128]{2,1,0:T(8,128)S(1)}, f32[3,8,128]{2,1,0:T(8,128)S(1)}, u32[]{:S(2)}, u32[]{:S(2)}) collective-permute-start(f32[3,8,128]{2,1,0:T(8,128)S(1)} %constant_dynamic-update-slice_fusion), channel_id=1, source_target_pairs={{289,313},{385,409},{417,441},{1,25},{33,57},{129,153},{161,185},{... | collective-permute-start | bytes 36872 | tf_op jit(solution)/shard_map/ppermute | solution.py:573
  35.8 3.2 %collective-permute-done.4 = f32[3,8,128]{2,1,0:T(8,128)S(1)} collective-permute-done((f32[3,8,128]{2,1,0:T(8,128)S(1)}, f32[3,8,128]{2,1,0:T(8,128)S(1)}, u32[]{:S(2)}, u32[]{:S(2)}) %collective-permute-start.4) | collective-permute-done | bytes 12320 | tf_op jit(solution)/shard_map/ppermute | solution.py:573
  39.0 1.8 %collective-permute-start.6 = (f32[9,8,128]{2,1,0:T(8,128)S(1)}, f32[9,8,128]{2,1,0:T(8,128)S(1)}, u32[]{:S(2)}, u32[]{:S(2)}) collective-permute-start(f32[9,8,128]{2,1,0:T(8,128)S(1)} %constant_dynamic-update-slice_fusion.3.mid), channel_id=1, source_target_pairs={{289,257},{385,289},{417,385},{1,417},{33,1},{129,33},{161,129},{2... | collective-permute-start | bytes 110600 | tf_op jit(solution)/shard_map/ppermute | solution.py:573
  40.8 1.6 %collective-permute-done.6.high = f32[9,8,128]{2,1,0:T(8,128)S(1)} collective-permute-done((f32[9,8,128]{2,1,0:T(8,128)S(1)}, f32[9,8,128]{2,1,0:T(8,128)S(1)}, u32[]{:S(2)}, u32[]{:S(2)}) %collective-permute-start.6) | collective-permute-done | bytes 36896 | tf_op jit(solution)/shard_map/ppermute | solution.py:573
  42.4 5.0 %collective-permute-done.5.low = f32[9,8,128]{2,1,0:T(8,128)S(1)} collective-permute-done((f32[9,8,128]{2,1,0:T(8,128)S(1)}, f32[9,8,128]{2,1,0:T(8,128)S(1)}, u32[]{:S(2)}, u32[]{:S(2)}) %collective-permute-start.5) | collective-permute-done | bytes 36896 | tf_op jit(solution)/shard_map/ppermute | solution.py:573
  47.4 1.5 %shard_map.134 = (f32[8,2048]{1,0:T(8,128)S(1)}, bf16[8,2048]{1,0:T(8,128)(2,1)S(1)}, f32[8,2048]{1,0:T(8,128)S(1)}, bf16[64,512]{1,0:T(8,128)(2,1)S(1)}, bf16[1...) custom-call(s32[1,128]{1,0:T(1,128)S(1)} %get-tuple-element.80.count_ref, ...), custom_call_target="tpu_custom_call" | custom-call | tf_op jit(solution)/shard_map/pallas_call | solution.py:537
  48.9 1.9 %collective-permute-start.7 = (bf16[16,512]{1,0:T(8,128)(2,1)S(1)}, bf16[16,512]{1,0:T(8,128)(2,1)S(1)}, u32[]{:S(2)}, u32[]{:S(2)}) collective-permute-start(bf16[16,512]{1,0:T(8,128)(2,1)S(1)} %get-tuple-element.104), channel_id=1, source_target_pairs={{289,288},{385,384},{417,416},{1,0},{33,32},{129,128},{161,160},{2... | collective-permute-start | bytes 49160 | tf_op jit(solution)/shard_map/ppermute | solution.py:573
  50.9 3.9 %collective-permute-start.8 = (bf16[16,512]{1,0:T(8,128)(2,1)S(1)}, bf16[16,512]{1,0:T(8,128)(2,1)S(1)}, u32[]{:S(2)}, u32[]{:S(2)}) collective-permute-start(bf16[16,512]{1,0:T(8,128)(2,1)S(1)} %get-tuple-element.104), channel_id=1, source_target_pairs={{289,290},{385,386},{417,418},{1,2},{33,34},{129,130},{161,162},{2... | collective-permute-start | bytes 49160 | tf_op jit(solution)/shard_map/ppermute | solution.py:573
  54.8 2.9 %collective-permute-done.8 = bf16[16,512]{1,0:T(8,128)(2,1)S(1)} collective-permute-done((bf16[16,512]{1,0:T(8,128)(2,1)S(1)}, bf16[16,512]{1,0:T(8,128)(2,1)S(1)}, u32[]{:S(2)}, u32[]{:S(2)}) %collective-permute-start.8) | collective-permute-done | bytes 16416 | tf_op jit(solution)/shard_map/ppermute | solution.py:573
  57.7 3.2 %collective-permute-start.9 = (bf16[48,512]{1,0:T(8,128)(2,1)S(1)}, bf16[48,512]{1,0:T(8,128)(2,1)S(1)}, u32[]{:S(2)}, u32[]{:S(2)}) collective-permute-start(bf16[48,512]{1,0:T(8,128)(2,1)S(1)} %constant_dynamic-update-slice_fusion.8), channel_id=1, source_target_pairs={{289,297},{385,393},{417,425},{1,9},{33,41},{129,137},{161,169},{2... | collective-permute-start | bytes 147464 | tf_op jit(solution)/shard_map/ppermute | solution.py:573
  60.9 2.8 %collective-permute-start.10 = (bf16[48,512]{1,0:T(8,128)(2,1)S(1)}, bf16[48,512]{1,0:T(8,128)(2,1)S(1)}, u32[]{:S(2)}, u32[]{:S(2)}) collective-permute-start(bf16[48,512]{1,0:T(8,128)(2,1)S(1)} %constant_dynamic-update-slice_fusion.8), channel_id=1, source_target_pairs={{289,313},{385,409},{417,441},{1,25},{33,57},{129,153},{161,185},{... | collective-permute-start | bytes 147464 | tf_op jit(solution)/shard_map/ppermute | solution.py:573
  63.8 3.1 %collective-permute-done.10 = bf16[48,512]{1,0:T(8,128)(2,1)S(1)} collective-permute-done((bf16[48,512]{1,0:T(8,128)(2,1)S(1)}, bf16[48,512]{1,0:T(8,128)(2,1)S(1)}, u32[]{:S(2)}, u32[]{:S(2)}) %collective-permute-start.10) | collective-permute-done | bytes 49184 | tf_op jit(solution)/shard_map/ppermute | solution.py:573
  66.9 0.5 collective-permute-start.11
  67.4 1.8 %shard_map.135 = (bf16[512,2048]{1,0:T(8,128)(2,1)S(1)}, f32[64,2048]{1,0:T(8,128)S(1)}, f32[64,2048]{1,0:T(8,128)S(1)}, f32[64,2048]{1,0:T(8,128)S(1)}, f32[64,...) custom-call(f32[8,2048]{1,0:T(8,128)S(1)} %get-tuple-element.92.facts_ref, ...), custom_call_target="tpu_custom_call" | custom-call | flops 500000000 | bytes 6000000 | tf_op jit(solution)/shard_map/pallas_call | solution.py:537
  69.2 0.4 collective-permute-done.12.high
  69.6 3.1 %collective-permute-done.11.low = bf16[144,512]{1,0:T(8,128)(2,1)S(1)} collective-permute-done((bf16[144,512]{1,0:T(8,128)(2,1)S(1)}, bf16[144,512]{1,0:T(8,128)(2,1)S(1)}, u32[]{:S(2)}, u32[]{:S(2)}) %collective-permute-start.11) | collective-permute-done | bytes 147488 | tf_op jit(solution)/shard_map/ppermute | solution.py:573
  72.7 8.9 %shard_map.136 = (f32[64,512]{1,0:T(8,128)S(1)}, bf16[144,512]{1,0:T(8,128)(2,1)S(1)}, bf16[144,512]{1,0:T(8,128)(2,1)S(1)}, bf16[144,512]{1,0:T(8,128)(2,1)S(1)...) custom-call(s32[1,128]{1,0:T(1,128)S(1)} %get-tuple-element.80.count_ref, f32[8,2048]{1,0:T(8,128)S(1)} %get-tuple-element.92.facts_ref, ...), custom_call_target="tpu_custom_call" | custom-call | tf_op jit(solution)/shard_map/pallas_call | solution.py:537
  81.6 0.0 collective-permute-start.13
  81.6 2.9 %collective-permute-start.14 = (bf16[144,512]{1,0:T(8,128)(2,1)S(1)}, bf16[144,512]{1,0:T(8,128)(2,1)S(1)}, u32[]{:S(2)}, u32[]{:S(2)}) collective-permute-start(bf16[144,512]{1,0:T(8,128)(2,1)S(1)} %get-tuple-element.114), channel_id=1, source_target_pairs={{289,257},{385,289},{417,385},{1,417},{33,1},{129,33},{161,129},{2... | collective-permute-start | bytes 442376 | tf_op jit(solution)/shard_map/ppermute | solution.py:573
  84.6 2.8 %collective-permute-done.13 = bf16[144,512]{1,0:T(8,128)(2,1)S(1)} collective-permute-done((bf16[144,512]{1,0:T(8,128)(2,1)S(1)}, bf16[144,512]{1,0:T(8,128)(2,1)S(1)}, u32[]{:S(2)}, u32[]{:S(2)}) %collective-permute-start.13) | collective-permute-done | bytes 147488 | tf_op jit(solution)/shard_map/ppermute | solution.py:573
  87.5 3.3 %collective-permute-start.15 = (bf16[48,512]{1,0:T(8,128)(2,1)S(1)}, bf16[48,512]{1,0:T(8,128)(2,1)S(1)}, u32[]{:S(2)}, u32[]{:S(2)}) collective-permute-start(bf16[48,512]{1,0:T(8,128)(2,1)S(1)} %get-tuple-element.126), channel_id=1, source_target_pairs={{289,297},{385,393},{417,425},{1,9},{33,41},{129,137},{161,169},{2... | collective-permute-start | bytes 147464 | tf_op jit(solution)/shard_map/ppermute | solution.py:573
  90.8 2.5 %collective-permute-start.16 = (bf16[48,512]{1,0:T(8,128)(2,1)S(1)}, bf16[48,512]{1,0:T(8,128)(2,1)S(1)}, u32[]{:S(2)}, u32[]{:S(2)}) collective-permute-start(bf16[48,512]{1,0:T(8,128)(2,1)S(1)} %get-tuple-element.127), channel_id=1, source_target_pairs={{289,313},{385,409},{417,441},{1,25},{33,57},{129,153},{161,185},{... | collective-permute-start | bytes 147464 | tf_op jit(solution)/shard_map/ppermute | solution.py:573
  93.3 0.1 collective-permute-done.15
  93.4 3.4 %collective-permute-done.16 = bf16[48,512]{1,0:T(8,128)(2,1)S(1)} collective-permute-done((bf16[48,512]{1,0:T(8,128)(2,1)S(1)}, bf16[48,512]{1,0:T(8,128)(2,1)S(1)}, u32[]{:S(2)}, u32[]{:S(2)}) %collective-permute-start.16) | collective-permute-done | bytes 49184 | tf_op jit(solution)/shard_map/ppermute | solution.py:573
  96.8 1.9 %collective-permute-start.17 = (bf16[16,512]{1,0:T(8,128)(2,1)S(1)}, bf16[16,512]{1,0:T(8,128)(2,1)S(1)}, u32[]{:S(2)}, u32[]{:S(2)}) collective-permute-start(bf16[16,512]{1,0:T(8,128)(2,1)S(1)} %get-tuple-element.128), channel_id=1, source_target_pairs={{289,288},{385,384},{417,416},{1,0},{33,32},{129,128},{161,160},{2... | collective-permute-start | bytes 49160 | tf_op jit(solution)/shard_map/ppermute | solution.py:573
  98.8 4.1 %collective-permute-start.18 = (bf16[16,512]{1,0:T(8,128)(2,1)S(1)}, bf16[16,512]{1,0:T(8,128)(2,1)S(1)}, u32[]{:S(2)}, u32[]{:S(2)}) collective-permute-start(bf16[16,512]{1,0:T(8,128)(2,1)S(1)} %get-tuple-element.129), channel_id=1, source_target_pairs={{289,290},{385,386},{417,418},{1,2},{33,34},{129,130},{161,162},{2... | collective-permute-start | bytes 49160 | tf_op jit(solution)/shard_map/ppermute | solution.py:573
  102.9 2.7 %collective-permute-done.18 = bf16[16,512]{1,0:T(8,128)(2,1)S(1)} collective-permute-done((bf16[16,512]{1,0:T(8,128)(2,1)S(1)}, bf16[16,512]{1,0:T(8,128)(2,1)S(1)}, u32[]{:S(2)}, u32[]{:S(2)}) %collective-permute-start.18) | collective-permute-done | bytes 16416 | tf_op jit(solution)/shard_map/ppermute | solution.py:573
  105.6 2.7 %shard_map.137 = (f32[8,128]{1,0:T(8,128)S(1)}, f32[9,8,128]{2,1,0:T(8,128)S(1)}, f32[9,8,128]{2,1,0:T(8,128)S(1)}, f32[9,8,128]{2,1,0:T(8,128)S(1)}) custom-call(s32[1,128]{1,0:T(1,128)S(1)} %get-tuple-element.80.count_ref, f32[8,2048]{1,0:T(8,128)S(1)} %get-tuple-element.92.facts_ref, f32[8,2048]{1,0:T(8,128)S(1)} %get-tuple-element.93.slope, ...), custom_call_target="tpu_custom_call" | custom-call | tf_op jit(solution)/shard_map/pallas_call | solution.py:537
  108.3 2.9 %collective-permute-start.20 = (f32[9,8,128]{2,1,0:T(8,128)S(1)}, f32[9,8,128]{2,1,0:T(8,128)S(1)}, u32[]{:S(2)}, u32[]{:S(2)}) collective-permute-start(f32[9,8,128]{2,1,0:T(8,128)S(1)} %get-tuple-element.123), channel_id=1, source_target_pairs={{289,257},{385,289},{417,385},{1,417},{33,1},{129,33},{161,129},{2... | collective-permute-start | bytes 110600 | tf_op jit(solution)/shard_map/ppermute | solution.py:573
  111.3 1.6 %collective-permute-done.19 = f32[9,8,128]{2,1,0:T(8,128)S(1)} collective-permute-done((f32[9,8,128]{2,1,0:T(8,128)S(1)}, f32[9,8,128]{2,1,0:T(8,128)S(1)}, u32[]{:S(2)}, u32[]{:S(2)}) %collective-permute-start.19) | collective-permute-done | bytes 36896 | tf_op jit(solution)/shard_map/ppermute | solution.py:573
  112.9 3.5 %collective-permute-start.21 = (f32[3,8,128]{2,1,0:T(8,128)S(1)}, f32[3,8,128]{2,1,0:T(8,128)S(1)}, u32[]{:S(2)}, u32[]{:S(2)}) collective-permute-start(f32[3,8,128]{2,1,0:T(8,128)S(1)} %get-tuple-element.130), channel_id=1, source_target_pairs={{289,297},{385,393},{417,425},{1,9},{33,41},{129,137},{161,169},{2... | collective-permute-start | bytes 36872 | tf_op jit(solution)/shard_map/ppermute | solution.py:573
  116.4 2.4 %collective-permute-start.22 = (f32[3,8,128]{2,1,0:T(8,128)S(1)}, f32[3,8,128]{2,1,0:T(8,128)S(1)}, u32[]{:S(2)}, u32[]{:S(2)}) collective-permute-start(f32[3,8,128]{2,1,0:T(8,128)S(1)} %get-tuple-element.131), channel_id=1, source_target_pairs={{289,313},{385,409},{417,441},{1,25},{33,57},{129,153},{161,185},{... | collective-permute-start | bytes 36872 | tf_op jit(solution)/shard_map/ppermute | solution.py:573
  118.8 3.2 %collective-permute-done.22 = f32[3,8,128]{2,1,0:T(8,128)S(1)} collective-permute-done((f32[3,8,128]{2,1,0:T(8,128)S(1)}, f32[3,8,128]{2,1,0:T(8,128)S(1)}, u32[]{:S(2)}, u32[]{:S(2)}) %collective-permute-start.22) | collective-permute-done | bytes 12320 | tf_op jit(solution)/shard_map/ppermute | solution.py:573
  122.0 1.9 %collective-permute-start.23 = (f32[1,8,128]{2,1,0:T(8,128)S(1)}, f32[1,8,128]{2,1,0:T(8,128)S(1)}, u32[]{:S(2)}, u32[]{:S(2)}) collective-permute-start(f32[1,8,128]{2,1,0:T(8,128)S(1)} %get-tuple-element.132), channel_id=1, source_target_pairs={{289,288},{385,384},{417,416},{1,0},{33,32},{129,128},{161,160},{2... | collective-permute-start | bytes 12296 | tf_op jit(solution)/shard_map/ppermute | solution.py:573
  123.9 3.9 %collective-permute-start.24 = (f32[1,8,128]{2,1,0:T(8,128)S(1)}, f32[1,8,128]{2,1,0:T(8,128)S(1)}, u32[]{:S(2)}, u32[]{:S(2)}) collective-permute-start(f32[1,8,128]{2,1,0:T(8,128)S(1)} %get-tuple-element.133), channel_id=1, source_target_pairs={{289,290},{385,386},{417,418},{1,2},{33,34},{129,130},{161,162},{2... | collective-permute-start | bytes 12296 | tf_op jit(solution)/shard_map/ppermute | solution.py:573
  127.9 2.8 %collective-permute-done.24 = f32[1,8,128]{2,1,0:T(8,128)S(1)} collective-permute-done((f32[1,8,128]{2,1,0:T(8,128)S(1)}, f32[1,8,128]{2,1,0:T(8,128)S(1)}, u32[]{:S(2)}, u32[]{:S(2)}) %collective-permute-start.24) | collective-permute-done | bytes 4128 | tf_op jit(solution)/shard_map/ppermute | solution.py:573
  130.6 0.1 shard_map.138
  130.7 1.9 %collective-permute-start.25 = (f32[8,128]{1,0:T(8,128)S(1)}, f32[8,128]{1,0:T(8,128)S(1)}, u32[]{:S(2)}, u32[]{:S(2)}) collective-permute-start(f32[8,128]{1,0:T(8,128)S(1)} %shard_map.138), channel_id=1, source_target_pairs={{289,0},{385,1},{417,2},{1,3},{33,4},{129,5},{161,6},{257,7},{297,... | collective-permute-start | bytes 12296 | tf_op jit(solution)/shard_map/ppermute | solution.py:719
  132.7 5.4 %collective-permute-done.25.out = f32[8,128]{1,0:T(8,128)S(1)} collective-permute-done((f32[8,128]{1,0:T(8,128)S(1)}, f32[8,128]{1,0:T(8,128)S(1)}, u32[]{:S(2)}, u32[]{:S(2)}) %collective-permute-start.25) | collective-permute-done | bytes 4128 | tf_op jit(solution)/shard_map/ppermute | solution.py:719
  138.1 0.6 shard_map.139
  (39 shorter events, 0.2 us)
Async XLA Ops:
  2.2 7.6 %collective-permute-start = (f32[24,128]{1,0:T(8,128)S(1)}, f32[24,128]{1,0:T(8,128)S(1)}, u32[]{:S(2)}, u32[]{:S(2)}) collective-permute-start(f32[24,128]{1,0:T(8,128)S(1)} %shard_map.131), channel_id=1, source_target_pairs={{0,289},{1,385},{2,417},{3,1},{4,33},{5,129},{6,161},{7,257},{8,29... | collective-permute-start | bytes 36872 | tf_op jit(solution)/shard_map/ppermute | solution.py:636
  9.9 15.2 %collective-permute-start.1 = (f32[1,8,128]{2,1,0:T(8,128)S(1)}, f32[1,8,128]{2,1,0:T(8,128)S(1)}, u32[]{:S(2)}, u32[]{:S(2)}) collective-permute-start(f32[1,8,128]{2,1,0:T(8,128)S(1)} %get-tuple-element.82), channel_id=1, source_target_pairs={{289,288},{385,384},{417,416},{1,0},{33,32},{129,128},{161,160},{2... | collective-permute-start | bytes 12296 | tf_op jit(solution)/shard_map/ppermute | solution.py:573
  23.2 6.7 %collective-permute-start.2 = (f32[1,8,128]{2,1,0:T(8,128)S(1)}, f32[1,8,128]{2,1,0:T(8,128)S(1)}, u32[]{:S(2)}, u32[]{:S(2)}) collective-permute-start(f32[1,8,128]{2,1,0:T(8,128)S(1)} %get-tuple-element.82), channel_id=1, source_target_pairs={{289,290},{385,386},{417,418},{1,2},{33,34},{129,130},{161,162},{2... | collective-permute-start | bytes 12296 | tf_op jit(solution)/shard_map/ppermute | solution.py:573
  29.9 5.8 %collective-permute-start.3 = (f32[3,8,128]{2,1,0:T(8,128)S(1)}, f32[3,8,128]{2,1,0:T(8,128)S(1)}, u32[]{:S(2)}, u32[]{:S(2)}) collective-permute-start(f32[3,8,128]{2,1,0:T(8,128)S(1)} %constant_dynamic-update-slice_fusion), channel_id=1, source_target_pairs={{289,297},{385,393},{417,425},{1,9},{33,41},{129,137},{161,169},{2... | collective-permute-start | bytes 36872 | tf_op jit(solution)/shard_map/ppermute | solution.py:573
  33.4 5.6 %collective-permute-start.4 = (f32[3,8,128]{2,1,0:T(8,128)S(1)}, f32[3,8,128]{2,1,0:T(8,128)S(1)}, u32[]{:S(2)}, u32[]{:S(2)}) collective-permute-start(f32[3,8,128]{2,1,0:T(8,128)S(1)} %constant_dynamic-update-slice_fusion), channel_id=1, source_target_pairs={{289,313},{385,409},{417,441},{1,25},{33,57},{129,153},{161,185},{... | collective-permute-start | bytes 36872 | tf_op jit(solution)/shard_map/ppermute | solution.py:573
  39.0 3.4 %collective-permute-start.6 = (f32[9,8,128]{2,1,0:T(8,128)S(1)}, f32[9,8,128]{2,1,0:T(8,128)S(1)}, u32[]{:S(2)}, u32[]{:S(2)}) collective-permute-start(f32[9,8,128]{2,1,0:T(8,128)S(1)} %constant_dynamic-update-slice_fusion.3.mid), channel_id=1, source_target_pairs={{289,257},{385,289},{417,385},{1,417},{33,1},{129,33},{161,129},{2... | collective-permute-start | bytes 110600 | tf_op jit(solution)/shard_map/ppermute | solution.py:573
  40.8 6.6 %collective-permute-start.5 = (f32[9,8,128]{2,1,0:T(8,128)S(1)}, f32[9,8,128]{2,1,0:T(8,128)S(1)}, u32[]{:S(2)}, u32[]{:S(2)}) collective-permute-start(f32[9,8,128]{2,1,0:T(8,128)S(1)} %constant_dynamic-update-slice_fusion.3.mid), channel_id=1, source_target_pairs={{289,385},{385,417},{417,1},{1,33},{33,129},{129,161},{161,257},{2... | collective-permute-start | bytes 110600 | tf_op jit(solution)/shard_map/ppermute | solution.py:573
  48.9 5.9 %collective-permute-start.7 = (bf16[16,512]{1,0:T(8,128)(2,1)S(1)}, bf16[16,512]{1,0:T(8,128)(2,1)S(1)}, u32[]{:S(2)}, u32[]{:S(2)}) collective-permute-start(bf16[16,512]{1,0:T(8,128)(2,1)S(1)} %get-tuple-element.104), channel_id=1, source_target_pairs={{289,288},{385,384},{417,416},{1,0},{33,32},{129,128},{161,160},{2... | collective-permute-start | bytes 49160 | tf_op jit(solution)/shard_map/ppermute | solution.py:573
  50.9 6.8 %collective-permute-start.8 = (bf16[16,512]{1,0:T(8,128)(2,1)S(1)}, bf16[16,512]{1,0:T(8,128)(2,1)S(1)}, u32[]{:S(2)}, u32[]{:S(2)}) collective-permute-start(bf16[16,512]{1,0:T(8,128)(2,1)S(1)} %get-tuple-element.104), channel_id=1, source_target_pairs={{289,290},{385,386},{417,418},{1,2},{33,34},{129,130},{161,162},{2... | collective-permute-start | bytes 49160 | tf_op jit(solution)/shard_map/ppermute | solution.py:573
  57.7 6.0 %collective-permute-start.9 = (bf16[48,512]{1,0:T(8,128)(2,1)S(1)}, bf16[48,512]{1,0:T(8,128)(2,1)S(1)}, u32[]{:S(2)}, u32[]{:S(2)}) collective-permute-start(bf16[48,512]{1,0:T(8,128)(2,1)S(1)} %constant_dynamic-update-slice_fusion.8), channel_id=1, source_target_pairs={{289,297},{385,393},{417,425},{1,9},{33,41},{129,137},{161,169},{2... | collective-permute-start | bytes 147464 | tf_op jit(solution)/shard_map/ppermute | solution.py:573
  60.9 6.0 %collective-permute-start.10 = (bf16[48,512]{1,0:T(8,128)(2,1)S(1)}, bf16[48,512]{1,0:T(8,128)(2,1)S(1)}, u32[]{:S(2)}, u32[]{:S(2)}) collective-permute-start(bf16[48,512]{1,0:T(8,128)(2,1)S(1)} %constant_dynamic-update-slice_fusion.8), channel_id=1, source_target_pairs={{289,313},{385,409},{417,441},{1,25},{33,57},{129,153},{161,185},{... | collective-permute-start | bytes 147464 | tf_op jit(solution)/shard_map/ppermute | solution.py:573
  66.9 2.7 %collective-permute-start.12 = (bf16[144,512]{1,0:T(8,128)(2,1)S(1)}, bf16[144,512]{1,0:T(8,128)(2,1)S(1)}, u32[]{:S(2)}, u32[]{:S(2)}) collective-permute-start(bf16[144,512]{1,0:T(8,128)(2,1)S(1)} %constant_dynamic-update-slice_fusion.11.mid), channel_id=1, source_target_pairs={{289,257},{385,289},{417,385},{1,417},{33,1},{129,33},{161,129},{2... | collective-permute-start | bytes 442376 | tf_op jit(solution)/shard_map/ppermute | solution.py:573
  66.9 5.8 %collective-permute-start.11 = (bf16[144,512]{1,0:T(8,128)(2,1)S(1)}, bf16[144,512]{1,0:T(8,128)(2,1)S(1)}, u32[]{:S(2)}, u32[]{:S(2)}) collective-permute-start(bf16[144,512]{1,0:T(8,128)(2,1)S(1)} %constant_dynamic-update-slice_fusion.11.mid), channel_id=1, source_target_pairs={{289,385},{385,417},{417,1},{1,33},{33,129},{129,161},{161,257},{2... | collective-permute-start | bytes 442376 | tf_op jit(solution)/shard_map/ppermute | solution.py:573
  81.6 5.8 %collective-permute-start.13 = (bf16[144,512]{1,0:T(8,128)(2,1)S(1)}, bf16[144,512]{1,0:T(8,128)(2,1)S(1)}, u32[]{:S(2)}, u32[]{:S(2)}) collective-permute-start(bf16[144,512]{1,0:T(8,128)(2,1)S(1)} %get-tuple-element.113), channel_id=1, source_target_pairs={{289,385},{385,417},{417,1},{1,33},{33,129},{129,161},{161,257},{2... | collective-permute-start | bytes 442376 | tf_op jit(solution)/shard_map/ppermute | solution.py:573
  81.6 5.8 %collective-permute-start.14 = (bf16[144,512]{1,0:T(8,128)(2,1)S(1)}, bf16[144,512]{1,0:T(8,128)(2,1)S(1)}, u32[]{:S(2)}, u32[]{:S(2)}) collective-permute-start(bf16[144,512]{1,0:T(8,128)(2,1)S(1)} %get-tuple-element.114), channel_id=1, source_target_pairs={{289,257},{385,289},{417,385},{1,417},{33,1},{129,33},{161,129},{2... | collective-permute-start | bytes 442376 | tf_op jit(solution)/shard_map/ppermute | solution.py:573
  87.5 6.0 %collective-permute-start.15 = (bf16[48,512]{1,0:T(8,128)(2,1)S(1)}, bf16[48,512]{1,0:T(8,128)(2,1)S(1)}, u32[]{:S(2)}, u32[]{:S(2)}) collective-permute-start(bf16[48,512]{1,0:T(8,128)(2,1)S(1)} %get-tuple-element.126), channel_id=1, source_target_pairs={{289,297},{385,393},{417,425},{1,9},{33,41},{129,137},{161,169},{2... | collective-permute-start | bytes 147464 | tf_op jit(solution)/shard_map/ppermute | solution.py:573
  90.8 6.0 %collective-permute-start.16 = (bf16[48,512]{1,0:T(8,128)(2,1)S(1)}, bf16[48,512]{1,0:T(8,128)(2,1)S(1)}, u32[]{:S(2)}, u32[]{:S(2)}) collective-permute-start(bf16[48,512]{1,0:T(8,128)(2,1)S(1)} %get-tuple-element.127), channel_id=1, source_target_pairs={{289,313},{385,409},{417,441},{1,25},{33,57},{129,153},{161,185},{... | collective-permute-start | bytes 147464 | tf_op jit(solution)/shard_map/ppermute | solution.py:573
  96.8 6.1 %collective-permute-start.17 = (bf16[16,512]{1,0:T(8,128)(2,1)S(1)}, bf16[16,512]{1,0:T(8,128)(2,1)S(1)}, u32[]{:S(2)}, u32[]{:S(2)}) collective-permute-start(bf16[16,512]{1,0:T(8,128)(2,1)S(1)} %get-tuple-element.128), channel_id=1, source_target_pairs={{289,288},{385,384},{417,416},{1,0},{33,32},{129,128},{161,160},{2... | collective-permute-start | bytes 49160 | tf_op jit(solution)/shard_map/ppermute | solution.py:573
  98.8 6.8 %collective-permute-start.18 = (bf16[16,512]{1,0:T(8,128)(2,1)S(1)}, bf16[16,512]{1,0:T(8,128)(2,1)S(1)}, u32[]{:S(2)}, u32[]{:S(2)}) collective-permute-start(bf16[16,512]{1,0:T(8,128)(2,1)S(1)} %get-tuple-element.129), channel_id=1, source_target_pairs={{289,290},{385,386},{417,418},{1,2},{33,34},{129,130},{161,162},{2... | collective-permute-start | bytes 49160 | tf_op jit(solution)/shard_map/ppermute | solution.py:573
  108.3 4.6 %collective-permute-start.19 = (f32[9,8,128]{2,1,0:T(8,128)S(1)}, f32[9,8,128]{2,1,0:T(8,128)S(1)}, u32[]{:S(2)}, u32[]{:S(2)}) collective-permute-start(f32[9,8,128]{2,1,0:T(8,128)S(1)} %get-tuple-element.122), channel_id=1, source_target_pairs={{289,385},{385,417},{417,1},{1,33},{33,129},{129,161},{161,257},{2... | collective-permute-start | bytes 110600 | tf_op jit(solution)/shard_map/ppermute | solution.py:573
  108.3 4.6 %collective-permute-start.20 = (f32[9,8,128]{2,1,0:T(8,128)S(1)}, f32[9,8,128]{2,1,0:T(8,128)S(1)}, u32[]{:S(2)}, u32[]{:S(2)}) collective-permute-start(f32[9,8,128]{2,1,0:T(8,128)S(1)} %get-tuple-element.123), channel_id=1, source_target_pairs={{289,257},{385,289},{417,385},{1,417},{33,1},{129,33},{161,129},{2... | collective-permute-start | bytes 110600 | tf_op jit(solution)/shard_map/ppermute | solution.py:573
  112.9 5.9 %collective-permute-start.21 = (f32[3,8,128]{2,1,0:T(8,128)S(1)}, f32[3,8,128]{2,1,0:T(8,128)S(1)}, u32[]{:S(2)}, u32[]{:S(2)}) collective-permute-start(f32[3,8,128]{2,1,0:T(8,128)S(1)} %get-tuple-element.130), channel_id=1, source_target_pairs={{289,297},{385,393},{417,425},{1,9},{33,41},{129,137},{161,169},{2... | collective-permute-start | bytes 36872 | tf_op jit(solution)/shard_map/ppermute | solution.py:573
  116.4 5.6 %collective-permute-start.22 = (f32[3,8,128]{2,1,0:T(8,128)S(1)}, f32[3,8,128]{2,1,0:T(8,128)S(1)}, u32[]{:S(2)}, u32[]{:S(2)}) collective-permute-start(f32[3,8,128]{2,1,0:T(8,128)S(1)} %get-tuple-element.131), channel_id=1, source_target_pairs={{289,313},{385,409},{417,441},{1,25},{33,57},{129,153},{161,185},{... | collective-permute-start | bytes 36872 | tf_op jit(solution)/shard_map/ppermute | solution.py:573
  122.0 5.8 %collective-permute-start.23 = (f32[1,8,128]{2,1,0:T(8,128)S(1)}, f32[1,8,128]{2,1,0:T(8,128)S(1)}, u32[]{:S(2)}, u32[]{:S(2)}) collective-permute-start(f32[1,8,128]{2,1,0:T(8,128)S(1)} %get-tuple-element.132), channel_id=1, source_target_pairs={{289,288},{385,384},{417,416},{1,0},{33,32},{129,128},{161,160},{2... | collective-permute-start | bytes 12296 | tf_op jit(solution)/shard_map/ppermute | solution.py:573
  123.9 6.7 %collective-permute-start.24 = (f32[1,8,128]{2,1,0:T(8,128)S(1)}, f32[1,8,128]{2,1,0:T(8,128)S(1)}, u32[]{:S(2)}, u32[]{:S(2)}) collective-permute-start(f32[1,8,128]{2,1,0:T(8,128)S(1)} %get-tuple-element.133), channel_id=1, source_target_pairs={{289,290},{385,386},{417,418},{1,2},{33,34},{129,130},{161,162},{2... | collective-permute-start | bytes 12296 | tf_op jit(solution)/shard_map/ppermute | solution.py:573
  130.7 7.3 %collective-permute-start.25 = (f32[8,128]{1,0:T(8,128)S(1)}, f32[8,128]{1,0:T(8,128)S(1)}, u32[]{:S(2)}, u32[]{:S(2)}) collective-permute-start(f32[8,128]{1,0:T(8,128)S(1)} %shard_map.138), channel_id=1, source_target_pairs={{289,0},{385,1},{417,2},{1,3},{33,4},{129,5},{161,6},{257,7},{297,... | collective-permute-start | bytes 12296 | tf_op jit(solution)/shard_map/ppermute | solution.py:719

commit v5 on v4

--- a/solution.py
+++ b/solution.py
@@ -348,16 +348,13 @@
 
 
 def second_kernel(
-    count_ref, facts_ref, slope, onehot, before_two, gate_two, own_rows, low, mid, high,
-    win, wout_t, wout, mix_t, rests, read,
-    grad_own, grad_low, grad_mid, grad_high, pair_out, energy,
-    feats, turned, radial, source, grad_radial, grad_source,
+    count_ref, facts_ref, onehot, before_two, gate_two, own_rows, low, mid, high, wout_t, mix_t, rests, read,
+    grad_own, grad_low, grad_mid, grad_high, grad_radial, grad_unit, energy,
+    feats, turned, radial, source, grad_source,
 ):
     count = count_ref[...]
     facts = facts_ref[...]
-    unit, inverse = unit_of(facts), facts[3:4, :]
-    before, gate = before_two[...], gate_two[...]
-    hidden = (before * gate).astype(BF16)
+    hidden = (before_two[...] * gate_two[...]).astype(BF16)
     feats[0:SLOTS, :] = own_rows[...]
     feats[SLOTS : SLOTS + SLAB, :] = low[...]
     feats[SLOTS + SLAB : SLOTS + 2 * SLAB, :] = mid[...]
@@ -366,7 +363,7 @@
     eye = (iota((C, C), 0) == iota((C, C), 1)).astype(F32).astype(BF16)
     for c in range(4):
         turned[c * C : (c + 1) * C, :] = dot_nt(eye, feats[:, c * C : (c + 1) * C]).astype(BF16)
-    units = [[column(unit[x : x + 1], m) for m in range(COLUMNS)] for x in range(3)]
+    units = [[column(facts[x : x + 1], m) for m in range(COLUMNS)] for x in range(3)]
     wide = 2 * LANES
     a0 = jnp.zeros((C, LANES), F32)
     a1 = [jnp.zeros((C, LANES), F32) for _ in range(3)]
@@ -416,9 +413,7 @@
         for x in range(3):
             grad_source[(x + 1) * C : (x + 2) * C, here] = (q * u[x] + r3 * d1[x]).astype(BF16)
             grad_units[x].append(jnp.sum(q * v[x] + t * d1[x], axis=0, keepdims=True))
-    grad_unit = stack_rows([jnp.concatenate(g, axis=1) for g in grad_units])
-    grad_distance = grad_distance_of(wout, win[1], grad_radial, before, gate, slope[...])
-    pair_out[...] = pair_gradient(unit, inverse, grad_unit, grad_distance)
+    grad_unit[...] = stack_rows([jnp.concatenate(g, axis=1) for g in grad_units])
     grad_projected = dot_nt(onehot[...], grad_source[...])
     outs = (grad_low, grad_mid, grad_high)
     live_rows = (iota((SLOTS, 1), 0) < count[:, 0:1]).astype(F32)
@@ -433,6 +428,12 @@
         for k in range(3):
             begin = SLOTS + k * SLAB
             outs[k][:, at] = rows[begin : begin + SLAB].astype(BF16)
+
+
+def pairs_kernel(facts_ref, slope, before, gate, grad_radial, grad_unit, wout, win, pair_out):
+    facts = facts_ref[...]
+    grad_distance = grad_distance_of(wout, win[1], grad_radial, before[...], gate[...], slope[...])
+    pair_out[...] = pair_gradient(unit_of(facts), facts[3:4, :], grad_unit[...], grad_distance)
 
 
 def third_kernel(
@@ -634,7 +635,6 @@
         cost=pl.CostEstimate(flops=200_000_000, bytes_accessed=2_000_000, transcendentals=0),
     )
     arrived = lax.ppermute(packed, AXES, MOVE_IN)
-    arrived, *weights = lax.optimization_barrier((arrived, *weights))
     (
         radial_in, radial_out_one, radial_out_two, mix_one, readout,
         emb_t, win_t, one_t, two_t, mix_a, mix_b, mix_two_t, spread, read_t, rests,
@@ -679,29 +679,34 @@
         cost=pl.CostEstimate(flops=500_000_000, bytes_accessed=6_000_000, transcendentals=0),
     )
     low, mid, high = spread_halo(outgoing)
-    grad_own, grad_low, grad_mid, grad_high, pairs, energy_two = call(
+    grad_own, grad_low, grad_mid, grad_high, grad_radial, grad_unit, energy_two = call(
         second_kernel,
         [
             ((SLOTS, 4 * C), F32),
             ((SLAB, 4 * C), BF16),
             ((SLAB, 4 * C), BF16),
             ((SLAB, 4 * C), BF16),
+            ((8 * C, PAIRS), BF16),
             ((8, PAIRS), F32),
             ((1, LANES), F32),
         ],
         [
-            count, facts, slope, onehot, before_two, gate_two, own_rows, low, mid, high, radial_in, two_t,
-            radial_out_two, mix_two_t, rests, readout,
+            count, facts, onehot, before_two, gate_two, own_rows, low, mid, high, two_t, mix_two_t, rests, readout,
         ],
         scratch=[
             ((TABLE, 4 * C), BF16),
             ((4 * C, TABLE), BF16),
             ((4 * C, PAIRS), F32),
             ((4 * C, PAIRS), F32),
-            ((8 * C, PAIRS), BF16),
             ((4 * C, PAIRS), BF16),
         ],
-        limit=36 << 20,
+        limit=30 << 20,
+    )
+    (pairs,) = call(
+        pairs_kernel,
+        [((8, PAIRS), F32)],
+        [facts, slope, before_two, gate_two, grad_radial, grad_unit, radial_out_two, radial_in],
+        cost=pl.CostEstimate(flops=500_000_000, bytes_accessed=6_000_000, transcendentals=0),
     )
     back = gather_halo(grad_low, grad_mid, grad_high)
     grad_mine, grad_low, grad_mid, grad_high = call(

time: 141 us -> 141 us (level)
  the two profiles are of different devices: /device:TPU:8 before, /device:TPU:52 now
where the time goes in v5:
time: 141 us; the launch traced here: 140 us
  starting transfers between devices  79.6 us (56%)
  waiting for transfers between devices  39.8 us (28%)
  Pallas kernels  19 us (13%)
  between operations  1.67 us (1%)
    ppermute x24, starting transfers between devices, send(): return lax.ppermute(value, AXES, moves(step))  55.6 us
    ppermute x24, waiting for transfers between devices, send(): return lax.ppermute(value, AXES, moves(step))  31.8 us
    pallas_call x10, Pallas kernels, call(): pl.pallas_call(kernel, out_shape=[jax.ShapeDtypeStruct(s, t) for s, t in...  19 us
    ppermute x1, starting transfers between devices, body(): arrived = lax.ppermute(packed, AXES, MOVE_IN)  15.5 us
    ppermute x1, starting transfers between devices, body(): out = lax.ppermute(out, AXES, MOVE_OUT)  8.55 us
    ppermute x1, waiting for transfers between devices, body(): out = lax.ppermute(out, AXES, MOVE_OUT)  6.54 us
  transfers between devices with their start and end apart: 26, of which 16 were waited for; matrix products, arithmetic and copies ran while one was open for 0% of the time, Pallas kernels for 3%

profile of v5, /device:TPU:52, one launch (start us, length us, event | category | flops | bytes accessed | tf_op | source)
XLA Modules:
  0.0 140.1 jit_solution(258510882688406949)
XLA Ops:
  1.3 0.9 shard_map.131
  2.2 15.5 %collective-permute-start = (f32[24,128]{1,0:T(8,128)S(1)}, f32[24,128]{1,0:T(8,128)S(1)}, u32[]{:S(2)}, u32[]{:S(2)}) collective-permute-start(f32[24,128]{1,0:T(8,128)S(1)} %shard_map.131), channel_id=1, source_target_pairs={{0,289},{1,385},{2,417},{3,1},{4,33},{5,129},{6,161},{7,257},{8,29... | collective-permute-start | bytes 36872 | tf_op jit(solution)/shard_map/ppermute | solution.py:637
  17.7 1.4 collective-permute-done.arrived
  19.1 0.1 shard_map.132
  19.1 1.9 %collective-permute-start.1 = (f32[1,8,128]{2,1,0:T(8,128)S(1)}, f32[1,8,128]{2,1,0:T(8,128)S(1)}, u32[]{:S(2)}, u32[]{:S(2)}) collective-permute-start(f32[1,8,128]{2,1,0:T(8,128)S(1)} %get-tuple-element.51), channel_id=1, source_target_pairs={{289,288},{385,384},{417,416},{1,0},{33,32},{129,128},{161,160},{2... | collective-permute-start | bytes 12296 | tf_op jit(solution)/shard_map/ppermute | solution.py:574
  21.1 3.9 %collective-permute-start.2 = (f32[1,8,128]{2,1,0:T(8,128)S(1)}, f32[1,8,128]{2,1,0:T(8,128)S(1)}, u32[]{:S(2)}, u32[]{:S(2)}) collective-permute-start(f32[1,8,128]{2,1,0:T(8,128)S(1)} %get-tuple-element.51), channel_id=1, source_target_pairs={{289,290},{385,386},{417,418},{1,2},{33,34},{129,130},{161,162},{2... | collective-permute-start | bytes 12296 | tf_op jit(solution)/shard_map/ppermute | solution.py:574
  25.0 1.5 %collective-permute-done.2 = f32[1,8,128]{2,1,0:T(8,128)S(1)} collective-permute-done((f32[1,8,128]{2,1,0:T(8,128)S(1)}, f32[1,8,128]{2,1,0:T(8,128)S(1)}, u32[]{:S(2)}, u32[]{:S(2)}) %collective-permute-start.2) | collective-permute-done | bytes 4128 | tf_op jit(solution)/shard_map/ppermute | solution.py:574
  26.6 3.2 %collective-permute-start.3 = (f32[3,8,128]{2,1,0:T(8,128)S(1)}, f32[3,8,128]{2,1,0:T(8,128)S(1)}, u32[]{:S(2)}, u32[]{:S(2)}) collective-permute-start(f32[3,8,128]{2,1,0:T(8,128)S(1)} %constant_dynamic-update-slice_fusion), channel_id=1, source_target_pairs={{289,297},{385,393},{417,425},{1,9},{33,41},{129,137},{161,169},{2... | collective-permute-start | bytes 36872 | tf_op jit(solution)/shard_map/ppermute | solution.py:574
  29.8 2.7 %collective-permute-start.4 = (f32[3,8,128]{2,1,0:T(8,128)S(1)}, f32[3,8,128]{2,1,0:T(8,128)S(1)}, u32[]{:S(2)}, u32[]{:S(2)}) collective-permute-start(f32[3,8,128]{2,1,0:T(8,128)S(1)} %constant_dynamic-update-slice_fusion), channel_id=1, source_target_pairs={{289,313},{385,409},{417,441},{1,25},{33,57},{129,153},{161,185},{... | collective-permute-start | bytes 36872 | tf_op jit(solution)/shard_map/ppermute | solution.py:574
  32.5 2.9 %collective-permute-done.4 = f32[3,8,128]{2,1,0:T(8,128)S(1)} collective-permute-done((f32[3,8,128]{2,1,0:T(8,128)S(1)}, f32[3,8,128]{2,1,0:T(8,128)S(1)}, u32[]{:S(2)}, u32[]{:S(2)}) %collective-permute-start.4) | collective-permute-done | bytes 12320 | tf_op jit(solution)/shard_map/ppermute | solution.py:574
  35.3 2.0 %collective-permute-start.5 = (f32[9,8,128]{2,1,0:T(8,128)S(1)}, f32[9,8,128]{2,1,0:T(8,128)S(1)}, u32[]{:S(2)}, u32[]{:S(2)}) collective-permute-start(f32[9,8,128]{2,1,0:T(8,128)S(1)} %constant_dynamic-update-slice_fusion.3.mid), channel_id=1, source_target_pairs={{289,385},{385,417},{417,1},{1,33},{33,129},{129,161},{161,257},{2... | collective-permute-start | bytes 110600 | tf_op jit(solution)/shard_map/ppermute | solution.py:574
  37.4 1.8 %shard_map.133 = (bf16[2,8,64]{2,1,0:T(8,128)(2,1)S(1)}, bf16[64,256]{1,0:T(8,128)(2,1)S(1)}, bf16[64,512]{1,0:T(8,128)(2,1)S(1)}, bf16[6,128,128]{2,1,0:T(8,128...) custom-call(bf16[7,128]{1,0:T(8,128)(2,1)} %embedding_far.1, ...), custom_call_target="tpu_custom_call" | custom-call | flops 200000000 | bytes 2000000 | tf_op jit(solution)/shard_map/pallas_call | solution.py:538
  39.2 1.5 %shard_map.134 = (f32[8,2048]{1,0:T(8,128)S(1)}, bf16[8,2048]{1,0:T(8,128)(2,1)S(1)}, f32[8,2048]{1,0:T(8,128)S(1)}, bf16[64,512]{1,0:T(8,128)(2,1)S(1)}, bf16[1...) custom-call(s32[1,128]{1,0:T(1,128)S(1)} %get-tuple-element.49.count_ref, ...), custom_call_target="tpu_custom_call" | custom-call | tf_op jit(solution)/shard_map/pallas_call | solution.py:538
  40.8 5.1 %collective-permute-start.7 = (bf16[16,512]{1,0:T(8,128)(2,1)S(1)}, bf16[16,512]{1,0:T(8,128)(2,1)S(1)}, u32[]{:S(2)}, u32[]{:S(2)}) collective-permute-start(bf16[16,512]{1,0:T(8,128)(2,1)S(1)} %get-tuple-element.73), channel_id=1, source_target_pairs={{289,288},{385,384},{417,416},{1,0},{33,32},{129,128},{161,160},{2... | collective-permute-start | bytes 49160 | tf_op jit(solution)/shard_map/ppermute | solution.py:574
  45.9 1.9 %collective-permute-start.8 = (bf16[16,512]{1,0:T(8,128)(2,1)S(1)}, bf16[16,512]{1,0:T(8,128)(2,1)S(1)}, u32[]{:S(2)}, u32[]{:S(2)}) collective-permute-start(bf16[16,512]{1,0:T(8,128)(2,1)S(1)} %get-tuple-element.73), channel_id=1, source_target_pairs={{289,290},{385,386},{417,418},{1,2},{33,34},{129,130},{161,162},{2... | collective-permute-start | bytes 49160 | tf_op jit(solution)/shard_map/ppermute | solution.py:574
  47.8 4.1 %collective-permute-done.8 = bf16[16,512]{1,0:T(8,128)(2,1)S(1)} collective-permute-done((bf16[16,512]{1,0:T(8,128)(2,1)S(1)}, bf16[16,512]{1,0:T(8,128)(2,1)S(1)}, u32[]{:S(2)}, u32[]{:S(2)}) %collective-permute-start.8) | collective-permute-done | bytes 16416 | tf_op jit(solution)/shard_map/ppermute | solution.py:574
  52.0 3.3 %collective-permute-start.9 = (bf16[48,512]{1,0:T(8,128)(2,1)S(1)}, bf16[48,512]{1,0:T(8,128)(2,1)S(1)}, u32[]{:S(2)}, u32[]{:S(2)}) collective-permute-start(bf16[48,512]{1,0:T(8,128)(2,1)S(1)} %constant_dynamic-update-slice_fusion.8), channel_id=1, source_target_pairs={{289,297},{385,393},{417,425},{1,9},{33,41},{129,137},{161,169},{2... | collective-permute-start | bytes 147464 | tf_op jit(solution)/shard_map/ppermute | solution.py:574
  55.3 2.5 %collective-permute-start.10 = (bf16[48,512]{1,0:T(8,128)(2,1)S(1)}, bf16[48,512]{1,0:T(8,128)(2,1)S(1)}, u32[]{:S(2)}, u32[]{:S(2)}) collective-permute-start(bf16[48,512]{1,0:T(8,128)(2,1)S(1)} %constant_dynamic-update-slice_fusion.8), channel_id=1, source_target_pairs={{289,313},{385,409},{417,441},{1,25},{33,57},{129,153},{161,185},{... | collective-permute-start | bytes 147464 | tf_op jit(solution)/shard_map/ppermute | solution.py:574
  57.8 0.1 collective-permute-done.9
  58.0 3.5 %collective-permute-done.10 = bf16[48,512]{1,0:T(8,128)(2,1)S(1)} collective-permute-done((bf16[48,512]{1,0:T(8,128)(2,1)S(1)}, bf16[48,512]{1,0:T(8,128)(2,1)S(1)}, u32[]{:S(2)}, u32[]{:S(2)}) %collective-permute-start.10) | collective-permute-done | bytes 49184 | tf_op jit(solution)/shard_map/ppermute | solution.py:574
  61.5 0.5 collective-permute-start.11
  62.0 1.8 %shard_map.135 = (bf16[512,2048]{1,0:T(8,128)(2,1)S(1)}, f32[64,2048]{1,0:T(8,128)S(1)}, f32[64,2048]{1,0:T(8,128)S(1)}, f32[64,2048]{1,0:T(8,128)S(1)}, f32[64,...) custom-call(f32[8,2048]{1,0:T(8,128)S(1)} %get-tuple-element.61.facts_ref, ...), custom_call_target="tpu_custom_call" | custom-call | flops 500000000 | bytes 6000000 | tf_op jit(solution)/shard_map/pallas_call | solution.py:538
  63.8 0.4 collective-permute-done.12.high
  64.2 1.9 %collective-permute-done.11.low = bf16[144,512]{1,0:T(8,128)(2,1)S(1)} collective-permute-done((bf16[144,512]{1,0:T(8,128)(2,1)S(1)}, bf16[144,512]{1,0:T(8,128)(2,1)S(1)}, u32[]{:S(2)}, u32[]{:S(2)}) %collective-permute-start.11) | collective-permute-done | bytes 147488 | tf_op jit(solution)/shard_map/ppermute | solution.py:574
  66.1 8.3 %shard_map.136 = (f32[64,512]{1,0:T(8,128)S(1)}, bf16[144,512]{1,0:T(8,128)(2,1)S(1)}, bf16[144,512]{1,0:T(8,128)(2,1)S(1)}, bf16[144,512]{1,0:T(8,128)(2,1)S(1)...) custom-call(s32[1,128]{1,0:T(1,128)S(1)} %get-tuple-element.49.count_ref, ...), custom_call_target="tpu_custom_call" | custom-call | tf_op jit(solution)/shard_map/pallas_call | solution.py:538
  74.4 2.6 %collective-permute-start.13 = (bf16[144,512]{1,0:T(8,128)(2,1)S(1)}, bf16[144,512]{1,0:T(8,128)(2,1)S(1)}, u32[]{:S(2)}, u32[]{:S(2)}) collective-permute-start(bf16[144,512]{1,0:T(8,128)(2,1)S(1)} %get-tuple-element.80), channel_id=1, source_target_pairs={{289,385},{385,417},{417,1},{1,33},{33,129},{129,161},{161,257},{2... | collective-permute-start | bytes 442376 | tf_op jit(solution)/shard_map/ppermute | solution.py:574
  77.0 2.0 %collective-permute-done.13 = bf16[144,512]{1,0:T(8,128)(2,1)S(1)} collective-permute-done((bf16[144,512]{1,0:T(8,128)(2,1)S(1)}, bf16[144,512]{1,0:T(8,128)(2,1)S(1)}, u32[]{:S(2)}, u32[]{:S(2)}) %collective-permute-start.13) | collective-permute-done | bytes 147488 | tf_op jit(solution)/shard_map/ppermute | solution.py:574
  79.0 0.7 collective-permute-done.14
  79.7 3.7 %collective-permute-start.15 = (bf16[48,512]{1,0:T(8,128)(2,1)S(1)}, bf16[48,512]{1,0:T(8,128)(2,1)S(1)}, u32[]{:S(2)}, u32[]{:S(2)}) collective-permute-start(bf16[48,512]{1,0:T(8,128)(2,1)S(1)} %get-tuple-element.96), channel_id=1, source_target_pairs={{289,297},{385,393},{417,425},{1,9},{33,41},{129,137},{161,169},{2... | collective-permute-start | bytes 147464 | tf_op jit(solution)/shard_map/ppermute | solution.py:574
  83.4 2.4 %collective-permute-start.16 = (bf16[48,512]{1,0:T(8,128)(2,1)S(1)}, bf16[48,512]{1,0:T(8,128)(2,1)S(1)}, u32[]{:S(2)}, u32[]{:S(2)}) collective-permute-start(bf16[48,512]{1,0:T(8,128)(2,1)S(1)} %get-tuple-element.97), channel_id=1, source_target_pairs={{289,313},{385,409},{417,441},{1,25},{33,57},{129,153},{161,185},{... | collective-permute-start | bytes 147464 | tf_op jit(solution)/shard_map/ppermute | solution.py:574
  85.8 3.6 %collective-permute-done.16 = bf16[48,512]{1,0:T(8,128)(2,1)S(1)} collective-permute-done((bf16[48,512]{1,0:T(8,128)(2,1)S(1)}, bf16[48,512]{1,0:T(8,128)(2,1)S(1)}, u32[]{:S(2)}, u32[]{:S(2)}) %collective-permute-start.16) | collective-permute-done | bytes 49184 | tf_op jit(solution)/shard_map/ppermute | solution.py:574
  89.4 4.4 %collective-permute-start.17 = (bf16[16,512]{1,0:T(8,128)(2,1)S(1)}, bf16[16,512]{1,0:T(8,128)(2,1)S(1)}, u32[]{:S(2)}, u32[]{:S(2)}) collective-permute-start(bf16[16,512]{1,0:T(8,128)(2,1)S(1)} %get-tuple-element.98), channel_id=1, source_target_pairs={{289,288},{385,384},{417,416},{1,0},{33,32},{129,128},{161,160},{2... | collective-permute-start | bytes 49160 | tf_op jit(solution)/shard_map/ppermute | solution.py:574
  93.8 1.9 %collective-permute-start.18 = (bf16[16,512]{1,0:T(8,128)(2,1)S(1)}, bf16[16,512]{1,0:T(8,128)(2,1)S(1)}, u32[]{:S(2)}, u32[]{:S(2)}) collective-permute-start(bf16[16,512]{1,0:T(8,128)(2,1)S(1)} %get-tuple-element.99), channel_id=1, source_target_pairs={{289,290},{385,386},{417,418},{1,2},{33,34},{129,130},{161,162},{2... | collective-permute-start | bytes 49160 | tf_op jit(solution)/shard_map/ppermute | solution.py:574
  95.7 1.0 shard_map.137.pair_in
  96.8 2.7 %collective-permute-done.18 = bf16[16,512]{1,0:T(8,128)(2,1)S(1)} collective-permute-done((bf16[16,512]{1,0:T(8,128)(2,1)S(1)}, bf16[16,512]{1,0:T(8,128)(2,1)S(1)}, u32[]{:S(2)}, u32[]{:S(2)}) %collective-permute-start.18) | collective-permute-done | bytes 16416 | tf_op jit(solution)/shard_map/ppermute | solution.py:574
  99.5 2.7 %shard_map.138 = (f32[8,128]{1,0:T(8,128)S(1)}, f32[9,8,128]{2,1,0:T(8,128)S(1)}, f32[9,8,128]{2,1,0:T(8,128)S(1)}, f32[9,8,128]{2,1,0:T(8,128)S(1)}) custom-call(s32[1,128]{1,0:T(1,128)S(1)} %get-tuple-element.49.count_ref, f32[8,2048]{1,0:T(8,128)S(1)} %get-tuple-element.61.facts_ref, f32[8,2048]{1,0:T(8,128)S(1)} %get-tuple-element.62.slope, ...), custom_call_target="tpu_custom_call" | custom-call | tf_op jit(solution)/shard_map/pallas_call | solution.py:538
  102.2 1.7 %collective-permute-start.20 = (f32[9,8,128]{2,1,0:T(8,128)S(1)}, f32[9,8,128]{2,1,0:T(8,128)S(1)}, u32[]{:S(2)}, u32[]{:S(2)}) collective-permute-start(f32[9,8,128]{2,1,0:T(8,128)S(1)} %get-tuple-element.93), channel_id=1, source_target_pairs={{289,257},{385,289},{417,385},{1,417},{33,1},{129,33},{161,129},{2... | collective-permute-start | bytes 110600 | tf_op jit(solution)/shard_map/ppermute | solution.py:574
  104.0 1.6 %collective-permute-done.19 = f32[9,8,128]{2,1,0:T(8,128)S(1)} collective-permute-done((f32[9,8,128]{2,1,0:T(8,128)S(1)}, f32[9,8,128]{2,1,0:T(8,128)S(1)}, u32[]{:S(2)}, u32[]{:S(2)}) %collective-permute-start.19) | collective-permute-done | bytes 36896 | tf_op jit(solution)/shard_map/ppermute | solution.py:574
  105.6 3.5 %collective-permute-start.21 = (f32[3,8,128]{2,1,0:T(8,128)S(1)}, f32[3,8,128]{2,1,0:T(8,128)S(1)}, u32[]{:S(2)}, u32[]{:S(2)}) collective-permute-start(f32[3,8,128]{2,1,0:T(8,128)S(1)} %get-tuple-element.100), channel_id=1, source_target_pairs={{289,297},{385,393},{417,425},{1,9},{33,41},{129,137},{161,169},{2... | collective-permute-start | bytes 36872 | tf_op jit(solution)/shard_map/ppermute | solution.py:574
  109.1 2.4 %collective-permute-start.22 = (f32[3,8,128]{2,1,0:T(8,128)S(1)}, f32[3,8,128]{2,1,0:T(8,128)S(1)}, u32[]{:S(2)}, u32[]{:S(2)}) collective-permute-start(f32[3,8,128]{2,1,0:T(8,128)S(1)} %get-tuple-element.101), channel_id=1, source_target_pairs={{289,313},{385,409},{417,441},{1,25},{33,57},{129,153},{161,185},{... | collective-permute-start | bytes 36872 | tf_op jit(solution)/shard_map/ppermute | solution.py:574
  111.5 3.2 %collective-permute-done.22 = f32[3,8,128]{2,1,0:T(8,128)S(1)} collective-permute-done((f32[3,8,128]{2,1,0:T(8,128)S(1)}, f32[3,8,128]{2,1,0:T(8,128)S(1)}, u32[]{:S(2)}, u32[]{:S(2)}) %collective-permute-start.22) | collective-permute-done | bytes 12320 | tf_op jit(solution)/shard_map/ppermute | solution.py:574
  114.7 4.1 %collective-permute-start.23 = (f32[1,8,128]{2,1,0:T(8,128)S(1)}, f32[1,8,128]{2,1,0:T(8,128)S(1)}, u32[]{:S(2)}, u32[]{:S(2)}) collective-permute-start(f32[1,8,128]{2,1,0:T(8,128)S(1)} %get-tuple-element.102), channel_id=1, source_target_pairs={{289,288},{385,384},{417,416},{1,0},{33,32},{129,128},{161,160},{2... | collective-permute-start | bytes 12296 | tf_op jit(solution)/shard_map/ppermute | solution.py:574
  118.8 1.9 %collective-permute-start.24 = (f32[1,8,128]{2,1,0:T(8,128)S(1)}, f32[1,8,128]{2,1,0:T(8,128)S(1)}, u32[]{:S(2)}, u32[]{:S(2)}) collective-permute-start(f32[1,8,128]{2,1,0:T(8,128)S(1)} %get-tuple-element.103), channel_id=1, source_target_pairs={{289,290},{385,386},{417,418},{1,2},{33,34},{129,130},{161,162},{2... | collective-permute-start | bytes 12296 | tf_op jit(solution)/shard_map/ppermute | solution.py:574
  120.8 3.6 %collective-permute-done.24 = f32[1,8,128]{2,1,0:T(8,128)S(1)} collective-permute-done((f32[1,8,128]{2,1,0:T(8,128)S(1)}, f32[1,8,128]{2,1,0:T(8,128)S(1)}, u32[]{:S(2)}, u32[]{:S(2)}) %collective-permute-start.24) | collective-permute-done | bytes 4128 | tf_op jit(solution)/shard_map/ppermute | solution.py:574
  124.3 0.1 shard_map.139
  124.4 8.6 %collective-permute-start.25 = (f32[8,128]{1,0:T(8,128)S(1)}, f32[8,128]{1,0:T(8,128)S(1)}, u32[]{:S(2)}, u32[]{:S(2)}) collective-permute-start(f32[8,128]{1,0:T(8,128)S(1)} %shard_map.139), channel_id=1, source_target_pairs={{289,0},{385,1},{417,2},{1,3},{33,4},{129,5},{161,6},{257,7},{297,... | collective-permute-start | bytes 12296 | tf_op jit(solution)/shard_map/ppermute | solution.py:724
  133.0 6.5 %collective-permute-done.25.out = f32[8,128]{1,0:T(8,128)S(1)} collective-permute-done((f32[8,128]{1,0:T(8,128)S(1)}, f32[8,128]{1,0:T(8,128)S(1)}, u32[]{:S(2)}, u32[]{:S(2)}) %collective-permute-start.25) | collective-permute-done | bytes 4128 | tf_op jit(solution)/shard_map/ppermute | solution.py:724
  139.5 0.6 shard_map.140
  (40 shorter events, 0.2 us)
Async XLA Ops:
  2.2 16.8 %collective-permute-start = (f32[24,128]{1,0:T(8,128)S(1)}, f32[24,128]{1,0:T(8,128)S(1)}, u32[]{:S(2)}, u32[]{:S(2)}) collective-permute-start(f32[24,128]{1,0:T(8,128)S(1)} %shard_map.131), channel_id=1, source_target_pairs={{0,289},{1,385},{2,417},{3,1},{4,33},{5,129},{6,161},{7,257},{8,29... | collective-permute-start | bytes 36872 | tf_op jit(solution)/shard_map/ppermute | solution.py:637
  19.1 5.9 %collective-permute-start.1 = (f32[1,8,128]{2,1,0:T(8,128)S(1)}, f32[1,8,128]{2,1,0:T(8,128)S(1)}, u32[]{:S(2)}, u32[]{:S(2)}) collective-permute-start(f32[1,8,128]{2,1,0:T(8,128)S(1)} %get-tuple-element.51), channel_id=1, source_target_pairs={{289,288},{385,384},{417,416},{1,0},{33,32},{129,128},{161,160},{2... | collective-permute-start | bytes 12296 | tf_op jit(solution)/shard_map/ppermute | solution.py:574
  21.1 5.5 %collective-permute-start.2 = (f32[1,8,128]{2,1,0:T(8,128)S(1)}, f32[1,8,128]{2,1,0:T(8,128)S(1)}, u32[]{:S(2)}, u32[]{:S(2)}) collective-permute-start(f32[1,8,128]{2,1,0:T(8,128)S(1)} %get-tuple-element.51), channel_id=1, source_target_pairs={{289,290},{385,386},{417,418},{1,2},{33,34},{129,130},{161,162},{2... | collective-permute-start | bytes 12296 | tf_op jit(solution)/shard_map/ppermute | solution.py:574
  26.6 5.8 %collective-permute-start.3 = (f32[3,8,128]{2,1,0:T(8,128)S(1)}, f32[3,8,128]{2,1,0:T(8,128)S(1)}, u32[]{:S(2)}, u32[]{:S(2)}) collective-permute-start(f32[3,8,128]{2,1,0:T(8,128)S(1)} %constant_dynamic-update-slice_fusion), channel_id=1, source_target_pairs={{289,297},{385,393},{417,425},{1,9},{33,41},{129,137},{161,169},{2... | collective-permute-start | bytes 36872 | tf_op jit(solution)/shard_map/ppermute | solution.py:574
  29.8 5.6 %collective-permute-start.4 = (f32[3,8,128]{2,1,0:T(8,128)S(1)}, f32[3,8,128]{2,1,0:T(8,128)S(1)}, u32[]{:S(2)}, u32[]{:S(2)}) collective-permute-start(f32[3,8,128]{2,1,0:T(8,128)S(1)} %constant_dynamic-update-slice_fusion), channel_id=1, source_target_pairs={{289,313},{385,409},{417,441},{1,25},{33,57},{129,153},{161,185},{... | collective-permute-start | bytes 36872 | tf_op jit(solution)/shard_map/ppermute | solution.py:574
  35.3 3.9 %collective-permute-start.6 = (f32[9,8,128]{2,1,0:T(8,128)S(1)}, f32[9,8,128]{2,1,0:T(8,128)S(1)}, u32[]{:S(2)}, u32[]{:S(2)}) collective-permute-start(f32[9,8,128]{2,1,0:T(8,128)S(1)} %constant_dynamic-update-slice_fusion.3.mid), channel_id=1, source_target_pairs={{289,257},{385,289},{417,385},{1,417},{33,1},{129,33},{161,129},{2... | collective-permute-start | bytes 110600 | tf_op jit(solution)/shard_map/ppermute | solution.py:574
  35.3 3.9 %collective-permute-start.5 = (f32[9,8,128]{2,1,0:T(8,128)S(1)}, f32[9,8,128]{2,1,0:T(8,128)S(1)}, u32[]{:S(2)}, u32[]{:S(2)}) collective-permute-start(f32[9,8,128]{2,1,0:T(8,128)S(1)} %constant_dynamic-update-slice_fusion.3.mid), channel_id=1, source_target_pairs={{289,385},{385,417},{417,1},{1,33},{33,129},{129,161},{161,257},{2... | collective-permute-start | bytes 110600 | tf_op jit(solution)/shard_map/ppermute | solution.py:574
  40.8 7.0 %collective-permute-start.7 = (bf16[16,512]{1,0:T(8,128)(2,1)S(1)}, bf16[16,512]{1,0:T(8,128)(2,1)S(1)}, u32[]{:S(2)}, u32[]{:S(2)}) collective-permute-start(bf16[16,512]{1,0:T(8,128)(2,1)S(1)} %get-tuple-element.73), channel_id=1, source_target_pairs={{289,288},{385,384},{417,416},{1,0},{33,32},{129,128},{161,160},{2... | collective-permute-start | bytes 49160 | tf_op jit(solution)/shard_map/ppermute | solution.py:574
  45.9 6.1 %collective-permute-start.8 = (bf16[16,512]{1,0:T(8,128)(2,1)S(1)}, bf16[16,512]{1,0:T(8,128)(2,1)S(1)}, u32[]{:S(2)}, u32[]{:S(2)}) collective-permute-start(bf16[16,512]{1,0:T(8,128)(2,1)S(1)} %get-tuple-element.73), channel_id=1, source_target_pairs={{289,290},{385,386},{417,418},{1,2},{33,34},{129,130},{161,162},{2... | collective-permute-start | bytes 49160 | tf_op jit(solution)/shard_map/ppermute | solution.py:574
  52.0 6.0 %collective-permute-start.9 = (bf16[48,512]{1,0:T(8,128)(2,1)S(1)}, bf16[48,512]{1,0:T(8,128)(2,1)S(1)}, u32[]{:S(2)}, u32[]{:S(2)}) collective-permute-start(bf16[48,512]{1,0:T(8,128)(2,1)S(1)} %constant_dynamic-update-slice_fusion.8), channel_id=1, source_target_pairs={{289,297},{385,393},{417,425},{1,9},{33,41},{129,137},{161,169},{2... | collective-permute-start | bytes 147464 | tf_op jit(solution)/shard_map/ppermute | solution.py:574
  55.3 6.2 %collective-permute-start.10 = (bf16[48,512]{1,0:T(8,128)(2,1)S(1)}, bf16[48,512]{1,0:T(8,128)(2,1)S(1)}, u32[]{:S(2)}, u32[]{:S(2)}) collective-permute-start(bf16[48,512]{1,0:T(8,128)(2,1)S(1)} %constant_dynamic-update-slice_fusion.8), channel_id=1, source_target_pairs={{289,313},{385,409},{417,441},{1,25},{33,57},{129,153},{161,185},{... | collective-permute-start | bytes 147464 | tf_op jit(solution)/shard_map/ppermute | solution.py:574
  61.5 2.7 %collective-permute-start.12 = (bf16[144,512]{1,0:T(8,128)(2,1)S(1)}, bf16[144,512]{1,0:T(8,128)(2,1)S(1)}, u32[]{:S(2)}, u32[]{:S(2)}) collective-permute-start(bf16[144,512]{1,0:T(8,128)(2,1)S(1)} %constant_dynamic-update-slice_fusion.11.mid), channel_id=1, source_target_pairs={{289,257},{385,289},{417,385},{1,417},{33,1},{129,33},{161,129},{2... | collective-permute-start | bytes 442376 | tf_op jit(solution)/shard_map/ppermute | solution.py:574
  61.5 4.6 %collective-permute-start.11 = (bf16[144,512]{1,0:T(8,128)(2,1)S(1)}, bf16[144,512]{1,0:T(8,128)(2,1)S(1)}, u32[]{:S(2)}, u32[]{:S(2)}) collective-permute-start(bf16[144,512]{1,0:T(8,128)(2,1)S(1)} %constant_dynamic-update-slice_fusion.11.mid), channel_id=1, source_target_pairs={{289,385},{385,417},{417,1},{1,33},{33,129},{129,161},{161,257},{2... | collective-permute-start | bytes 442376 | tf_op jit(solution)/shard_map/ppermute | solution.py:574
  74.4 4.6 %collective-permute-start.13 = (bf16[144,512]{1,0:T(8,128)(2,1)S(1)}, bf16[144,512]{1,0:T(8,128)(2,1)S(1)}, u32[]{:S(2)}, u32[]{:S(2)}) collective-permute-start(bf16[144,512]{1,0:T(8,128)(2,1)S(1)} %get-tuple-element.80), channel_id=1, source_target_pairs={{289,385},{385,417},{417,1},{1,33},{33,129},{129,161},{161,257},{2... | collective-permute-start | bytes 442376 | tf_op jit(solution)/shard_map/ppermute | solution.py:574
  77.0 2.7 %collective-permute-start.14 = (bf16[144,512]{1,0:T(8,128)(2,1)S(1)}, bf16[144,512]{1,0:T(8,128)(2,1)S(1)}, u32[]{:S(2)}, u32[]{:S(2)}) collective-permute-start(bf16[144,512]{1,0:T(8,128)(2,1)S(1)} %get-tuple-element.81), channel_id=1, source_target_pairs={{289,257},{385,289},{417,385},{1,417},{33,1},{129,33},{161,129},{2... | collective-permute-start | bytes 442376 | tf_op jit(solution)/shard_map/ppermute | solution.py:574
  79.7 6.0 %collective-permute-start.15 = (bf16[48,512]{1,0:T(8,128)(2,1)S(1)}, bf16[48,512]{1,0:T(8,128)(2,1)S(1)}, u32[]{:S(2)}, u32[]{:S(2)}) collective-permute-start(bf16[48,512]{1,0:T(8,128)(2,1)S(1)} %get-tuple-element.96), channel_id=1, source_target_pairs={{289,297},{385,393},{417,425},{1,9},{33,41},{129,137},{161,169},{2... | collective-permute-start | bytes 147464 | tf_op jit(solution)/shard_map/ppermute | solution.py:574
  83.4 6.0 %collective-permute-start.16 = (bf16[48,512]{1,0:T(8,128)(2,1)S(1)}, bf16[48,512]{1,0:T(8,128)(2,1)S(1)}, u32[]{:S(2)}, u32[]{:S(2)}) collective-permute-start(bf16[48,512]{1,0:T(8,128)(2,1)S(1)} %get-tuple-element.97), channel_id=1, source_target_pairs={{289,313},{385,409},{417,441},{1,25},{33,57},{129,153},{161,185},{... | collective-permute-start | bytes 147464 | tf_op jit(solution)/shard_map/ppermute | solution.py:574
  89.4 7.4 %collective-permute-start.17 = (bf16[16,512]{1,0:T(8,128)(2,1)S(1)}, bf16[16,512]{1,0:T(8,128)(2,1)S(1)}, u32[]{:S(2)}, u32[]{:S(2)}) collective-permute-start(bf16[16,512]{1,0:T(8,128)(2,1)S(1)} %get-tuple-element.98), channel_id=1, source_target_pairs={{289,288},{385,384},{417,416},{1,0},{33,32},{129,128},{161,160},{2... | collective-permute-start | bytes 49160 | tf_op jit(solution)/shard_map/ppermute | solution.py:574
  93.8 5.6 %collective-permute-start.18 = (bf16[16,512]{1,0:T(8,128)(2,1)S(1)}, bf16[16,512]{1,0:T(8,128)(2,1)S(1)}, u32[]{:S(2)}, u32[]{:S(2)}) collective-permute-start(bf16[16,512]{1,0:T(8,128)(2,1)S(1)} %get-tuple-element.99), channel_id=1, source_target_pairs={{289,290},{385,386},{417,418},{1,2},{33,34},{129,130},{161,162},{2... | collective-permute-start | bytes 49160 | tf_op jit(solution)/shard_map/ppermute | solution.py:574
  102.2 3.4 %collective-permute-start.19 = (f32[9,8,128]{2,1,0:T(8,128)S(1)}, f32[9,8,128]{2,1,0:T(8,128)S(1)}, u32[]{:S(2)}, u32[]{:S(2)}) collective-permute-start(f32[9,8,128]{2,1,0:T(8,128)S(1)} %get-tuple-element.92), channel_id=1, source_target_pairs={{289,385},{385,417},{417,1},{1,33},{33,129},{129,161},{161,257},{2... | collective-permute-start | bytes 110600 | tf_op jit(solution)/shard_map/ppermute | solution.py:574
  102.2 3.4 %collective-permute-start.20 = (f32[9,8,128]{2,1,0:T(8,128)S(1)}, f32[9,8,128]{2,1,0:T(8,128)S(1)}, u32[]{:S(2)}, u32[]{:S(2)}) collective-permute-start(f32[9,8,128]{2,1,0:T(8,128)S(1)} %get-tuple-element.93), channel_id=1, source_target_pairs={{289,257},{385,289},{417,385},{1,417},{33,1},{129,33},{161,129},{2... | collective-permute-start | bytes 110600 | tf_op jit(solution)/shard_map/ppermute | solution.py:574
  105.6 5.9 %collective-permute-start.21 = (f32[3,8,128]{2,1,0:T(8,128)S(1)}, f32[3,8,128]{2,1,0:T(8,128)S(1)}, u32[]{:S(2)}, u32[]{:S(2)}) collective-permute-start(f32[3,8,128]{2,1,0:T(8,128)S(1)} %get-tuple-element.100), channel_id=1, source_target_pairs={{289,297},{385,393},{417,425},{1,9},{33,41},{129,137},{161,169},{2... | collective-permute-start | bytes 36872 | tf_op jit(solution)/shard_map/ppermute | solution.py:574
  109.1 5.6 %collective-permute-start.22 = (f32[3,8,128]{2,1,0:T(8,128)S(1)}, f32[3,8,128]{2,1,0:T(8,128)S(1)}, u32[]{:S(2)}, u32[]{:S(2)}) collective-permute-start(f32[3,8,128]{2,1,0:T(8,128)S(1)} %get-tuple-element.101), channel_id=1, source_target_pairs={{289,313},{385,409},{417,441},{1,25},{33,57},{129,153},{161,185},{... | collective-permute-start | bytes 36872 | tf_op jit(solution)/shard_map/ppermute | solution.py:574
  114.7 6.0 %collective-permute-start.23 = (f32[1,8,128]{2,1,0:T(8,128)S(1)}, f32[1,8,128]{2,1,0:T(8,128)S(1)}, u32[]{:S(2)}, u32[]{:S(2)}) collective-permute-start(f32[1,8,128]{2,1,0:T(8,128)S(1)} %get-tuple-element.102), channel_id=1, source_target_pairs={{289,288},{385,384},{417,416},{1,0},{33,32},{129,128},{161,160},{2... | collective-permute-start | bytes 12296 | tf_op jit(solution)/shard_map/ppermute | solution.py:574
  118.8 5.5 %collective-permute-start.24 = (f32[1,8,128]{2,1,0:T(8,128)S(1)}, f32[1,8,128]{2,1,0:T(8,128)S(1)}, u32[]{:S(2)}, u32[]{:S(2)}) collective-permute-start(f32[1,8,128]{2,1,0:T(8,128)S(1)} %get-tuple-element.103), channel_id=1, source_target_pairs={{289,290},{385,386},{417,418},{1,2},{33,34},{129,130},{161,162},{2... | collective-permute-start | bytes 12296 | tf_op jit(solution)/shard_map/ppermute | solution.py:574
  124.4 15.1 %collective-permute-start.25 = (f32[8,128]{1,0:T(8,128)S(1)}, f32[8,128]{1,0:T(8,128)S(1)}, u32[]{:S(2)}, u32[]{:S(2)}) collective-permute-start(f32[8,128]{1,0:T(8,128)S(1)} %shard_map.139), channel_id=1, source_target_pairs={{289,0},{385,1},{417,2},{1,3},{33,4},{129,5},{161,6},{257,7},{297,... | collective-permute-start | bytes 12296 | tf_op jit(solution)/shard_map/ppermute | solution.py:724
